TPU v7x, 32 devices: a whole 2x2x4 slice. The times are simulated.
32 devices in a mesh: rows: 4 (over y, core), feat: 8 (over z, x).
Axes of the slice: x: 2, y: 2, z: 4, core: 2. Of those that a mesh axis runs over, the one named last changes fastest.
Arguments:
- margins: float32 [12288, 32], P(('rows', 'feat')), may hold values from -30 to 260
- labels: int32 [12288], P(('rows', 'feat')), may hold values from 0 to 31
- row_bins: int32 [1024, 12288], P('feat', 'rows'), may hold values from 0 to 63
- parents: int32 [12288], P('rows'), may hold values from 0 to 7
- split_feature: int32 [8], replicated, may hold values from 0 to 1023
- split_bin: int32 [8], replicated, may hold values from 16 to 47
- leaf_values: float32 [16, 32], replicated, may hold values from -4 to 4
Outputs:
- split_gains: float32 [16, 1024, 64], P('rows', 'feat')
- node_totals: float32 [16, 64], replicated
All inputs are finite; a program needn't handle non-finite values.
Results may differ from a plain program's by a relative error of at most 0.0017.
Values may be sent and summed in bfloat16 or wider, within the bound.
No kernel may reach another device: no remote copies, remote signals or barrier semaphores. Data moves between devices by JAX's collectives and lax.ppermute only.
A program may use at most 192 MiB of HBM per device.

v0:
```python
import jax
import jax.numpy as jnp
from jax import lax
from jax.sharding import PartitionSpec as P

BINS = 64


hess_ridge = 1.0


def prefix(value, axis, join, neutral):
    count, mine = (lax.axis_size(axis), lax.axis_index(axis))
    pieces = lax.all_gather(value, axis)
    subtotal = jnp.full_like(value, 0) + jnp.asarray(neutral, value.dtype)

    def turn(position, subtotal):
        longer = join(subtotal, pieces[position])
        return jnp.where(position < mine, longer, subtotal)

    return lax.fori_loop(0, count - 1, turn, subtotal)


def gain_scores(left_sums, totals, classes):
    grad_left = left_sums[..., :classes]
    hess_left = left_sums[..., classes:]
    grad_whole = totals[..., :classes]
    hess_whole = totals[..., classes:]
    grad_right = grad_whole - grad_left
    hess_right = hess_whole - hess_left
    score = (
        grad_left * grad_left / (hess_left + hess_ridge)
        + grad_right * grad_right / (hess_right + hess_ridge)
        - grad_whole * grad_whole / (hess_whole + hess_ridge)
    )
    return jnp.mean(score, axis=-1)


def add_terms(earlier, later):
    return earlier + later


def body(margins, labels, row_bins, parents, split_feature, split_bin, leaf_values):
    feat_dev, group_rows = row_bins.shape
    classes = margins.shape[1]
    node_count = leaf_values.shape[0]
    parent_count = split_feature.shape[0]
    bin_count = BINS
    feat_size = lax.axis_size("feat")
    feat_index = lax.axis_index("feat")
    own_rows = group_rows // feat_size
    parent_hot = parents[:, None] == jnp.arange(parent_count, dtype=jnp.int32)[None, :]
    row_feature = jnp.sum(jnp.where(parent_hot, split_feature[None, :], 0), axis=1)
    row_threshold = jnp.sum(jnp.where(parent_hot, split_bin[None, :], 0), axis=1)
    local_column = row_feature - feat_index * feat_dev
    column_hot = local_column[None, :] == jnp.arange(feat_dev, dtype=jnp.int32)[:, None]
    is_owned = jnp.any(column_hot, axis=0)
    chosen = jnp.sum(jnp.where(column_hot, row_bins, 0), axis=0)
    right_part = jnp.where(is_owned & (chosen > row_threshold), 1.0, 0.0).astype(jnp.float32)
    right_all = lax.psum(right_part.astype(jnp.bfloat16), "feat").astype(jnp.float32)
    node_all = 2 * parents + (right_all > 0.5).astype(jnp.int32)
    node_own = lax.dynamic_slice_in_dim(node_all, feat_index * own_rows, own_rows)
    node_hot_own = (node_own[:, None] == jnp.arange(node_count, dtype=jnp.int32)[None, :]).astype(
        jnp.float32
    )
    logits = margins + jnp.dot(node_hot_own, leaf_values, precision=lax.Precision.HIGHEST)
    probabilities = jax.nn.softmax(logits, axis=1)
    label_hot = (labels[:, None] == jnp.arange(classes, dtype=jnp.int32)[None, :]).astype(
        jnp.float32
    )
    gradient = probabilities - label_hot
    hessian = 2.0 * probabilities * (1.0 - probabilities)
    grad_hess = jnp.concatenate([gradient, hessian], axis=1).astype(jnp.bfloat16)
    partial_totals = lax.dot_general(
        node_hot_own.astype(jnp.bfloat16),
        grad_hess,
        (((0,), (0,)), ((), ())),
        preferred_element_type=jnp.float32,
    )
    node_totals = lax.psum(partial_totals, ("rows", "feat"))
    grad_all = lax.all_gather(grad_hess, "feat", axis=0, tiled=True)
    row_size = lax.axis_size("rows")
    node_hot = node_all[:, None] == jnp.arange(node_count, dtype=jnp.int32)[None, :]
    weighted = jnp.where(node_hot[:, :, None], grad_all[:, None, :], jnp.zeros((), jnp.bfloat16))
    flat_weighted = weighted.reshape(group_rows, node_count * 2 * classes)
    own_bins = bin_count // row_size
    span_rows = own_bins * feat_dev * lax.axis_size("rows")
    bin_span = span_rows // feat_dev
    bin_group = 8

    def one_group(offset):
        values = offset + jnp.arange(bin_group, dtype=jnp.int32)
        one_hot = (row_bins[None, :, :] == values[:, None, None]).astype(jnp.bfloat16)
        one_hot = one_hot.reshape(bin_group * feat_dev, group_rows)
        return jnp.dot(one_hot, flat_weighted, preferred_element_type=jnp.float32)

    blocks = lax.map(one_group, jnp.arange(0, bin_span, bin_group, dtype=jnp.int32))
    own_hist = lax.psum_scatter(
        blocks.reshape(span_rows, node_count * 2 * classes), "rows", scatter_dimension=0, tiled=True
    )
    shaped = own_hist.reshape(own_bins, feat_dev, node_count, 2 * classes)
    running = jnp.cumsum(shaped, axis=0)
    before = prefix(running[-1], "rows", add_terms, jnp.zeros_like(running[-1]))
    left_sums = running + before[None]
    gains_here = gain_scores(left_sums, node_totals[None, None], classes)
    gains_moved = jnp.transpose(gains_here, (2, 1, 0))
    split_gains = lax.all_to_all(gains_moved, "rows", split_axis=0, concat_axis=2, tiled=True)
    return (split_gains, node_totals)


def solution(mesh):
    return jax.shard_map(
        body,
        mesh=mesh,
        in_specs=(
            P(("rows", "feat"), None),
            P(("rows", "feat")),
            P("feat", "rows"),
            P("rows"),
            P(),
            P(),
            P(),
        ),
        out_specs=(P("rows", "feat", None), P()),
        check_vma=False,
    )
```

profile of v0, /device:TPU:0, one launch (start us, length us, event | category | flops | bytes accessed | tf_op | source)
XLA Modules:
  0.0 532.2 jit_solution(12949149705158159860)
XLA Ops:
  7.3 0.8 select_reduce_fusion.1
  8.3 1.6 select_reduce_fusion
  9.9 23.4 %psum.14 = bf16[3072]{0:T(1024)(128)(2,1)S(1)} all-reduce(bf16[3072]{0:T(1024)(128)(2,1)S(1)} %select_convert_fusion), channel_id=1, replica_groups=mesh['rows'=4,'feat'=8] {'feat'}, use_global_device_ids=true, to_apply=%region_4.5 | all-reduce | flops 3072 | bytes 12288 | tf_op jit(solution)/shard_map/psum | solution.py:60
  33.3 0.7 convert_add_fusion
  34.2 1.1 fusion.10
  35.3 0.7 subtract_convert_fusion
  36.1 31.2 %all_gather.6 = bf16[3072,64]{0,1:T(8,128)(2,1)S(1)} all-gather(bf16[384,64]{0,1:T(8,128)(2,1)S(1)} %pad_maximum_fusion), channel_id=1, replica_groups=mesh['rows'=4,'feat'=8] {'feat'}, dimensions={0}, use_global_device_ids=true | all-gather | bytes 442368 | tf_op jit(solution)/shard_map/all_gather | solution.py:81
  67.2 108.7 %while.25 = (s32[]{:T(128)}, f32[8,1024,1024]{2,1,0:T(8,128)}, s32[128,3072]{1,0:T(8,128)}, s32[8]{0:T(128)S(1)}, bf16[3072,64]{0,1:T(8,128)(2,1)S(1)}, /*index=5*/pred[3072,16]{0,1:T(8,128)(4,1)S(1)}, s32[]{:T(128)}) while((s32[]{:T(128)}, f32[8,1024,1024]{2,1,0:T(8,128)}, s32[128,3072]{1,0:T(8,128)}, s32[8]{0:T(128)S(1)}, ...), condition=%wide.region_8.9_spmd.clone, body=%wide.region_7.8_spmd.clone.sunk | while | flops 6448742400 | bytes 25092764 | solution.py:97
  67.2 0.6 dynamic_slice.20
  67.8 0.6 iota_add_fusion.2
  68.5 3.4 bitcast_compare_fusion.2
  71.9 0.6 broadcast_select_fusion.2
  72.5 8.3 %bitcast_dynamic-update-slice_fusion.2 = f32[8,1024,1024]{2,1,0:T(8,128)} fusion(f32[8,1024,1024]{2,1,0:T(8,128)} %get-tuple-element.270, s32[]{:T(128)} %get-tuple-element.269, pred[1024,3072]{1,0:T(32,128)(4,1)S(1)} %bitcast_compare_fusion.2, bf16[3072,1024]{0,1:T(8,128)(2,1)S(1)} %bitcast.48), kind=kOutput, calls=%fused_computation.3.clone.1 | convolution fusion | flops 6442450944 | bytes 13632000 | tf_op jit(solution)/shard_map/while/body/eval_jaxpr/dot_general | solution.py:95
  80.9 0.6 dynamic_slice.20
  81.4 0.6 iota_add_fusion.2
  82.2 3.4 bitcast_compare_fusion.2
  85.6 0.6 broadcast_select_fusion.2
  86.2 8.3 %bitcast_dynamic-update-slice_fusion.2 = f32[8,1024,1024]{2,1,0:T(8,128)} fusion(f32[8,1024,1024]{2,1,0:T(8,128)} %get-tuple-element.270, s32[]{:T(128)} %get-tuple-element.269, pred[1024,3072]{1,0:T(32,128)(4,1)S(1)} %bitcast_compare_fusion.2, bf16[3072,1024]{0,1:T(8,128)(2,1)S(1)} %bitcast.48), kind=kOutput, calls=%fused_computation.3.clone.1 | convolution fusion | flops 6442450944 | bytes 13632000 | tf_op jit(solution)/shard_map/while/body/eval_jaxpr/dot_general | solution.py:95
  94.5 0.6 dynamic_slice.20
  95.0 0.6 iota_add_fusion.2
  95.8 3.4 bitcast_compare_fusion.2
  99.2 0.6 broadcast_select_fusion.2
  99.7 8.3 %bitcast_dynamic-update-slice_fusion.2 = f32[8,1024,1024]{2,1,0:T(8,128)} fusion(f32[8,1024,1024]{2,1,0:T(8,128)} %get-tuple-element.270, s32[]{:T(128)} %get-tuple-element.269, pred[1024,3072]{1,0:T(32,128)(4,1)S(1)} %bitcast_compare_fusion.2, bf16[3072,1024]{0,1:T(8,128)(2,1)S(1)} %bitcast.48), kind=kOutput, calls=%fused_computation.3.clone.1 | convolution fusion | flops 6442450944 | bytes 13632000 | tf_op jit(solution)/shard_map/while/body/eval_jaxpr/dot_general | solution.py:95
  108.0 0.6 dynamic_slice.20
  108.6 0.6 iota_add_fusion.2
  109.3 3.4 bitcast_compare_fusion.2
  112.7 0.6 broadcast_select_fusion.2
  113.3 8.3 %bitcast_dynamic-update-slice_fusion.2 = f32[8,1024,1024]{2,1,0:T(8,128)} fusion(f32[8,1024,1024]{2,1,0:T(8,128)} %get-tuple-element.270, s32[]{:T(128)} %get-tuple-element.269, pred[1024,3072]{1,0:T(32,128)(4,1)S(1)} %bitcast_compare_fusion.2, bf16[3072,1024]{0,1:T(8,128)(2,1)S(1)} %bitcast.48), kind=kOutput, calls=%fused_computation.3.clone.1 | convolution fusion | flops 6442450944 | bytes 13632000 | tf_op jit(solution)/shard_map/while/body/eval_jaxpr/dot_general | solution.py:95
  121.6 0.6 dynamic_slice.20
  122.2 0.6 iota_add_fusion.2
  122.9 3.4 bitcast_compare_fusion.2
  126.3 0.6 broadcast_select_fusion.2
  126.9 8.3 %bitcast_dynamic-update-slice_fusion.2 = f32[8,1024,1024]{2,1,0:T(8,128)} fusion(f32[8,1024,1024]{2,1,0:T(8,128)} %get-tuple-element.270, s32[]{:T(128)} %get-tuple-element.269, pred[1024,3072]{1,0:T(32,128)(4,1)S(1)} %bitcast_compare_fusion.2, bf16[3072,1024]{0,1:T(8,128)(2,1)S(1)} %bitcast.48), kind=kOutput, calls=%fused_computation.3.clone.1 | convolution fusion | flops 6442450944 | bytes 13632000 | tf_op jit(solution)/shard_map/while/body/eval_jaxpr/dot_general | solution.py:95
  135.2 0.6 dynamic_slice.20
  135.8 0.6 iota_add_fusion.2
  136.5 3.4 bitcast_compare_fusion.2
  139.9 0.6 broadcast_select_fusion.2
  140.5 8.3 %bitcast_dynamic-update-slice_fusion.2 = f32[8,1024,1024]{2,1,0:T(8,128)} fusion(f32[8,1024,1024]{2,1,0:T(8,128)} %get-tuple-element.270, s32[]{:T(128)} %get-tuple-element.269, pred[1024,3072]{1,0:T(32,128)(4,1)S(1)} %bitcast_compare_fusion.2, bf16[3072,1024]{0,1:T(8,128)(2,1)S(1)} %bitcast.48), kind=kOutput, calls=%fused_computation.3.clone.1 | convolution fusion | flops 6442450944 | bytes 13632000 | tf_op jit(solution)/shard_map/while/body/eval_jaxpr/dot_general | solution.py:95
  148.8 0.6 dynamic_slice.20
  149.4 0.6 iota_add_fusion.2
  150.1 3.4 bitcast_compare_fusion.2
  153.5 0.6 broadcast_select_fusion.2
  154.1 8.3 %bitcast_dynamic-update-slice_fusion.2 = f32[8,1024,1024]{2,1,0:T(8,128)} fusion(f32[8,1024,1024]{2,1,0:T(8,128)} %get-tuple-element.270, s32[]{:T(128)} %get-tuple-element.269, pred[1024,3072]{1,0:T(32,128)(4,1)S(1)} %bitcast_compare_fusion.2, bf16[3072,1024]{0,1:T(8,128)(2,1)S(1)} %bitcast.48), kind=kOutput, calls=%fused_computation.3.clone.1 | convolution fusion | flops 6442450944 | bytes 13632000 | tf_op jit(solution)/shard_map/while/body/eval_jaxpr/dot_general | solution.py:95
  162.4 0.6 dynamic_slice.20
  162.9 0.6 iota_add_fusion.2
  163.7 3.4 bitcast_compare_fusion.2
  167.1 0.6 broadcast_select_fusion.2
  167.6 8.3 %bitcast_dynamic-update-slice_fusion.2 = f32[8,1024,1024]{2,1,0:T(8,128)} fusion(f32[8,1024,1024]{2,1,0:T(8,128)} %get-tuple-element.270, s32[]{:T(128)} %get-tuple-element.269, pred[1024,3072]{1,0:T(32,128)(4,1)S(1)} %bitcast_compare_fusion.2, bf16[3072,1024]{0,1:T(8,128)(2,1)S(1)} %bitcast.48), kind=kOutput, calls=%fused_computation.3.clone.1 | convolution fusion | flops 6442450944 | bytes 13632000 | tf_op jit(solution)/shard_map/while/body/eval_jaxpr/dot_general | solution.py:95
  175.9 31.1 %copy.51 = f32[8192,1024]{0,1:T(8,128)} copy(f32[8192,1024]{1,0:T(8,128)} %bitcast.49) | data formatting | bytes 67108864 | tf_op jit(solution)/shard_map/reshape | solution.py:99
  207.3 229.4 %reduce-scatter.2.cloned.1.call-done = f32[2048,1024]{0,1:T(8,128)} async-done(((f32[8192,1024]{0,1:T(8,128)}), f32[2048,1024]{0,1:T(8,128)}) %reduce-scatter.2.cloned.1.call-update) | async-done | bytes 8388624 | tf_op jit(solution)/shard_map/reduce_scatter | solution.py:98
  436.7 8.6 %copy.62 = f32[128,8,16,128]{3,2,1,0:T(8,128)} copy(f32[128,8,16,128]{3,1,2,0:T(8,128)} %bitcast.51) | data formatting | bytes 16777216
  445.3 15.0 %fusion.2 = f32[16,128,16,64]{1,2,3,0:T(8,128)} fusion(f32[16,128,16,64]{1,0,3,2:T(8,128)} %bitcast.50), kind=kOutput, calls=%fused_computation.8 | output fusion | flops 31457280 | bytes 16777216 | tf_op jit(solution)/shard_map/jit(cumsum)/reduce_window_sum | solution.py:102
  460.3 1.1 slice.20
  461.4 1.0 copy.53
  462.7 39.9 %psum.15 = f32[16,64]{1,0:T(8,128)S(1)} all-reduce(f32[16,64]{1,0:T(8,128)S(1)} %fusion.5), channel_id=1, replica_groups=mesh['rows'=4,'feat'=8] {'rows','feat'}, use_global_device_ids=true, to_apply=%region_13.14 | all-reduce | flops 1024 | bytes 8192 | tf_op jit(solution)/shard_map/psum | solution.py:80
  503.2 5.8 %while.26 = (s32[]{:T(128)}, f32[128,16,64]{2,1,0:T(8,128)S(1)}, s32[]{:T(128)}, f32[4,128,16,64]{1,3,2,0:T(8,128)}, s32[]{:T(128)}, /*index=5*/s32[]{:T(128)}) while((s32[]{:T(128)}, f32[128,16,64]{2,1,0:T(8,128)S(1)}, s32[]{:T(128)}, f32[4,128,16,64]{1,3,2,0:T(8,128)}, s32[]{:T(128)}, /*index=5*/s32[]{:T(128)}) %tuple.67), condition=%wide.region_12.13_spmd.clone, body=%wide.region_11.12_spmd.clone.sunk | while | flops 393220 | bytes 3670109 | solution.py:21
  503.2 1.1 constant_dynamic-slice_fusion.2
  505.1 1.1 constant_dynamic-slice_fusion.2
  507.0 1.1 constant_dynamic-slice_fusion.2
  508.9 0.6 copy.55
  509.5 4.4 broadcast_add_fusion
  513.9 2.7 subtract_reduce_fusion
  516.7 8.0 %all_to_all.18 = f32[16,128,16]{1,2,0:T(8,128)S(1)} all-to-all(f32[16,128,16]{1,2,0:T(8,128)S(1)} %copy.59), channel_id=1, replica_groups=mesh['rows'=4,'feat'=8] {'rows'}, dimensions={0} | all-to-all | bytes 262144 | tf_op jit(solution)/shard_map/all_to_all | solution.py:107
  524.7 0.7 copy.60
  (42 shorter events, 4.6 us)
Async XLA Ops:
  7.2 27.0 %copy-start = (f32[16,32]{1,0:T(8,128)S(1)}, f32[16,32]{1,0:T(8,128)}, u32[]{:S(2)}) copy-start(f32[16,32]{1,0:T(8,128)} %param.17) | copy-start | bytes 6148
  7.2 429.5 %reduce-scatter.2.cloned.1.call-start = ((), (), s32[]{:S(2)}) async-start(), calls=%async_computation.2 | async-start | bytes 41943040 | tf_op jit(solution)/shard_map/reduce_scatter | solution.py:98
  207.1 295.8 %all-gather.2.cloned.1.call-start = ((), (), s32[]{:S(2)}) async-start(), calls=%async_computation.3 | async-start | bytes 2621440 | tf_op jit(solution)/shard_map/all_gather | solution.py:14
  502.6 0.6 copy-start.2
  509.5 15.9 %copy-start.1 = (f32[16,32]{1,0:T(8,128)S(1)}, f32[16,32]{1,0:T(8,128)}, u32[]{:S(2)}) copy-start(f32[16,32]{1,0:T(8,128)} %param.17) | copy-start | bytes 6148
Sparse Core Ops, SparseCore 0:
  207.2 229.4 reduce-scatter.1
  462.5 22.7 all-gather.1
where the time goes:
time: 534 us; the launch traced here: 532 us
  waiting for transfers between devices  229 us (43%)
  blocking collectives  102 us (19%)
  matrix products  67.8 us (13%)
  other arithmetic  64.3 us (12%)
  local copies, waits for them, and re-layouts  53.6 us (10%)
  between operations  14.2 us (3%)
    reduce_scatter x1, waiting for transfers between devices, body(): lax.psum_scatter(blocks.reshape(span_rows, node_count * 2 * classes), 'ro...  229 us
    dot_general x8, matrix products, one_group(): return jnp.dot(one_hot, flat_weighted, preferred_element_type=jnp.float32)  66.4 us
    psum x1, blocking collectives, body(): node_totals = lax.psum(partial_totals, ('rows', 'feat'))  39.9 us
    all_gather x1, blocking collectives, body(): grad_all = lax.all_gather(grad_hess, 'feat', axis=0, tiled=True)  31.2 us
    reshape x1, local copies, waits for them, and re-layouts, body(): blocks.reshape(span_rows, node_count * 2 * classes)  31.1 us
    eq x8, other arithmetic, one_group(): row_bins[None, :, :] == values[:, None, None]  27.1 us
    psum x1, blocking collectives, body(): lax.psum(right_part.astype(jnp.bfloat16), 'feat').astype(jnp.float32)  23.4 us
    another operation x1, other arithmetic, body(): running = jnp.cumsum(shaped, axis=0)  15 us
  transfers between devices with their start and end apart: 2, of which 1 were waited for; matrix products, arithmetic and copies ran while one was open for 0% of the time, Pallas kernels for 0%

commit v1 on v0

v1 whole, which is shorter than its diff:
```python
import functools

import jax
import jax.numpy as jnp
from jax import lax
from jax.experimental import pallas as pl
from jax.experimental.pallas import tpu as pltpu
from jax.sharding import PartitionSpec as P

BINS = 64
LANES = 128
TILE = 16
GROUP_NODES = 4
CHUNK = 512
COPY_TILES = 4
COLS = 256

hess_ridge = 1.0

F32 = jnp.float32
BF16 = jnp.bfloat16
I32 = jnp.int32
NT = (((1,), (1,)), ((), ()))
VMEM = pl.BlockSpec(memory_space=pltpu.VMEM)
SMEM = pl.BlockSpec(memory_space=pltpu.SMEM)


def cdiv(a, b):
    return -(-a // b)


def iota(shape, dim):
    return lax.broadcasted_iota(I32, shape, dim)


def first_message_kernel(parent_count, nf, scal, margins, labels, bins, parents, out):
    own, classes = margins.shape
    feat_dev = bins.shape[0]
    out[0:classes, :] = margins[...].T
    par = parents[...]
    right = jnp.zeros(par.shape, F32)
    for p in range(parent_count):
        local = scal[p] - scal[2 * parent_count]
        owned = jnp.logical_and(local >= 0, local < feat_dev)
        threshold = jnp.where(owned, scal[parent_count + p], BINS)
        row = bins[pl.ds(jnp.clip(local, 0, feat_dev - 1), 1), :]
        right = right + jnp.where((par == p) & (row > threshold), 1.0, 0.0)
    out[classes : classes + 8, :] = jnp.broadcast_to(labels[...].astype(F32), (8, own))
    for k in range(nf):
        out[classes + 8 + k : classes + 9 + k, :] = right[:, k * own : (k + 1) * own]


def slot_kernel_part(par, parents_per_group, own):
    group = par.astype(I32) // parents_per_group
    groups = iota((16, own), 0)
    hot = group == groups
    earlier = (iota((own, own), 0) < iota((own, own), 1)).astype(F32).astype(BF16)
    ahead = jnp.dot(hot.astype(F32).astype(BF16), earlier, preferred_element_type=F32)
    start = jnp.sum((group < groups).astype(F32), axis=1, keepdims=True)
    return jnp.sum(jnp.where(hot, ahead + start, 0.0), axis=0, keepdims=True)


def placing(slot, own):
    return (iota((own, own), 0) == slot.astype(I32)).astype(F32).astype(BF16)


def sort_bins_kernel(nr, nf, parents_per_group, *refs):
    bins = refs[:nr]
    parents, out, slots = refs[nr:]
    own_feats, own = bins[0].shape[1:]
    copies = LANES // own_feats
    for j in range(nr):

        @pl.loop(0, nf)
        def _(k):
            slot = slot_kernel_part(parents[j, pl.ds(k, 1), :], parents_per_group, own)
            slots[j, pl.ds(k, 1), :] = slot
            block = jnp.concatenate([bins[j][k]] * copies, axis=0)
            placed = lax.dot_general(placing(slot, own), block, NT, preferred_element_type=F32)
            first = pl.multiple_of((j * nf + k) * own, TILE)
            out[pl.ds(first, own), :] = placed.astype(BF16)


def level_kernel(sizes, scal, offsets, near, far, parents, slots, bins, leaf, gains, totals, grads, mbins, mgrads, acc):
    nr, nf, ny, lo, hi, own, own_feats, classes, nodes = sizes
    blocks = nr * nf
    groups = nodes // GROUP_NODES
    half = GROUP_NODES * classes
    width = BINS * own_feats
    tiles = own // TILE
    me_feat = scal[0]
    leaf_t = leaf[...]
    label_row = hi * classes
    right_row = label_row + cdiv(hi, 8) * 8

    for jc, source in enumerate((near, far)):

        @pl.loop(0, ny * nf)
        def _(i):
            jy = i // nf
            jx = lax.rem(i, lo)
            jz = lax.rem(i // lo, hi)
            k = jnp.bitwise_xor(me_feat, jz * lo + jx)
            j = jy * 2 + jc
            yx = jy * lo + jx
            margins = source[yx, pl.ds(pl.multiple_of(jz * classes, 8), classes), :]
            label = source[yx, pl.ds(label_row + jz, 1), :]
            right = source[jy * lo, pl.ds(right_row + k, 1), :]
            for other in range(1, lo):
                right = right + source[jy * lo + other, pl.ds(right_row + k, 1), :]
            node = 2.0 * parents[j, pl.ds(k, 1), :] + right
            node_hot = (node == iota((nodes, own), 0).astype(F32)).astype(F32)
            moved = jnp.dot(leaf_t, node_hot, precision=lax.Precision.HIGHEST, preferred_element_type=F32)
            logits = margins + moved
            powers = jnp.exp(logits - jnp.max(logits, axis=0, keepdims=True))
            prob = powers / jnp.sum(powers, axis=0, keepdims=True)
            hot = label == iota((classes, own), 0).astype(F32)
            gradient = prob - jnp.where(hot, 1.0, 0.0)
            hessian = 2.0 * prob * (1.0 - prob)
            pad = jnp.broadcast_to(node, (LANES - 2 * classes, own))
            columns = jnp.concatenate([gradient, hessian, pad], axis=0).astype(BF16)
            slot = slots[j, pl.ds(k, 1), :]
            placed = lax.dot_general(placing(slot, own), columns, NT, preferred_element_type=F32)
            first = pl.multiple_of((j * nf + k) * own, TILE)
            grads[pl.ds(first, own), :] = placed.astype(BF16)

    acc[...] = jnp.zeros(acc.shape, F32)
    lane_bin = (iota((1, LANES), 1) // own_feats).astype(F32)
    bins_per = LANES // own_feats

    @pl.loop(0, groups)
    def _(q):
        def gather(block, place):
            begin = offsets[block, q]
            end = offsets[block, q + 1]
            t0 = begin // TILE
            count = jnp.where(end > begin, (end + TILE - 1) // TILE - t0, 0)
            base = block * tiles + t0

            @pl.loop(0, (count + COPY_TILES - 1) // COPY_TILES)
            def _(c):
                src = pl.multiple_of((base + c * COPY_TILES) * TILE, TILE)
                dst = pl.multiple_of((place + c * COPY_TILES) * TILE, TILE)
                rows = COPY_TILES * TILE
                mbins[pl.ds(dst, rows), :] = bins[pl.ds(src, rows), :]
                mgrads[pl.ds(dst, rows), :] = grads[pl.ds(src, rows), :]

            return place + count

        place = lax.fori_loop(0, blocks, gather, jnp.int32(0))
        tail = pl.multiple_of(place * TILE, TILE)
        mgrads[pl.ds(tail, CHUNK), :] = jnp.full((CHUNK, LANES), -1.0, BF16)

        @pl.loop(0, (place * TILE + CHUNK - 1) // CHUNK)
        def _(i):
            at = pl.multiple_of(i * CHUNK, CHUNK)
            columns = mgrads[pl.ds(at, CHUNK), :].T
            node = columns[2 * classes : 2 * classes + classes, :]
            parts = []
            for side in range(2):
                value = columns[side * classes : (side + 1) * classes, :]
                for n in range(GROUP_NODES):
                    wanted = (q * GROUP_NODES + n).astype(F32).astype(BF16)
                    parts.append(jnp.where(node == wanted, value, jnp.zeros_like(value)))
            weights = jnp.concatenate(parts, axis=0)
            value = (mbins[pl.ds(at, CHUNK), :].astype(F32) - lane_bin).astype(BF16)
            for m in range(width // COLS):
                below = []
                for s in range(COLS // LANES):
                    limit = (m * (COLS // LANES) + s) * bins_per
                    below.append(
                        jnp.where(value <= jnp.asarray(limit, BF16), jnp.asarray(1, BF16), jnp.asarray(0, BF16))
                    )
                below = jnp.concatenate(below, axis=1)
                span = slice(m * COLS, (m + 1) * COLS)
                acc[q, :, span] += jnp.dot(weights, below, preferred_element_type=F32)

        whole = acc[q, :, width - 1 : width]
        totals[q] = whole
        grad_whole = whole[:half]
        hess_whole = whole[half:]
        parent_score = grad_whole * grad_whole / (hess_whole + hess_ridge)
        for m in range(width // LANES):
            span = slice(m * LANES, (m + 1) * LANES)
            grad_left = acc[q, :half, span]
            hess_left = acc[q, half:, span]
            grad_right = grad_whole - grad_left
            hess_right = hess_whole - hess_left
            score = (
                grad_left * grad_left / (hess_left + hess_ridge)
                + grad_right * grad_right / (hess_right + hess_ridge)
                - parent_score
            )
            for n in range(GROUP_NODES):
                total = jnp.sum(score[n * classes : (n + 1) * classes], axis=0, keepdims=True)
                gains[q, n : n + 1, span] = total * (1.0 / classes)


def flip_by(value, index, count):
    step = 1
    while step < count:
        shaped = value.reshape((count // (2 * step), 2, step) + value.shape[1:])
        flipped = jnp.flip(shaped, axis=1)
        value = jnp.where((index // step) % 2 == 1, flipped, shaped).reshape(value.shape)
        step *= 2
    return value


def swap(value, axes, sizes, offsets):
    total = 1
    for size in sizes:
        total *= size
    flat = 0
    for size, offset in zip(sizes, offsets):
        flat = flat * size + offset
    return lax.ppermute(value, axes, [(i, i ^ flat) for i in range(total)])


def body(margins, labels, row_bins, parents, split_feature, split_bin, leaf_values):
    feat_dev, group_rows = row_bins.shape
    own, classes = margins.shape
    nodes = leaf_values.shape[0]
    parent_count = split_feature.shape[0]
    nf, nr = lax.axis_size("feat"), lax.axis_size("rows")
    feat, row = lax.axis_index("feat"), lax.axis_index("rows")
    own_feats = feat_dev // nr
    lo, ny = 2, nr // 2
    hi = nf // lo
    groups = nodes // GROUP_NODES
    parents_per_group = parent_count // groups
    blocks = nr * nf
    width = BINS * own_feats
    axes, sizes = ("rows", "feat"), (nr, nf)

    scal = jnp.concatenate([split_feature, split_bin, jnp.full((1,), feat * feat_dev, I32)])
    first_rows = classes + 8 + nf
    first = pl.pallas_call(
        functools.partial(first_message_kernel, parent_count, nf),
        out_shape=jax.ShapeDtypeStruct((first_rows, own), F32),
        in_specs=[SMEM] + [VMEM] * 4,
        out_specs=VMEM,
        name="first_message",
    )(scal, margins, labels.reshape(1, own), row_bins, parents.reshape(1, group_rows))

    along_z = [first] + [swap(first, axes, sizes, (0, lo * j)) for j in range(1, hi)]

    extra = cdiv(nf, own_feats)
    parent_rows = jnp.zeros((extra * own_feats, own), BF16).at[:nf].set(parents.reshape(nf, own).astype(BF16))
    parent_rows = jnp.broadcast_to(parent_rows.reshape(1, extra, own_feats, own), (nr, extra, own_feats, own))
    sent = row_bins.astype(BF16).reshape(nr, own_feats, nf, own).transpose(0, 2, 1, 3)
    sent = jnp.concatenate([sent, parent_rows], axis=1)
    bins_by = []
    for j in range(nr):
        piece = lax.dynamic_index_in_dim(sent, jnp.bitwise_xor(row, j), 0, keepdims=False)
        bins_by.append(piece if j == 0 else swap(piece, axes, sizes, (j, 0)))
    all_parents = jnp.stack([b[nf:].reshape(extra * own_feats, own)[:nf] for b in bins_by]).astype(F32)

    second = jnp.concatenate(
        [m[:classes] for m in along_z]
        + [m[classes : classes + 1] for m in along_z]
        + [jnp.zeros((cdiv(hi, 8) * 8 - hi, own), F32)]
        + [sum(m[classes + 8 :] for m in along_z)],
        axis=0,
    )
    plane = []
    for jy in range(ny):
        for jx in range(lo):
            plane.append(second if jy + jx == 0 else swap(second, axes, sizes, (2 * jy, jx)))
    near = jnp.stack(plane)
    far = swap(near, axes, sizes, (1, 0))

    placed_bins, slots = pl.pallas_call(
        functools.partial(sort_bins_kernel, nr, nf, parents_per_group),
        out_shape=(
            jax.ShapeDtypeStruct((blocks * own + COPY_TILES * TILE, LANES), BF16),
            jax.ShapeDtypeStruct((nr, nf, own), F32),
        ),
        in_specs=[VMEM] * (nr + 1),
        out_specs=(VMEM, VMEM),
        name="sort_bins",
    )(*bins_by, all_parents)

    group_of = all_parents.reshape(blocks, own).astype(I32) // parents_per_group
    offsets = jnp.stack([jnp.sum((group_of < q).astype(I32), axis=1) for q in range(groups + 1)], axis=1)

    shape = (nr, nf, ny, lo, hi, own, own_feats, classes, nodes)
    cap = blocks * own + CHUNK + COPY_TILES * TILE
    gains, totals = pl.pallas_call(
        functools.partial(level_kernel, shape),
        out_shape=(
            jax.ShapeDtypeStruct((groups, GROUP_NODES, width), F32),
            jax.ShapeDtypeStruct((groups, 2 * GROUP_NODES * classes, 1), F32),
        ),
        in_specs=[SMEM, SMEM] + [VMEM] * 6,
        out_specs=(VMEM, VMEM),
        scratch_shapes=[
            pltpu.VMEM((blocks * own + COPY_TILES * TILE, LANES), BF16),
            pltpu.VMEM((cap, LANES), BF16),
            pltpu.VMEM((cap, LANES), BF16),
            pltpu.VMEM((groups, 2 * GROUP_NODES * classes, width), F32),
        ],
        compiler_params=pltpu.CompilerParams(vmem_limit_bytes=60 * 2**20),
        name="level",
    )(feat.reshape(1), offsets, near, far, all_parents, slots, placed_bins, leaf_values.T)

    node_totals = totals.reshape(groups, 2, GROUP_NODES, classes).transpose(0, 2, 1, 3).reshape(nodes, 2 * classes)

    by_owner = gains.reshape(nr, nodes // nr, BINS, own_feats).transpose(0, 1, 3, 2)
    relative = flip_by(by_owner, row, nr)
    kept = jnp.stack(
        [relative[0]] + [swap(relative[j], axes, sizes, (j, 0)) for j in range(1, nr)]
    )
    split_gains = flip_by(kept, row, nr).transpose(1, 0, 2, 3).reshape(nodes // nr, feat_dev, BINS)
    return split_gains, node_totals


def solution(mesh):
    return jax.shard_map(
        body,
        mesh=mesh,
        in_specs=(
            P(("rows", "feat"), None),
            P(("rows", "feat")),
            P("feat", "rows"),
            P("rows"),
            P(),
            P(),
            P(),
        ),
        out_specs=(P("rows", "feat", None), P()),
        check_vma=False,
    )
```

time: 534 us -> 124 us (0.23)
  waiting for transfers between devices: 229 us -> 26.8 us
  blocking collectives: 102 us -> 0 us
  matrix products: 67.8 us -> 0 us
  Pallas kernels: 0 us -> 67.6 us
  other arithmetic: 64.3 us -> 3.79 us
  local copies, waits for them, and re-layouts: 53.6 us -> 10.8 us
  between operations: 14.2 us -> 0.92 us
  starting transfers between devices: 0.26 us -> 13.3 us
    reduce_scatter x1 -> x0, waiting for transfers between devices: 229 us -> none  [body(): lax.psum_scatter(blocks.reshape(span_rows, node_count * 2 * classes), 'ro...]
    dot_general x10 -> x0, matrix products: 67.8 us -> none  [the longest x8 66.4 us: one_group(): return jnp.dot(one_hot, flat_weighted, preferred_element_type=jnp.float32)]
    pallas_call x0 -> x3, Pallas kernels: none -> 67.6 us  [the longest x1 49.8 us: body(): pl.pallas_call(functools.partial(level_kernel, shape), out_shape=(jax.Sha...]
    psum x2 -> x0, blocking collectives: 63.3 us -> none  [the longest x1 39.9 us: body(): node_totals = lax.psum(partial_totals, ('rows', 'feat'))]
    all_gather x1 -> x0, blocking collectives: 31.2 us -> none  [body(): grad_all = lax.all_gather(grad_hess, 'feat', axis=0, tiled=True)]
    reshape x1 -> x5, local copies, waits for them, and re-layouts: 31.1 us -> 3.26 us  [the longest x1 1.24 us: body(): labels.reshape(1, own)]
    eq x9 -> x0, other arithmetic: 27.1 us -> none  [the longest x8 27.1 us: one_group(): row_bins[None, :, :] == values[:, None, None]]
    ppermute x0 -> x13, waiting for transfers between devices: none -> 26.8 us  [swap(): return lax.ppermute(value, axes, [(i, i ^ flat) for i in range(total)])]
  transfers between devices with their start and end apart: 2 -> 13, of which waited for: 1 -> 8; matrix products, arithmetic and copies ran while one was open for 0% -> 5% of each run, Pallas kernels for 0% -> 13%
where the time goes in v1:
time: 124 us; the launch traced here: 123 us
  Pallas kernels  67.6 us (55%)
  waiting for transfers between devices  26.8 us (22%)
  starting transfers between devices  13.3 us (11%)
  local copies, waits for them, and re-layouts  10.8 us (9%)
  other arithmetic  3.79 us (3%)
    pallas_call x1, Pallas kernels, body(): pl.pallas_call(functools.partial(level_kernel, shape), out_shape=(jax.Sha...  49.8 us
    ppermute x13, waiting for transfers between devices, swap(): return lax.ppermute(value, axes, [(i, i ^ flat) for i in range(total)])  26.8 us
    pallas_call x1, Pallas kernels, body(): pl.pallas_call(functools.partial(sort_bins_kernel, nr, nf, parents_per_gr...  15.6 us
    ppermute x13, starting transfers between devices, swap(): return lax.ppermute(value, axes, [(i, i ^ flat) for i in range(total)])  13.3 us
    unnamed x24, local copies, waits for them, and re-layouts  4.48 us
  transfers between devices with their start and end apart: 13, of which 8 were waited for; matrix products, arithmetic and copies ran while one was open for 5% of the time, Pallas kernels for 13%

profile of v1, /device:TPU:0, one launch (start us, length us, event | category | flops | bytes accessed | tf_op | source)
XLA Modules:
  0.0 123.3 jit_solution(13938056830555499570)
XLA Ops:
  0.6 0.0 copy-start
  0.6 1.7 %copy.40.margins = f32[384,32]{1,0:T(8,128)} copy(f32[384,32]{0,1:T(8,128)} %param.9) | data formatting | bytes 98304 | tf_op args[0]
  2.4 1.2 %reshape.108.labels = s32[1,384]{1,0:T(1,128)} reshape(s32[384]{0:T(512)} %param.10) | data formatting | bytes 3072 | tf_op jit(solution)/shard_map/reshape | solution.py:243
  3.6 1.3 %pad_add_fusion.scal = s32[17]{0:T(128)} fusion(s32[1]{0:T(128)} %bitcast.6, s32[8]{0:T(128)} %param.14, s32[8]{0:T(128)} %param.13), kind=kLoop, calls=%fused_computation.45 | loop fusion | flops 34 | bytes 136 | tf_op jit(solution)/shard_map/concatenate | solution.py:235
  4.9 2.3 %first_message.1 = f32[48,384]{1,0:T(8,128)} custom-call(s32[17]{0:T(128)} %pad_add_fusion.scal, f32[384,32]{1,0:T(8,128)} %copy.40.margins, s32[1,384]{1,0:T(1,128)} %reshape.108.labels, s32[128,3072]{1,0:T(8,128)} %bins.1, s32[1,3072]{1,0:T(1,128)} %bitcast.64), custom_call_target="tpu_custom_call" | custom-call | tf_op jit(solution)/shard_map/first_message/pallas_call | solution.py:237
  7.2 3.1 %collective-permute-start.3 = (f32[48,384]{1,0:T(8,128)}, f32[48,384]{1,0:T(8,128)S(1)}, u32[]{:S(2)}, u32[]{:S(2)}) collective-permute-start(f32[48,384]{1,0:T(8,128)} %first_message.1), channel_id=1, source_target_pairs={{0,2},{1,3},{2,0},{3,1},{4,6},{5,7},{6,4},{7,5},{8,10},{9,11},{10,... | collective-permute-start | bytes 221192 | tf_op jit(solution)/shard_map/ppermute | solution.py:216
  10.3 2.6 %collective-permute-start.4 = (f32[48,384]{1,0:T(8,128)}, f32[48,384]{1,0:T(8,128)S(1)}, u32[]{:S(2)}, u32[]{:S(2)}) collective-permute-start(f32[48,384]{1,0:T(8,128)} %first_message.1), channel_id=1, source_target_pairs={{0,4},{1,5},{2,6},{3,7},{4,0},{5,1},{6,2},{7,3},{8,12},{9,13},{10,... | collective-permute-start | bytes 221192 | tf_op jit(solution)/shard_map/ppermute | solution.py:216
  12.8 0.0 collective-permute-start.5
  12.9 0.9 slice.113
  13.7 0.7 slice.117
  14.4 0.0 collective-permute-done.3
  14.4 3.8 %collective-permute-done.4 = f32[48,384]{1,0:T(8,128)S(1)} collective-permute-done((f32[48,384]{1,0:T(8,128)}, f32[48,384]{1,0:T(8,128)S(1)}, u32[]{:S(2)}, u32[]{:S(2)}) %collective-permute-start.4) | collective-permute-done | bytes 73760 | tf_op jit(solution)/shard_map/ppermute | solution.py:216
  18.3 1.0 collective-permute-done.5
  19.3 0.7 slice_add_fusion
  20.1 1.6 %collective-permute-start.7 = (f32[144,384]{1,0:T(8,128)S(1)}, f32[144,384]{1,0:T(8,128)S(1)}, u32[]{:S(2)}, u32[]{:S(2)}) collective-permute-start(f32[144,384]{1,0:T(8,128)S(1)} %concatenate.13), channel_id=1, source_target_pairs={{0,16},{1,17},{2,18},{3,19},{4,20},{5,21},{6,22},{7,23},{8,24},{9,... | collective-permute-start | bytes 663560 | tf_op jit(solution)/shard_map/ppermute | solution.py:216
  21.7 1.4 %collective-permute-start.8 = (f32[144,384]{1,0:T(8,128)S(1)}, f32[144,384]{1,0:T(8,128)S(1)}, u32[]{:S(2)}, u32[]{:S(2)}) collective-permute-start(f32[144,384]{1,0:T(8,128)S(1)} %concatenate.13), channel_id=1, source_target_pairs={{0,17},{1,16},{2,19},{3,18},{4,21},{5,20},{6,23},{7,22},{8,25},{9,... | collective-permute-start | bytes 663560 | tf_op jit(solution)/shard_map/ppermute | solution.py:216
  23.1 0.5 collective-permute-start.6
  23.7 6.6 %collective-permute-done.7 = f32[144,384]{1,0:T(8,128)S(1)} collective-permute-done((f32[144,384]{1,0:T(8,128)S(1)}, f32[144,384]{1,0:T(8,128)S(1)}, u32[]{:S(2)}, u32[]{:S(2)}) %collective-permute-start.7) | collective-permute-done | bytes 221216 | tf_op jit(solution)/shard_map/ppermute | solution.py:216
  30.3 0.0 collective-permute-done.8
  30.3 1.2 collective-permute-done.6
  31.5 0.1 pad_maximum_fusion.near
  31.6 0.0 copy-start.1
  31.6 0.1 collective-permute-start.9
  31.7 0.1 convert_element_type.41
  31.8 0.0 copy-done.8
  31.8 0.0 copy-start.9
  31.8 0.1 copy.46
  32.0 0.1 copy.48
  32.2 0.1 fusion.3
  32.3 0.2 copy-done.1
  32.5 0.3 collective-permute-start
  32.8 1.5 %collective-permute-start.1 = (bf16[9,32,384]{2,1,0:T(8,128)(2,1)S(1)}, bf16[9,32,384]{2,1,0:T(8,128)(2,1)S(1)}, u32[]{:S(2)}, u32[]{:S(2)}) collective-permute-start(bf16[9,32,384]{2,1,0:T(8,128)(2,1)S(1)} %get-tuple-element.35), channel_id=1, source_target_pairs={{0,16},{1,17},{2,18},{3,19},{4,20},{5,21},{6,22},{7,23},{8,24},{9,... | collective-permute-start | bytes 663560 | tf_op jit(solution)/shard_map/ppermute | solution.py:216
  34.4 0.0 collective-permute-start.2
  34.4 0.0 copy-done.9
  34.4 0.7 copy.41
  35.0 0.0 collective-permute-done.refs_1_
  35.1 6.1 %collective-permute-done.1.refs_2_ = bf16[9,32,384]{2,1,0:T(8,128)(2,1)S(1)} collective-permute-done((bf16[9,32,384]{2,1,0:T(8,128)(2,1)S(1)}, bf16[9,32,384]{2,1,0:T(8,128)(2,1)S(1)}, u32[]{:S(2)}, u32[]{:S(2)}) %collective-permute-start.1) | collective-permute-done | bytes 221216 | tf_op jit(solution)/shard_map/ppermute | solution.py:216
  41.2 3.1 %collective-permute-done.2.refs_3_ = bf16[9,32,384]{2,1,0:T(8,128)(2,1)S(1)} collective-permute-done((bf16[9,32,384]{2,1,0:T(8,128)(2,1)S(1)}, bf16[9,32,384]{2,1,0:T(8,128)(2,1)S(1)}, u32[]{:S(2)}, u32[]{:S(2)}) %collective-permute-start.2) | collective-permute-done | bytes 221216 | tf_op jit(solution)/shard_map/ppermute | solution.py:216
  44.3 0.4 convert_reduce_fusion
  44.7 0.1 stack.56
  44.8 0.1 stack.57
  44.9 0.1 stack.58
  45.0 0.1 stack.59
  45.1 0.1 stack.60
  45.2 0.7 copy.42.offsets
  45.9 0.6 maximum_convert_fusion.refs_4_.parents
  46.5 0.0 copy-done.5
  46.5 15.6 %sort_bins.1 = (bf16[12352,128]{1,0:T(8,128)(2,1)}, f32[4,8,384]{2,1,0:T(8,128)}) custom-call(bf16[9,32,384]{2,1,0:T(8,128)(2,1)} %bitcast.54, bf16[9,32,384]{2,1,0:T(8,128)(2,1)} %copy-done.5, bf16[9,32,384]{2,1,0:T(8,128)(2,1)} %copy-done.6, bf16[9,32,384]{2,1,0:T(8,128)(2,1)} %copy-done.7, f32[4,8,384]{2,1,0:T(8,128)} %maximum_convert_fusion.refs_4_.parents), custom_call_target="tpu_custom_call" | custom-call | tf_op jit(solution)/shard_map/sort_bins/pallas_call | solution.py:272
  62.1 0.0 collective-permute-done.9.far
  62.1 0.9 copy-done.3
  63.0 49.8 %level.1 = (f32[4,4,2048]{2,1,0:T(4,128)}, f32[4,256,1]{2,1,0:T(8,128)}) custom-call(s32[1]{0:T(128)} %bitcast.scal, s32[32,5]{1,0:T(8,128)} %copy.42.offsets, f32[4,144,384]{2,1,0:T(8,128)} %copy-done.1, f32[4,144,384]{2,1,0:T(8,128)} %copy-done.3, f32[4,8,384]{2,1,0:T(8,128)} %maximum_convert_fusion.refs_4_.parents, f32[4,8,384]{2,1,0:T(8,128)} %get-tuple-element.18.slots, ...), custom_call_target="tpu_custom_call" | custom-call | tf_op jit(solution)/shard_map/level/pallas_call | solution.py:288
  112.8 1.1 reshape.110
  114.1 0.7 collective-permute-start.10
  114.8 1.5 %collective-permute-start.11 = (f32[4,32,64]{1,2,0:T(8,128)S(1)}, f32[4,32,64]{1,2,0:T(8,128)S(1)}, u32[]{:S(2)}, u32[]{:S(2)}) collective-permute-start(f32[4,32,64]{1,2,0:T(8,128)S(1)} %get-tuple-element.39), channel_id=1, source_target_pairs={{0,16},{1,17},{2,18},{3,19},{4,20},{5,21},{6,22},{7,23},{8,24},{9,... | collective-permute-start | bytes 98312 | tf_op jit(solution)/shard_map/ppermute | solution.py:216
  116.3 0.0 collective-permute-start.12
  116.3 0.0 copy-done.4
  116.3 0.2 reduce.7
  116.5 0.1 reshape.116
  116.6 0.7 reshape.117
  117.3 0.0 collective-permute-done.10
  117.3 3.9 %collective-permute-done.11 = f32[4,32,64]{1,2,0:T(8,128)S(1)} collective-permute-done((f32[4,32,64]{1,2,0:T(8,128)S(1)}, f32[4,32,64]{1,2,0:T(8,128)S(1)}, u32[]{:S(2)}, u32[]{:S(2)}) %collective-permute-start.11) | collective-permute-done | bytes 32800 | tf_op jit(solution)/shard_map/ppermute | solution.py:216
  121.2 1.0 collective-permute-done.12
  122.3 0.2 copy.43
  122.5 0.8 copy.45
  (35 shorter events, 0.4 us)
Async XLA Ops:
  0.6 31.1 %copy-start = (s32[128,3072]{1,0:T(8,128)S(1)}, s32[128,3072]{1,0:T(8,128)}, u32[]{:S(2)}) copy-start(s32[128,3072]{1,0:T(8,128)} %bins.1) | copy-start | bytes 4718596
  4.9 26.9 %copy-start.8 = (s32[3072]{0:T(1024)S(1)}, s32[3072]{0:T(1024)}, u32[]{:S(2)}) copy-start(s32[3072]{0:T(1024)} %param.12) | copy-start | bytes 36868
  7.2 7.2 %collective-permute-start.3 = (f32[48,384]{1,0:T(8,128)}, f32[48,384]{1,0:T(8,128)S(1)}, u32[]{:S(2)}, u32[]{:S(2)}) collective-permute-start(f32[48,384]{1,0:T(8,128)} %first_message.1), channel_id=1, source_target_pairs={{0,2},{1,3},{2,0},{3,1},{4,6},{5,7},{6,4},{7,5},{8,10},{9,11},{10,... | collective-permute-start | bytes 221192 | tf_op jit(solution)/shard_map/ppermute | solution.py:216
  10.3 8.0 %collective-permute-start.4 = (f32[48,384]{1,0:T(8,128)}, f32[48,384]{1,0:T(8,128)S(1)}, u32[]{:S(2)}, u32[]{:S(2)}) collective-permute-start(f32[48,384]{1,0:T(8,128)} %first_message.1), channel_id=1, source_target_pairs={{0,4},{1,5},{2,6},{3,7},{4,0},{5,1},{6,2},{7,3},{8,12},{9,13},{10,... | collective-permute-start | bytes 221192 | tf_op jit(solution)/shard_map/ppermute | solution.py:216
  12.8 6.5 %collective-permute-start.5 = (f32[48,384]{1,0:T(8,128)}, f32[48,384]{1,0:T(8,128)S(1)}, u32[]{:S(2)}, u32[]{:S(2)}) collective-permute-start(f32[48,384]{1,0:T(8,128)} %first_message.1), channel_id=1, source_target_pairs={{0,6},{1,7},{2,4},{3,5},{4,2},{5,3},{6,0},{7,1},{8,14},{9,15},{10,... | collective-permute-start | bytes 221192 | tf_op jit(solution)/shard_map/ppermute | solution.py:216
  20.1 10.2 %collective-permute-start.7 = (f32[144,384]{1,0:T(8,128)S(1)}, f32[144,384]{1,0:T(8,128)S(1)}, u32[]{:S(2)}, u32[]{:S(2)}) collective-permute-start(f32[144,384]{1,0:T(8,128)S(1)} %concatenate.13), channel_id=1, source_target_pairs={{0,16},{1,17},{2,18},{3,19},{4,20},{5,21},{6,22},{7,23},{8,24},{9,... | collective-permute-start | bytes 663560 | tf_op jit(solution)/shard_map/ppermute | solution.py:216
  21.7 8.6 %collective-permute-start.8 = (f32[144,384]{1,0:T(8,128)S(1)}, f32[144,384]{1,0:T(8,128)S(1)}, u32[]{:S(2)}, u32[]{:S(2)}) collective-permute-start(f32[144,384]{1,0:T(8,128)S(1)} %concatenate.13), channel_id=1, source_target_pairs={{0,17},{1,16},{2,19},{3,18},{4,21},{5,20},{6,23},{7,22},{8,25},{9,... | collective-permute-start | bytes 663560 | tf_op jit(solution)/shard_map/ppermute | solution.py:216
  23.1 8.4 %collective-permute-start.6 = (f32[144,384]{1,0:T(8,128)S(1)}, f32[144,384]{1,0:T(8,128)S(1)}, u32[]{:S(2)}, u32[]{:S(2)}) collective-permute-start(f32[144,384]{1,0:T(8,128)S(1)} %concatenate.13), channel_id=1, source_target_pairs={{0,1},{1,0},{2,3},{3,2},{4,5},{5,4},{6,7},{7,6},{8,9},{9,8},{10,11... | collective-permute-start | bytes 663560 | tf_op jit(solution)/shard_map/ppermute | solution.py:216
  31.6 0.9 copy-start.1
  31.6 30.5 %collective-permute-start.9 = (f32[4,144,384]{2,1,0:T(8,128)S(1)}, f32[4,144,384]{2,1,0:T(8,128)S(1)}, u32[]{:S(2)}, u32[]{:S(2)}) collective-permute-start(f32[4,144,384]{2,1,0:T(8,128)S(1)} %pad_maximum_fusion.near), channel_id=1, source_target_pairs={{0,8},{1,9},{2,10},{3,11},{4,12},{5,13},{6,14},{7,15},{8,0},{9,1},... | collective-permute-start | bytes 2654216 | tf_op jit(solution)/shard_map/ppermute | solution.py:216
  31.8 2.6 %copy-start.9 = (f32[16,32]{1,0:T(8,128)S(1)}, f32[16,32]{1,0:T(8,128)}, u32[]{:S(2)}) copy-start(f32[16,32]{1,0:T(8,128)} %param.15) | copy-start | bytes 6148
  32.5 14.0 %copy-start.2 = (bf16[1,9,32,384]{3,2,1,0:T(8,128)(2,1)}, bf16[1,9,32,384]{3,2,1,0:T(8,128)(2,1)S(1)}, u32[]{:S(2)}) copy-start(bf16[1,9,32,384]{3,2,1,0:T(8,128)(2,1)S(1)} %get-tuple-element.33) | copy-start | bytes 663556
  32.5 2.5 %collective-permute-start = (bf16[9,32,384]{2,1,0:T(8,128)(2,1)S(1)}, bf16[9,32,384]{2,1,0:T(8,128)(2,1)S(1)}, u32[]{:S(2)}, u32[]{:S(2)}) collective-permute-start(bf16[9,32,384]{2,1,0:T(8,128)(2,1)S(1)} %get-tuple-element.34), channel_id=1, source_target_pairs={{0,8},{1,9},{2,10},{3,11},{4,12},{5,13},{6,14},{7,15},{8,0},{9,1},... | collective-permute-start | bytes 663560 | tf_op jit(solution)/shard_map/ppermute | solution.py:216
  32.8 8.3 %collective-permute-start.1 = (bf16[9,32,384]{2,1,0:T(8,128)(2,1)S(1)}, bf16[9,32,384]{2,1,0:T(8,128)(2,1)S(1)}, u32[]{:S(2)}, u32[]{:S(2)}) collective-permute-start(bf16[9,32,384]{2,1,0:T(8,128)(2,1)S(1)} %get-tuple-element.35), channel_id=1, source_target_pairs={{0,16},{1,17},{2,18},{3,19},{4,20},{5,21},{6,22},{7,23},{8,24},{9,... | collective-permute-start | bytes 663560 | tf_op jit(solution)/shard_map/ppermute | solution.py:216
  34.4 9.9 %collective-permute-start.2 = (bf16[9,32,384]{2,1,0:T(8,128)(2,1)S(1)}, bf16[9,32,384]{2,1,0:T(8,128)(2,1)S(1)}, u32[]{:S(2)}, u32[]{:S(2)}) collective-permute-start(bf16[9,32,384]{2,1,0:T(8,128)(2,1)S(1)} %get-tuple-element.36), channel_id=1, source_target_pairs={{0,24},{1,25},{2,26},{3,27},{4,28},{5,29},{6,30},{7,31},{8,16},{9,... | collective-permute-start | bytes 663560 | tf_op jit(solution)/shard_map/ppermute | solution.py:216
  35.1 11.5 %copy-start.5 = (bf16[9,32,384]{2,1,0:T(8,128)(2,1)}, bf16[9,32,384]{2,1,0:T(8,128)(2,1)S(1)}, u32[]{:S(2)}) copy-start(bf16[9,32,384]{2,1,0:T(8,128)(2,1)S(1)} %collective-permute-done.refs_1_) | copy-start | bytes 663556
  41.2 5.4 %copy-start.6 = (bf16[9,32,384]{2,1,0:T(8,128)(2,1)}, bf16[9,32,384]{2,1,0:T(8,128)(2,1)S(1)}, u32[]{:S(2)}) copy-start(bf16[9,32,384]{2,1,0:T(8,128)(2,1)S(1)} %collective-permute-done.1.refs_2_) | copy-start | bytes 663556
  44.3 2.2 %copy-start.7 = (bf16[9,32,384]{2,1,0:T(8,128)(2,1)}, bf16[9,32,384]{2,1,0:T(8,128)(2,1)S(1)}, u32[]{:S(2)}) copy-start(bf16[9,32,384]{2,1,0:T(8,128)(2,1)S(1)} %collective-permute-done.2.refs_3_) | copy-start | bytes 663556
  62.1 0.9 copy-start.3
  112.8 3.5 %copy-start.4 = (f32[4,256,1]{2,1,0:T(8,128)S(1)}, f32[4,256,1]{2,1,0:T(8,128)}, u32[]{:S(2)}) copy-start(f32[4,256,1]{2,1,0:T(8,128)} %get-tuple-element.21) | copy-start | bytes 12292
  114.1 3.2 %collective-permute-start.10 = (f32[4,32,64]{1,2,0:T(8,128)S(1)}, f32[4,32,64]{1,2,0:T(8,128)S(1)}, u32[]{:S(2)}, u32[]{:S(2)}) collective-permute-start(f32[4,32,64]{1,2,0:T(8,128)S(1)} %get-tuple-element.40), channel_id=1, source_target_pairs={{0,8},{1,9},{2,10},{3,11},{4,12},{5,13},{6,14},{7,15},{8,0},{9,1},... | collective-permute-start | bytes 98312 | tf_op jit(solution)/shard_map/ppermute | solution.py:216
  114.8 6.4 %collective-permute-start.11 = (f32[4,32,64]{1,2,0:T(8,128)S(1)}, f32[4,32,64]{1,2,0:T(8,128)S(1)}, u32[]{:S(2)}, u32[]{:S(2)}) collective-permute-start(f32[4,32,64]{1,2,0:T(8,128)S(1)} %get-tuple-element.39), channel_id=1, source_target_pairs={{0,16},{1,17},{2,18},{3,19},{4,20},{5,21},{6,22},{7,23},{8,24},{9,... | collective-permute-start | bytes 98312 | tf_op jit(solution)/shard_map/ppermute | solution.py:216
  116.3 5.9 %collective-permute-start.12 = (f32[4,32,64]{1,2,0:T(8,128)S(1)}, f32[4,32,64]{1,2,0:T(8,128)S(1)}, u32[]{:S(2)}, u32[]{:S(2)}) collective-permute-start(f32[4,32,64]{1,2,0:T(8,128)S(1)} %get-tuple-element.38), channel_id=1, source_target_pairs={{0,24},{1,25},{2,26},{3,27},{4,28},{5,29},{6,30},{7,31},{8,16},{9,... | collective-permute-start | bytes 98312 | tf_op jit(solution)/shard_map/ppermute | solution.py:216

commit v2 on v1

v2 whole, which is shorter than its diff:
```python
import functools

import jax
import jax.numpy as jnp
from jax import lax
from jax.experimental import pallas as pl
from jax.experimental.pallas import tpu as pltpu
from jax.sharding import PartitionSpec as P


BINS = 64
LANES = 128
TILE = 16
GROUP_NODES = 4
CHUNK = 512
COLS = 256
VMEM_SMALL = 12 * 2**20
VMEM_LARGE = 24 * 2**20
VMEM_WHOLE = 60 * 2**20


hess_ridge = 1.0

F32 = jnp.float32
BF16 = jnp.bfloat16
I32 = jnp.int32
NT = (((1,), (1,)), ((), ()))
VMEM = pl.BlockSpec(memory_space=pltpu.VMEM)
SMEM = pl.BlockSpec(memory_space=pltpu.SMEM)


def iota(shape, dim):
    return lax.broadcasted_iota(I32, shape, dim)


def first_kernel(nr, nf, *refs):
    sources = refs[:6]
    out = refs[6]
    sent = refs[7 : 7 + nr]
    held = refs[7 + nr : 13 + nr]
    sems = refs[13 + nr]
    copies = [pltpu.make_async_copy(source, here, sems.at[i]) for i, (source, here) in enumerate(zip(sources, held))]
    for copy in copies:
        copy.start()
    split_feature, split_bin, margins, labels, bins, parents = held
    classes, own = margins.shape
    feat_dev = bins.shape[0]
    own_feats = feat_dev // nr
    feat = lax.axis_index("feat")
    base = feat * feat_dev
    row = lax.axis_index("rows")
    for copy in copies:
        copy.wait()
    par = parents[...]
    cuts = [slice(k * own, (k + 1) * own) for k in range(nf)]
    par_rows = jnp.concatenate([par[:, cut] for cut in cuts], axis=0).astype(F32).astype(BF16)
    for j in range(nr):
        first = pl.multiple_of(jnp.bitwise_xor(row, j) * own_feats, own_feats)
        for k, cut in enumerate(cuts):
            piece = bins[pl.ds(first, own_feats), cut]
            sent[j][k * own_feats : (k + 1) * own_feats, :] = piece.astype(F32).astype(BF16)
        sent[j][nf * own_feats :, :] = par_rows
    out[0:classes, :] = margins[...]
    right = jnp.zeros(par.shape, F32)
    for p in range(split_feature.shape[0]):
        local = split_feature[p] - base
        owned = jnp.logical_and(local >= 0, local < feat_dev)
        threshold = jnp.where(owned, split_bin[p], BINS)
        deciding = bins[pl.ds(jnp.clip(local, 0, feat_dev - 1), 1), :]
        right = right + jnp.where((par == p) & (deciding > threshold), 1.0, 0.0)
    label = 2.0 * labels[...].astype(F32).reshape(1, own)
    mine = iota((nf, own), 0) == feat
    out[classes:, :] = jnp.concatenate([right[:, cut] for cut in cuts], axis=0) + jnp.where(mine, label, 0.0)


def plan_kernel(groups, parents_per_group, spare, parents, slots, where, chunks):
    blocks, own = parents.shape
    group = parents[...].astype(I32) // parents_per_group
    hot = [(group == q).astype(F32) for q in range(groups)]
    earlier = (iota((own, own), 0) < iota((own, own), 1)).astype(F32).astype(BF16)
    ahead = jnp.dot(jnp.concatenate(hot, axis=0).astype(BF16), earlier, preferred_element_type=F32)
    lane = iota((blocks, LANES), 1)
    used = jnp.zeros((blocks, 1), I32)
    counts, starts = [], []
    slot = jnp.zeros((blocks, own), F32)
    table = jnp.zeros((blocks, LANES), I32)
    for q in range(groups):
        rows = jnp.sum(hot[q], axis=1, keepdims=True).astype(I32)
        counts.append((rows + TILE - 1) // TILE)
        starts.append(used)
        first = (used * TILE).astype(F32)
        slot = slot + hot[q] * (ahead[q * blocks : (q + 1) * blocks] + first)
        table = table + jnp.where(lane == q, counts[q], 0)
        used = used + counts[q]
    slots[...] = slot
    above = (iota((blocks, blocks), 1) < iota((blocks, blocks), 0)).astype(F32).astype(BF16)
    before = jnp.dot(above, table.astype(F32).astype(BF16), preferred_element_type=F32).astype(I32)
    region = jnp.zeros((1, 1), I32)
    place = jnp.where(lane >= used, spare, 0)
    row8 = iota((8, LANES), 0)
    lane8 = iota((8, LANES), 1)
    spans = jnp.zeros((8, LANES), I32)
    per_chunk = CHUNK // TILE
    for q in range(groups):
        inside = (lane >= starts[q]) & (lane < starts[q] + counts[q])
        at = region * per_chunk + before[:, q : q + 1] + lane - starts[q]
        place = place + jnp.where(inside, at, 0)
        total = jnp.sum(counts[q], axis=0, keepdims=True)
        length = (total + per_chunk - 1) // per_chunk
        spans = spans + jnp.where((lane8 == q) & (row8 == 0), region, 0)
        spans = spans + jnp.where((lane8 == q) & (row8 == 1), length, 0)
        region = region + length
    where[...] = place
    chunks[...] = spans


def put_block(values, slot, tiles, where, block, out):
    own = values.shape[1]
    hot = (iota((tiles * TILE, own), 0) == slot.astype(I32)).astype(F32).astype(BF16)
    placed = lax.dot_general(hot, values, NT, preferred_element_type=F32).astype(BF16)
    for t in range(tiles):
        to = pl.multiple_of(where[block, t] * TILE, TILE)
        out[pl.ds(to, TILE), :] = placed[t * TILE : (t + 1) * TILE]


def sort_bins_kernel(nr, nf, tiles, unroll, where, *refs):
    bins = refs[:nr]
    slots, out = refs[nr:]
    own_feats = (bins[0].shape[0] - nf) // nf
    copies = LANES // own_feats
    for j in range(nr):

        @pl.loop(0, nf // unroll)
        def _(i):
            for u in range(unroll):
                k = i * unroll + u
                block = j * nf + k
                values = bins[j][pl.ds(pl.multiple_of(k * own_feats, own_feats), own_feats), :]
                values = jnp.concatenate([values] * copies, axis=0)
                put_block(values, slots[pl.ds(block, 1), :], tiles, where, block, out)


def put_grads(sizes, jc, where, source, parents, slots, leaf, grads):
    _, nf, ny, lo, hi, own, _, classes, nodes, tiles = sizes
    me_feat = lax.axis_index("feat")
    code_row = hi * classes
    rest = leaf[...]
    leaf_parts = []
    for _ in range(3):
        leaf_parts.append(rest.astype(BF16))
        rest = rest - leaf_parts[-1].astype(F32)
    leaf_parts = jnp.concatenate(leaf_parts, axis=1)
    grads[...] = jnp.zeros(grads.shape, BF16)

    @pl.loop(0, ny)
    def _(jy):
        j = jy * 2 + jc
        for jx, jz in [(jx, jz) for jx in range(lo) for jz in range(hi)]:
            yx = jy * lo + jx
            k = jnp.bitwise_xor(me_feat, jz * lo + jx)
            block = j * nf + k
            margins = source[yx, jz * classes : (jz + 1) * classes, :]
            code = source[jy * lo, pl.ds(code_row + k, 1), :]
            for other in range(1, lo):
                code = code + source[jy * lo + other, pl.ds(code_row + k, 1), :]
            label = jnp.floor(code * 0.5)
            right = code - 2.0 * label
            node = 2.0 * parents[pl.ds(block, 1), :] + right
            node_hot = (node == iota((nodes, own), 0).astype(F32)).astype(F32).astype(BF16)
            moved = jnp.dot(leaf_parts, jnp.concatenate([node_hot] * 3, axis=0), preferred_element_type=F32)
            logits = margins + moved
            powers = jnp.exp(logits - jnp.max(logits, axis=0, keepdims=True))
            prob = powers / jnp.sum(powers, axis=0, keepdims=True)
            hot = label == iota((classes, own), 0).astype(F32)
            gradient = prob - jnp.where(hot, 1.0, 0.0)
            hessian = 2.0 * prob * (1.0 - prob)
            pad = jnp.broadcast_to(node, (LANES - 2 * classes, own))
            columns = jnp.concatenate([gradient, hessian, pad], axis=0).astype(BF16)
            put_block(columns, slots[pl.ds(block, 1), :], tiles, where, block, grads)


def near_kernel(sizes, where, near, parents, slots, leaf, grads):
    put_grads(sizes, 0, where, near, parents, slots, leaf, grads)


def level_kernel(sizes, where, chunks, near_grads, far, parents, slots, bins, leaf, gains, totals, grads, acc):
    _, _, _, _, _, _, own_feats, classes, nodes, _ = sizes
    groups = nodes // GROUP_NODES
    half = GROUP_NODES * classes
    width = BINS * own_feats
    put_grads(sizes, 1, where, far, parents, slots, leaf, grads)
    lane_bin = (iota((1, LANES), 1) // own_feats).astype(F32)
    bins_per = LANES // own_feats

    @pl.loop(0, groups)
    def _(q):
        first = chunks[0, q]

        @pl.when(chunks[1, q] == 0)
        def _():
            acc[q] = jnp.zeros(acc.shape[1:], F32)

        @pl.loop(0, chunks[1, q])
        def _(i):
            at = pl.multiple_of((first + i) * CHUNK, CHUNK)
            columns = (near_grads[pl.ds(at, CHUNK), :] + grads[pl.ds(at, CHUNK), :]).T
            node = columns[2 * classes : 2 * classes + classes, :]
            parts = []
            for side in range(2):
                value = columns[side * classes : (side + 1) * classes, :]
                for n in range(GROUP_NODES):
                    wanted = (q * GROUP_NODES + n).astype(F32).astype(BF16)
                    parts.append(jnp.where(node == wanted, value, jnp.zeros_like(value)))
            weights = jnp.concatenate(parts, axis=0)
            value = (bins[pl.ds(at, CHUNK), :].astype(F32) - lane_bin).astype(BF16)
            for m in range(width // COLS):
                below = []
                for s in range(COLS // LANES):
                    limit = (m * (COLS // LANES) + s) * bins_per
                    below.append(
                        jnp.where(value <= jnp.asarray(limit, BF16), jnp.asarray(1, BF16), jnp.asarray(0, BF16))
                    )
                below = jnp.concatenate(below, axis=1)
                span = slice(m * COLS, (m + 1) * COLS)
                so_far = jnp.where(i == 0, 0.0, acc[q, :, span])
                acc[q, :, span] = so_far + jnp.dot(weights, below, preferred_element_type=F32)

        whole = acc[q, :, width - 1 : width]
        totals[q] = whole
        grad_whole = whole[:half]
        hess_whole = whole[half:]
        parent_score = grad_whole * grad_whole / (hess_whole + hess_ridge)
        for m in range(width // LANES):
            span = slice(m * LANES, (m + 1) * LANES)
            grad_left = acc[q, :half, span]
            hess_left = acc[q, half:, span]
            grad_right = grad_whole - grad_left
            hess_right = hess_whole - hess_left
            score = (
                grad_left * grad_left / (hess_left + hess_ridge)
                + grad_right * grad_right / (hess_right + hess_ridge)
                - parent_score
            )
            for n in range(GROUP_NODES):
                total = jnp.sum(score[n * classes : (n + 1) * classes], axis=0, keepdims=True)
                gains[q, n : n + 1, span] = total * (1.0 / classes)


def flip_by(value, index, count):
    step = 1
    while step < count:
        shaped = value.reshape((count // (2 * step), 2, step) + value.shape[1:])
        flipped = jnp.flip(shaped, axis=1)
        value = jnp.where((index // step) % 2 == 1, flipped, shaped).reshape(value.shape)
        step *= 2
    return value


def swap(value, axes, sizes, offsets):
    total = 1
    for size in sizes:
        total *= size
    flat = 0
    for size, offset in zip(sizes, offsets):
        flat = flat * size + offset
    return lax.ppermute(value, axes, [(i, i ^ flat) for i in range(total)])


def body(margins, labels, row_bins, parents, split_feature, split_bin, leaf_values):
    feat_dev, group_rows = row_bins.shape
    own, classes = margins.shape
    nodes = leaf_values.shape[0]
    parent_count = split_feature.shape[0]
    nf, nr = lax.axis_size("feat"), lax.axis_size("rows")
    row = lax.axis_index("rows")
    own_feats = feat_dev // nr
    lo, ny = 2, nr // 2
    hi = nf // lo
    groups = nodes // GROUP_NODES
    blocks = nr * nf
    width = BINS * own_feats
    axes, sizes = ("rows", "feat"), (nr, nf)

    message_rows = nf * own_feats + nf
    first_inputs = (split_feature, split_bin, margins.T, labels, row_bins, parents.reshape(1, group_rows))
    first, *sent = pl.pallas_call(
        functools.partial(first_kernel, nr, nf),
        out_shape=[jax.ShapeDtypeStruct((classes + nf, own), F32)]
        + [jax.ShapeDtypeStruct((message_rows, own), BF16)] * nr,
        in_specs=[pl.BlockSpec(memory_space=pltpu.HBM)] * 6,
        out_specs=[VMEM] * (nr + 1),
        scratch_shapes=[pltpu.SMEM(x.shape, x.dtype) for x in first_inputs[:2]]
        + [pltpu.VMEM(x.shape, x.dtype) for x in first_inputs[2:]]
        + [pltpu.SemaphoreType.DMA((6,))],
        compiler_params=pltpu.CompilerParams(vmem_limit_bytes=VMEM_WHOLE),
        name="first",
    )(*first_inputs)

    bins_by = [sent[0]]
    for j in range(1, nr):
        bins_by.append(swap(sent[j], axes, sizes, (j, 0)))
    along_z = [first] + [swap(first, axes, sizes, (0, lo * j)) for j in range(1, hi)]

    all_parents = jnp.concatenate([b[nf * own_feats :] for b in bins_by]).astype(F32)

    second = jnp.concatenate([m[:classes] for m in along_z] + [sum(m[classes:] for m in along_z)], axis=0)
    plane = []
    for jy in range(ny):
        for jx in range(lo):
            plane.append(second if jy + jx == 0 else swap(second, axes, sizes, (2 * jy, jx)))
    near = jnp.stack(plane)
    far = swap(near, axes, sizes, (1, 0))

    tiles = own // TILE + groups * (TILE - 1) // TILE
    spare = blocks * tiles + groups * (CHUNK // TILE - 1)
    ordered_rows = (spare + 1) * TILE
    slots, where, chunks = pl.pallas_call(
        functools.partial(plan_kernel, groups, parent_count // groups, spare),
        out_shape=(
            jax.ShapeDtypeStruct((blocks, own), F32),
            jax.ShapeDtypeStruct((blocks, LANES), I32),
            jax.ShapeDtypeStruct((8, LANES), I32),
        ),
        in_specs=[VMEM],
        out_specs=(VMEM,) * 3,
        compiler_params=pltpu.CompilerParams(vmem_limit_bytes=VMEM_SMALL),
        name="plan",
    )(all_parents)

    ordered_bins = pl.pallas_call(
        functools.partial(sort_bins_kernel, nr, nf, tiles, 8),
        out_shape=jax.ShapeDtypeStruct((ordered_rows, LANES), BF16),
        in_specs=[SMEM] + [VMEM] * (nr + 1),
        out_specs=VMEM,
        compiler_params=pltpu.CompilerParams(vmem_limit_bytes=VMEM_SMALL),
        name="sort_bins",
    )(where, *bins_by, slots)

    shape = (nr, nf, ny, lo, hi, own, own_feats, classes, nodes, tiles)
    leaf_t = leaf_values.T
    near_grads = pl.pallas_call(
        functools.partial(near_kernel, shape),
        out_shape=jax.ShapeDtypeStruct((ordered_rows, LANES), BF16),
        in_specs=[SMEM] + [VMEM] * 4,
        out_specs=VMEM,
        compiler_params=pltpu.CompilerParams(vmem_limit_bytes=VMEM_SMALL),
        name="near",
    )(where, near, all_parents, slots, leaf_t)

    gains, totals = pl.pallas_call(
        functools.partial(level_kernel, shape),
        out_shape=(
            jax.ShapeDtypeStruct((groups, GROUP_NODES, width), F32),
            jax.ShapeDtypeStruct((groups, 2 * GROUP_NODES * classes, 1), F32),
        ),
        in_specs=[SMEM] * 2 + [VMEM] * 6,
        out_specs=(VMEM, VMEM),
        scratch_shapes=[
            pltpu.VMEM((ordered_rows, LANES), BF16),
            pltpu.VMEM((groups, 2 * GROUP_NODES * classes, width), F32),
        ],
        compiler_params=pltpu.CompilerParams(vmem_limit_bytes=VMEM_LARGE),
        name="level",
    )(where, chunks, near_grads, far, all_parents, slots, ordered_bins, leaf_t)

    node_totals = totals.reshape(groups, 2, GROUP_NODES, classes).transpose(0, 2, 1, 3).reshape(nodes, 2 * classes)

    kept_nodes = nodes // nr
    relative = flip_by(gains.reshape(nr, kept_nodes, width), row, nr)
    kept = [relative[0]] + [swap(relative[j], axes, sizes, (j, 0)) for j in range(1, nr)]
    kept = flip_by(jnp.stack(kept), row, nr).reshape(nr, kept_nodes, BINS, own_feats)
    split_gains = kept.transpose(1, 0, 3, 2).reshape(kept_nodes, feat_dev, BINS)
    return split_gains, node_totals


def solution(mesh):
    return jax.shard_map(
        body,
        mesh=mesh,
        in_specs=(
            P(("rows", "feat"), None),
            P(("rows", "feat")),
            P("feat", "rows"),
            P("rows"),
            P(),
            P(),
            P(),
        ),
        out_specs=(P("rows", "feat", None), P()),
        check_vma=False,
    )
```

time: 124 us -> 85.6 us (0.69)
  Pallas kernels: 67.6 us -> 41.9 us
  local copies, waits for them, and re-layouts: 10.8 us -> 5.21 us
  waiting for transfers between devices: 26.8 us -> 22.9 us
  other arithmetic: 3.79 us -> 1.13 us
    pallas_call x1, Pallas kernels: 49.8 us -> 29.2 us  [body(): pl.pallas_call(functools.partial(level_kernel, shape), out_shape=(jax.Sha...]
    pallas_call x2 -> x4, Pallas kernels: 17.9 us -> 12.7 us  [the longest x1 5.13 us: body(): pl.pallas_call(functools.partial(near_kernel, shape), out_shape=jax.Shape...]
    ppermute x13, waiting for transfers between devices: 26.8 us -> 22.9 us  [swap(): return lax.ppermute(value, axes, [(i, i ^ flat) for i in range(total)])]
    reshape x3 -> x0, local copies, waits for them, and re-layouts: 2.49 us -> none  [the longest x1 1.24 us: body(): labels.reshape(1, own)]
    unnamed x24 -> x8, local copies, waits for them, and re-layouts: 4.48 us -> 3.35 us
  transfers between devices with their start and end apart: 13 -> 13, of which waited for: 8 -> 9; matrix products, arithmetic and copies ran while one was open for 5% -> 4% of each run, Pallas kernels for 13% -> 12%
where the time goes in v2:
time: 85.6 us; the launch traced here: 85.2 us
  Pallas kernels  41.9 us (49%)
  waiting for transfers between devices  22.9 us (27%)
  starting transfers between devices  13.3 us (16%)
  local copies, waits for them, and re-layouts  5.21 us (6%)
  other arithmetic  1.13 us (1%)
    pallas_call x1, Pallas kernels, body(): pl.pallas_call(functools.partial(level_kernel, shape), out_shape=(jax.Sha...  29.2 us
    ppermute x13, waiting for transfers between devices, swap(): return lax.ppermute(value, axes, [(i, i ^ flat) for i in range(total)])  22.9 us
    ppermute x13, starting transfers between devices, swap(): return lax.ppermute(value, axes, [(i, i ^ flat) for i in range(total)])  13.3 us
    pallas_call x1, Pallas kernels, body(): pl.pallas_call(functools.partial(near_kernel, shape), out_shape=jax.Shape...  5.13 us
    pallas_call x1, Pallas kernels, body(): pl.pallas_call(functools.partial(sort_bins_kernel, nr, nf, tiles, 8), out...  4.64 us
    unnamed x8, local copies, waits for them, and re-layouts  3.35 us
    pallas_call x1, Pallas kernels, body(): pl.pallas_call(functools.partial(first_kernel, nr, nf), out_shape=[jax.Sh...  2.5 us
  transfers between devices with their start and end apart: 13, of which 9 were waited for; matrix products, arithmetic and copies ran while one was open for 4% of the time, Pallas kernels for 12%

profile of v2, /device:TPU:0, one launch (start us, length us, event | category | flops | bytes accessed | tf_op | source)
XLA Modules:
  0.0 85.2 jit_solution(3014983666576067416)
XLA Ops:
  0.6 2.5 %first.1 = (f32[40,384]{1,0:T(8,128)}, bf16[264,384]{1,0:T(8,128)(2,1)}, bf16[264,384]{1,0:T(8,128)(2,1)}, bf16[264,384]{1,0:T(8,128)(2,1)}, bf16[264,384]{1,0:T(8,128)(2,1)}) custom-call(s32[8]{0:T(128)} %refs_0_.1, s32[8]{0:T(128)} %refs_1_.1, f32[32,384]{1,0:T(8,128)} %bitcast.38, s32[384]{0:T(512)} %refs_3_.1, s32[128,3072]{1,0:T(8,128)} %refs_4_.1, ...), custom_call_target="tpu_custom_call" | custom-call | tf_op jit(solution)/shard_map/first/pallas_call | solution.py:286
  3.1 3.1 %collective-permute-start.3 = (f32[40,384]{1,0:T(8,128)}, f32[40,384]{1,0:T(8,128)S(1)}, u32[]{:S(2)}, u32[]{:S(2)}) collective-permute-start(f32[40,384]{1,0:T(8,128)} %get-tuple-element.18), channel_id=1, source_target_pairs={{0,2},{1,3},{2,0},{3,1},{4,6},{5,7},{6,4},{7,5},{8,10},{9,11},{10,... | collective-permute-start | bytes 184328 | tf_op jit(solution)/shard_map/ppermute | solution.py:266
  6.3 2.6 %collective-permute-start.4 = (f32[40,384]{1,0:T(8,128)}, f32[40,384]{1,0:T(8,128)S(1)}, u32[]{:S(2)}, u32[]{:S(2)}) collective-permute-start(f32[40,384]{1,0:T(8,128)} %get-tuple-element.18), channel_id=1, source_target_pairs={{0,4},{1,5},{2,6},{3,7},{4,0},{5,1},{6,2},{7,3},{8,12},{9,13},{10,... | collective-permute-start | bytes 184328 | tf_op jit(solution)/shard_map/ppermute | solution.py:266
  8.9 0.0 collective-permute-start.5
  8.9 0.9 %slice_dynamic-update-slice_fusion.3 = f32[136,384]{1,0:T(8,128)S(1)} fusion(f32[40,384]{1,0:T(8,128)} %get-tuple-element.18), kind=kLoop, calls=%fused_computation.11 | loop fusion | bytes 98304
  9.7 0.0 collective-permute-done.3
  9.7 3.1 %collective-permute-done.4 = f32[40,384]{1,0:T(8,128)S(1)} collective-permute-done((f32[40,384]{1,0:T(8,128)}, f32[40,384]{1,0:T(8,128)S(1)}, u32[]{:S(2)}, u32[]{:S(2)}) %collective-permute-start.4) | collective-permute-done | bytes 61472 | tf_op jit(solution)/shard_map/ppermute | solution.py:266
  12.8 2.2 %collective-permute-done.5 = f32[40,384]{1,0:T(8,128)S(1)} collective-permute-done((f32[40,384]{1,0:T(8,128)}, f32[40,384]{1,0:T(8,128)S(1)}, u32[]{:S(2)}, u32[]{:S(2)}) %collective-permute-start.5) | collective-permute-done | bytes 61472 | tf_op jit(solution)/shard_map/ppermute | solution.py:266
  15.1 0.7 fusion.2
  15.8 2.4 %collective-permute-start.8 = (f32[136,384]{1,0:T(8,128)S(1)}, f32[136,384]{1,0:T(8,128)S(1)}, u32[]{:S(2)}, u32[]{:S(2)}) collective-permute-start(f32[136,384]{1,0:T(8,128)S(1)} %fusion.2), channel_id=1, source_target_pairs={{0,17},{1,16},{2,19},{3,18},{4,21},{5,20},{6,23},{7,22},{8,25},{9,... | collective-permute-start | bytes 626696 | tf_op jit(solution)/shard_map/ppermute | solution.py:266
  18.2 0.5 collective-permute-start.7
  18.8 0.5 collective-permute-start.6
  19.3 5.2 %collective-permute-done.8 = f32[136,384]{1,0:T(8,128)S(1)} collective-permute-done((f32[136,384]{1,0:T(8,128)S(1)}, f32[136,384]{1,0:T(8,128)S(1)}, u32[]{:S(2)}, u32[]{:S(2)}) %collective-permute-start.8) | collective-permute-done | bytes 208928 | tf_op jit(solution)/shard_map/ppermute | solution.py:266
  24.4 2.0 %collective-permute-done.7 = f32[136,384]{1,0:T(8,128)S(1)} collective-permute-done((f32[136,384]{1,0:T(8,128)S(1)}, f32[136,384]{1,0:T(8,128)S(1)}, u32[]{:S(2)}, u32[]{:S(2)}) %collective-permute-start.7) | collective-permute-done | bytes 208928 | tf_op jit(solution)/shard_map/ppermute | solution.py:266
  26.5 0.1 collective-permute-done.6
  26.6 0.1 pad_maximum_fusion.near
  26.6 0.1 collective-permute-start.9
  26.7 1.5 %collective-permute-start.2 = (bf16[264,384]{1,0:T(8,128)(2,1)}, bf16[264,384]{1,0:T(8,128)(2,1)S(1)}, u32[]{:S(2)}, u32[]{:S(2)}) collective-permute-start(bf16[264,384]{1,0:T(8,128)(2,1)} %get-tuple-element.15), channel_id=1, source_target_pairs={{0,24},{1,25},{2,26},{3,27},{4,28},{5,29},{6,30},{7,31},{8,16},{9,... | collective-permute-start | bytes 608264 | tf_op jit(solution)/shard_map/ppermute | solution.py:266
  28.2 0.6 collective-permute-start.1
  28.9 0.0 collective-permute-start
  28.9 0.7 slice.48
  29.5 0.8 copy.15
  30.3 3.7 %collective-permute-done.2.refs_3_ = bf16[264,384]{1,0:T(8,128)(2,1)S(1)} collective-permute-done((bf16[264,384]{1,0:T(8,128)(2,1)}, bf16[264,384]{1,0:T(8,128)(2,1)S(1)}, u32[]{:S(2)}, u32[]{:S(2)}) %collective-permute-start.2) | collective-permute-done | bytes 202784 | tf_op jit(solution)/shard_map/ppermute | solution.py:266
  34.0 4.7 %collective-permute-done.1.refs_2_ = bf16[264,384]{1,0:T(8,128)(2,1)S(1)} collective-permute-done((bf16[264,384]{1,0:T(8,128)(2,1)}, bf16[264,384]{1,0:T(8,128)(2,1)S(1)}, u32[]{:S(2)}, u32[]{:S(2)}) %collective-permute-start.1) | collective-permute-done | bytes 202784 | tf_op jit(solution)/shard_map/ppermute | solution.py:266
  38.7 0.0 collective-permute-done.refs_1_
  38.7 0.4 plan.1
  39.1 0.0 copy-start
  39.1 0.9 %copy-done = bf16[264,384]{1,0:T(8,128)(2,1)S(1)} copy-done((bf16[264,384]{1,0:T(8,128)(2,1)S(1)}, bf16[264,384]{1,0:T(8,128)(2,1)}, u32[]{:S(2)}) %copy-start) | copy-done | bytes 202776
  40.0 4.6 %sort_bins.1.bins = bf16[15824,128]{1,0:T(8,128)(2,1)S(1)} custom-call(s32[32,128]{1,0:T(8,128)S(1)} %get-tuple-element.16.where, bf16[264,384]{1,0:T(8,128)(2,1)S(1)} %copy-done, bf16[264,384]{1,0:T(8,128)(2,1)S(1)} %collective-permute-done.refs_1_, bf16[264,384]{1,0:T(8,128)(2,1)S(1)} %collective-permute-done.1.refs_2_, ...), custom_call_target="tpu_custom_call" | custom-call | tf_op jit(solution)/shard_map/sort_bins/pallas_call | solution.py:330
  44.7 5.1 %near.1.near_grads = bf16[15824,128]{1,0:T(8,128)(2,1)S(1)} custom-call(s32[32,128]{1,0:T(8,128)S(1)} %get-tuple-element.16.where, f32[4,136,384]{2,1,0:T(8,128)S(1)} %pad_maximum_fusion.near, f32[32,384]{1,0:T(8,128)S(1)} %maximum_convert_fusion.parents, f32[32,384]{1,0:T(8,128)S(1)} %get-tuple-element.19.slots.refs_4_, f32[32,16]{1,0:T(8,128)S(1)} %bitcast.26), custom_call_target="tpu_custom_call" | custom-call | tf_op jit(solution)/shard_map/near/pallas_call | solution.py:341
  49.8 0.0 collective-permute-done.9.far
  49.8 29.2 %level.1 = (f32[4,4,2048]{2,1,0:T(4,128)S(1)}, f32[4,256,1]{2,1,0:T(8,128)S(1)}) custom-call(s32[32,128]{1,0:T(8,128)S(1)} %get-tuple-element.16.where, s32[8,128]{1,0:T(8,128)S(1)} %get-tuple-element.17.chunks, bf16[15824,128]{1,0:T(8,128)(2,1)S(1)} %near.1.near_grads, f32[4,136,384]{2,1,0:T(8,128)S(1)} %collective-permute-done.9.far, ...), custom_call_target="tpu_custom_call" | custom-call | tf_op jit(solution)/shard_map/level/pallas_call | solution.py:350
  79.2 0.6 collective-permute-start.12
  79.8 1.0 %collective-permute-start.11 = (f32[4,2048]{1,0:T(4,128)S(1)}, f32[4,2048]{1,0:T(4,128)S(1)}, u32[]{:S(2)}, u32[]{:S(2)}) collective-permute-start(f32[4,2048]{1,0:T(4,128)S(1)} %get-tuple-element.28), channel_id=1, source_target_pairs={{0,16},{1,17},{2,18},{3,19},{4,20},{5,21},{6,22},{7,23},{8,24},{9,... | collective-permute-start | bytes 98312 | tf_op jit(solution)/shard_map/ppermute | solution.py:266
  80.7 0.4 collective-permute-start.10
  81.1 0.2 reduce
  81.3 0.1 reshape.30
  81.4 0.7 reshape.31
  82.1 0.8 collective-permute-done.12
  82.9 1.1 %collective-permute-done.11 = f32[4,2048]{1,0:T(4,128)S(1)} collective-permute-done((f32[4,2048]{1,0:T(4,128)S(1)}, f32[4,2048]{1,0:T(4,128)S(1)}, u32[]{:S(2)}, u32[]{:S(2)}) %collective-permute-start.11) | collective-permute-done | bytes 32800 | tf_op jit(solution)/shard_map/ppermute | solution.py:266
  84.0 0.0 collective-permute-done.10
  84.1 0.2 reshape_reshape.11
  84.3 0.2 copy.16
  84.5 0.8 copy.18
  (14 shorter events, 0.2 us)
Async XLA Ops:
  3.1 6.6 %collective-permute-start.3 = (f32[40,384]{1,0:T(8,128)}, f32[40,384]{1,0:T(8,128)S(1)}, u32[]{:S(2)}, u32[]{:S(2)}) collective-permute-start(f32[40,384]{1,0:T(8,128)} %get-tuple-element.18), channel_id=1, source_target_pairs={{0,2},{1,3},{2,0},{3,1},{4,6},{5,7},{6,4},{7,5},{8,10},{9,11},{10,... | collective-permute-start | bytes 184328 | tf_op jit(solution)/shard_map/ppermute | solution.py:266
  6.3 6.6 %collective-permute-start.4 = (f32[40,384]{1,0:T(8,128)}, f32[40,384]{1,0:T(8,128)S(1)}, u32[]{:S(2)}, u32[]{:S(2)}) collective-permute-start(f32[40,384]{1,0:T(8,128)} %get-tuple-element.18), channel_id=1, source_target_pairs={{0,4},{1,5},{2,6},{3,7},{4,0},{5,1},{6,2},{7,3},{8,12},{9,13},{10,... | collective-permute-start | bytes 184328 | tf_op jit(solution)/shard_map/ppermute | solution.py:266
  8.9 6.2 %collective-permute-start.5 = (f32[40,384]{1,0:T(8,128)}, f32[40,384]{1,0:T(8,128)S(1)}, u32[]{:S(2)}, u32[]{:S(2)}) collective-permute-start(f32[40,384]{1,0:T(8,128)} %get-tuple-element.18), channel_id=1, source_target_pairs={{0,6},{1,7},{2,4},{3,5},{4,2},{5,3},{6,0},{7,1},{8,14},{9,15},{10,... | collective-permute-start | bytes 184328 | tf_op jit(solution)/shard_map/ppermute | solution.py:266
  15.8 8.6 %collective-permute-start.8 = (f32[136,384]{1,0:T(8,128)S(1)}, f32[136,384]{1,0:T(8,128)S(1)}, u32[]{:S(2)}, u32[]{:S(2)}) collective-permute-start(f32[136,384]{1,0:T(8,128)S(1)} %fusion.2), channel_id=1, source_target_pairs={{0,17},{1,16},{2,19},{3,18},{4,21},{5,20},{6,23},{7,22},{8,25},{9,... | collective-permute-start | bytes 626696 | tf_op jit(solution)/shard_map/ppermute | solution.py:266
  18.2 8.2 %collective-permute-start.7 = (f32[136,384]{1,0:T(8,128)S(1)}, f32[136,384]{1,0:T(8,128)S(1)}, u32[]{:S(2)}, u32[]{:S(2)}) collective-permute-start(f32[136,384]{1,0:T(8,128)S(1)} %fusion.2), channel_id=1, source_target_pairs={{0,16},{1,17},{2,18},{3,19},{4,20},{5,21},{6,22},{7,23},{8,24},{9,... | collective-permute-start | bytes 626696 | tf_op jit(solution)/shard_map/ppermute | solution.py:266
  18.8 7.8 %collective-permute-start.6 = (f32[136,384]{1,0:T(8,128)S(1)}, f32[136,384]{1,0:T(8,128)S(1)}, u32[]{:S(2)}, u32[]{:S(2)}) collective-permute-start(f32[136,384]{1,0:T(8,128)S(1)} %fusion.2), channel_id=1, source_target_pairs={{0,1},{1,0},{2,3},{3,2},{4,5},{5,4},{6,7},{7,6},{8,9},{9,8},{10,11... | collective-permute-start | bytes 626696 | tf_op jit(solution)/shard_map/ppermute | solution.py:266
  26.6 23.2 %collective-permute-start.9 = (f32[4,136,384]{2,1,0:T(8,128)S(1)}, f32[4,136,384]{2,1,0:T(8,128)S(1)}, u32[]{:S(2)}, u32[]{:S(2)}) collective-permute-start(f32[4,136,384]{2,1,0:T(8,128)S(1)} %pad_maximum_fusion.near), channel_id=1, source_target_pairs={{0,8},{1,9},{2,10},{3,11},{4,12},{5,13},{6,14},{7,15},{8,0},{9,1},... | collective-permute-start | bytes 2506760 | tf_op jit(solution)/shard_map/ppermute | solution.py:266
  26.7 7.3 %collective-permute-start.2 = (bf16[264,384]{1,0:T(8,128)(2,1)}, bf16[264,384]{1,0:T(8,128)(2,1)S(1)}, u32[]{:S(2)}, u32[]{:S(2)}) collective-permute-start(bf16[264,384]{1,0:T(8,128)(2,1)} %get-tuple-element.15), channel_id=1, source_target_pairs={{0,24},{1,25},{2,26},{3,27},{4,28},{5,29},{6,30},{7,31},{8,16},{9,... | collective-permute-start | bytes 608264 | tf_op jit(solution)/shard_map/ppermute | solution.py:266
  28.2 10.4 %collective-permute-start.1 = (bf16[264,384]{1,0:T(8,128)(2,1)}, bf16[264,384]{1,0:T(8,128)(2,1)S(1)}, u32[]{:S(2)}, u32[]{:S(2)}) collective-permute-start(bf16[264,384]{1,0:T(8,128)(2,1)} %get-tuple-element.14), channel_id=1, source_target_pairs={{0,16},{1,17},{2,18},{3,19},{4,20},{5,21},{6,22},{7,23},{8,24},{9,... | collective-permute-start | bytes 608264 | tf_op jit(solution)/shard_map/ppermute | solution.py:266
  28.9 9.8 %collective-permute-start = (bf16[264,384]{1,0:T(8,128)(2,1)}, bf16[264,384]{1,0:T(8,128)(2,1)S(1)}, u32[]{:S(2)}, u32[]{:S(2)}) collective-permute-start(bf16[264,384]{1,0:T(8,128)(2,1)} %get-tuple-element.13), channel_id=1, source_target_pairs={{0,8},{1,9},{2,10},{3,11},{4,12},{5,13},{6,14},{7,15},{8,0},{9,1},... | collective-permute-start | bytes 608264 | tf_op jit(solution)/shard_map/ppermute | solution.py:266
  39.1 0.9 %copy-start = (bf16[264,384]{1,0:T(8,128)(2,1)S(1)}, bf16[264,384]{1,0:T(8,128)(2,1)}, u32[]{:S(2)}) copy-start(bf16[264,384]{1,0:T(8,128)(2,1)} %get-tuple-element.12.refs_0_) | copy-start | bytes 608260
  79.2 3.7 %collective-permute-start.12 = (f32[4,2048]{1,0:T(4,128)S(1)}, f32[4,2048]{1,0:T(4,128)S(1)}, u32[]{:S(2)}, u32[]{:S(2)}) collective-permute-start(f32[4,2048]{1,0:T(4,128)S(1)} %get-tuple-element.27), channel_id=1, source_target_pairs={{0,24},{1,25},{2,26},{3,27},{4,28},{5,29},{6,30},{7,31},{8,16},{9,... | collective-permute-start | bytes 98312 | tf_op jit(solution)/shard_map/ppermute | solution.py:266
  79.8 4.2 %collective-permute-start.11 = (f32[4,2048]{1,0:T(4,128)S(1)}, f32[4,2048]{1,0:T(4,128)S(1)}, u32[]{:S(2)}, u32[]{:S(2)}) collective-permute-start(f32[4,2048]{1,0:T(4,128)S(1)} %get-tuple-element.28), channel_id=1, source_target_pairs={{0,16},{1,17},{2,18},{3,19},{4,20},{5,21},{6,22},{7,23},{8,24},{9,... | collective-permute-start | bytes 98312 | tf_op jit(solution)/shard_map/ppermute | solution.py:266
  80.7 3.3 %collective-permute-start.10 = (f32[4,2048]{1,0:T(4,128)S(1)}, f32[4,2048]{1,0:T(4,128)S(1)}, u32[]{:S(2)}, u32[]{:S(2)}) collective-permute-start(f32[4,2048]{1,0:T(4,128)S(1)} %get-tuple-element.29), channel_id=1, source_target_pairs={{0,8},{1,9},{2,10},{3,11},{4,12},{5,13},{6,14},{7,15},{8,0},{9,1},... | collective-permute-start | bytes 98312 | tf_op jit(solution)/shard_map/ppermute | solution.py:266

commit v3 on v2

--- a/solution.py
+++ b/solution.py
@@ -12,10 +12,11 @@
 LANES = 128
 TILE = 16
 GROUP_NODES = 4
-CHUNK = 512
+CHUNK = 256
+PIECES = (2048, 1024, 512, 256)
 COLS = 256
 VMEM_SMALL = 12 * 2**20
-VMEM_LARGE = 24 * 2**20
+VMEM_MORE = 6 * 2**20
 VMEM_WHOLE = 60 * 2**20
 
 
@@ -174,8 +175,9 @@
             hot = label == iota((classes, own), 0).astype(F32)
             gradient = prob - jnp.where(hot, 1.0, 0.0)
             hessian = 2.0 * prob * (1.0 - prob)
-            pad = jnp.broadcast_to(node, (LANES - 2 * classes, own))
-            columns = jnp.concatenate([gradient, hessian, pad], axis=0).astype(BF16)
+            member = node - GROUP_NODES * jnp.floor(node * (1.0 / GROUP_NODES))
+            parts = [jnp.where(member == n, v, 0.0) for v in (gradient, hessian) for n in range(GROUP_NODES)]
+            columns = jnp.concatenate(parts, axis=0).astype(BF16)
             put_block(columns, slots[pl.ds(block, 1), :], tiles, where, block, grads)
 
 
@@ -189,8 +191,11 @@
     half = GROUP_NODES * classes
     width = BINS * own_feats
     put_grads(sizes, 1, where, far, parents, slots, leaf, grads)
+    bins_per = LANES // own_feats
     lane_bin = (iota((1, LANES), 1) // own_feats).astype(F32)
-    bins_per = LANES // own_feats
+    one, none = jnp.asarray(1, BF16), jnp.asarray(0, BF16)
+    member = (iota((8, half), 1) // classes == iota((8, half), 0)).astype(F32)
+    member = jnp.concatenate([member] * 3, axis=1).astype(BF16)
 
     @pl.loop(0, groups)
     def _(q):
@@ -200,50 +205,58 @@
         def _():
             acc[q] = jnp.zeros(acc.shape[1:], F32)
 
-        @pl.loop(0, chunks[1, q])
-        def _(i):
-            at = pl.multiple_of((first + i) * CHUNK, CHUNK)
-            columns = (near_grads[pl.ds(at, CHUNK), :] + grads[pl.ds(at, CHUNK), :]).T
-            node = columns[2 * classes : 2 * classes + classes, :]
-            parts = []
-            for side in range(2):
-                value = columns[side * classes : (side + 1) * classes, :]
-                for n in range(GROUP_NODES):
-                    wanted = (q * GROUP_NODES + n).astype(F32).astype(BF16)
-                    parts.append(jnp.where(node == wanted, value, jnp.zeros_like(value)))
-            weights = jnp.concatenate(parts, axis=0)
-            value = (bins[pl.ds(at, CHUNK), :].astype(F32) - lane_bin).astype(BF16)
+        def add_rows(at, rows):
+            at = pl.multiple_of(at * CHUNK, CHUNK)
+            fresh = at == first * CHUNK
+            columns = near_grads[pl.ds(at, rows), :] + grads[pl.ds(at, rows), :]
+            value = (bins[pl.ds(at, rows), :].astype(F32) - lane_bin).astype(BF16).T
             for m in range(width // COLS):
                 below = []
                 for s in range(COLS // LANES):
                     limit = (m * (COLS // LANES) + s) * bins_per
-                    below.append(
-                        jnp.where(value <= jnp.asarray(limit, BF16), jnp.asarray(1, BF16), jnp.asarray(0, BF16))
-                    )
-                below = jnp.concatenate(below, axis=1)
+                    below.append(jnp.where(value <= jnp.asarray(limit, BF16), one, none))
+                below = jnp.concatenate(below, axis=0)
                 span = slice(m * COLS, (m + 1) * COLS)
-                so_far = jnp.where(i == 0, 0.0, acc[q, :, span])
-                acc[q, :, span] = so_far + jnp.dot(weights, below, preferred_element_type=F32)
-
-        whole = acc[q, :, width - 1 : width]
+                so_far = jnp.where(fresh, 0.0, acc[q, span, :])
+                acc[q, span, :] = so_far + jnp.dot(below, columns, preferred_element_type=F32)
+
+        length = chunks[1, q]
+        largest = PIECES[0] // CHUNK
+
+        @pl.loop(0, length // largest)
+        def _(i):
+            add_rows(first + i * largest, PIECES[0])
+
+        for rows in PIECES[1:]:
+            units = rows // CHUNK
+
+            @pl.when((length // units) % 2 == 1)
+            def _():
+                add_rows(first + length // (2 * units) * (2 * units), rows)
+
+        whole = acc[q, width - 1 : width, :]
         totals[q] = whole
-        grad_whole = whole[:half]
-        hess_whole = whole[half:]
+        grad_whole = whole[:, :half]
+        hess_whole = whole[:, half:]
         parent_score = grad_whole * grad_whole / (hess_whole + hess_ridge)
         for m in range(width // LANES):
             span = slice(m * LANES, (m + 1) * LANES)
-            grad_left = acc[q, :half, span]
-            hess_left = acc[q, half:, span]
+            grad_left = acc[q, span, :half]
+            hess_left = acc[q, span, half:]
             grad_right = grad_whole - grad_left
             hess_right = hess_whole - hess_left
-            score = (
+            rest = (
                 grad_left * grad_left / (hess_left + hess_ridge)
                 + grad_right * grad_right / (hess_right + hess_ridge)
                 - parent_score
             )
-            for n in range(GROUP_NODES):
-                total = jnp.sum(score[n * classes : (n + 1) * classes], axis=0, keepdims=True)
-                gains[q, n : n + 1, span] = total * (1.0 / classes)
+            parts = []
+            for _ in range(3):
+                parts.append(rest.astype(BF16))
+                rest = rest - parts[-1].astype(F32)
+            parts = jnp.concatenate(parts, axis=1)
+            total = lax.dot_general(member, parts, NT, preferred_element_type=F32)
+            gains[q, :, span] = total[:GROUP_NODES] * (1.0 / classes)
 
 
 def flip_by(value, index, count):
@@ -336,14 +349,17 @@
         name="sort_bins",
     )(where, *bins_by, slots)
 
+    columns = 2 * GROUP_NODES * classes
+    level_bytes = ordered_rows * 2 * (2 * columns + LANES) + groups * width * columns * 4 + VMEM_MORE
+    near_bytes = ordered_rows * 2 * columns + VMEM_MORE
     shape = (nr, nf, ny, lo, hi, own, own_feats, classes, nodes, tiles)
     leaf_t = leaf_values.T
     near_grads = pl.pallas_call(
         functools.partial(near_kernel, shape),
-        out_shape=jax.ShapeDtypeStruct((ordered_rows, LANES), BF16),
+        out_shape=jax.ShapeDtypeStruct((ordered_rows, columns), BF16),
         in_specs=[SMEM] + [VMEM] * 4,
         out_specs=VMEM,
-        compiler_params=pltpu.CompilerParams(vmem_limit_bytes=VMEM_SMALL),
+        compiler_params=pltpu.CompilerParams(vmem_limit_bytes=near_bytes),
         name="near",
     )(where, near, all_parents, slots, leaf_t)
 
@@ -351,15 +367,15 @@
         functools.partial(level_kernel, shape),
         out_shape=(
             jax.ShapeDtypeStruct((groups, GROUP_NODES, width), F32),
-            jax.ShapeDtypeStruct((groups, 2 * GROUP_NODES * classes, 1), F32),
+            jax.ShapeDtypeStruct((groups, 1, columns), F32),
         ),
         in_specs=[SMEM] * 2 + [VMEM] * 6,
         out_specs=(VMEM, VMEM),
         scratch_shapes=[
-            pltpu.VMEM((ordered_rows, LANES), BF16),
-            pltpu.VMEM((groups, 2 * GROUP_NODES * classes, width), F32),
+            pltpu.VMEM((ordered_rows, columns), BF16),
+            pltpu.VMEM((groups, width, columns), F32),
         ],
-        compiler_params=pltpu.CompilerParams(vmem_limit_bytes=VMEM_LARGE),
+        compiler_params=pltpu.CompilerParams(vmem_limit_bytes=level_bytes),
         name="level",
     )(where, chunks, near_grads, far, all_parents, slots, ordered_bins, leaf_t)
 

time: 85.6 us -> 82.1 us (0.959)
  Pallas kernels: 41.9 us -> 38.4 us
  waiting for transfers between devices: 22.9 us -> 23.8 us
    pallas_call x1, Pallas kernels: 29.2 us -> 25.3 us  [body(): pl.pallas_call(functools.partial(level_kernel, shape), out_shape=(jax.Sha...]
    ppermute x13, waiting for transfers between devices: 22.9 us -> 23.8 us  [swap(): return lax.ppermute(value, axes, [(i, i ^ flat) for i in range(total)])]
    unnamed x8 -> x10, local copies, waits for them, and re-layouts: 3.35 us -> 2.66 us
  transfers between devices with their start and end apart: 13 -> 13, of which waited for: 9 -> 9; matrix products, arithmetic and copies ran while one was open for 4% -> 3% of each run, Pallas kernels for 12% -> 13%
where the time goes in v3:
time: 82.1 us; the launch traced here: 81.7 us
  Pallas kernels  38.4 us (47%)
  waiting for transfers between devices  23.8 us (29%)
  starting transfers between devices  13.3 us (16%)
  local copies, waits for them, and re-layouts  4.52 us (6%)
  other arithmetic  0.97 us (1%)
    pallas_call x1, Pallas kernels, body(): pl.pallas_call(functools.partial(level_kernel, shape), out_shape=(jax.Sha...  25.3 us
    ppermute x13, waiting for transfers between devices, swap(): return lax.ppermute(value, axes, [(i, i ^ flat) for i in range(total)])  23.8 us
    ppermute x13, starting transfers between devices, swap(): return lax.ppermute(value, axes, [(i, i ^ flat) for i in range(total)])  13.3 us
    pallas_call x1, Pallas kernels, body(): pl.pallas_call(functools.partial(near_kernel, shape), out_shape=jax.Shape...  5.54 us
    pallas_call x1, Pallas kernels, body(): pl.pallas_call(functools.partial(sort_bins_kernel, nr, nf, tiles, 8), out...  4.64 us
    unnamed x10, local copies, waits for them, and re-layouts  2.66 us
    pallas_call x1, Pallas kernels, body(): pl.pallas_call(functools.partial(first_kernel, nr, nf), out_shape=[jax.Sh...  2.48 us
  transfers between devices with their start and end apart: 13, of which 9 were waited for; matrix products, arithmetic and copies ran while one was open for 3% of the time, Pallas kernels for 13%

profile of v3, /device:TPU:0, one launch (start us, length us, event | category | flops | bytes accessed | tf_op | source)
XLA Modules:
  0.0 81.7 jit_solution(7188076686393580030)
XLA Ops:
  0.6 0.0 copy-start.1
  0.6 2.5 %first.1 = (f32[40,384]{1,0:T(8,128)}, bf16[264,384]{1,0:T(8,128)(2,1)}, bf16[264,384]{1,0:T(8,128)(2,1)}, bf16[264,384]{1,0:T(8,128)(2,1)}, bf16[264,384]{1,0:T(8,128)(2,1)}) custom-call(s32[8]{0:T(128)} %refs_0_.1, s32[8]{0:T(128)} %refs_1_.1, f32[32,384]{1,0:T(8,128)} %bitcast.38, s32[384]{0:T(512)} %refs_3_.1, s32[128,3072]{1,0:T(8,128)} %refs_4_.1, ...), custom_call_target="tpu_custom_call" | custom-call | tf_op jit(solution)/shard_map/first/pallas_call | solution.py:299
  3.1 3.1 %collective-permute-start.3 = (f32[40,384]{1,0:T(8,128)}, f32[40,384]{1,0:T(8,128)S(1)}, u32[]{:S(2)}, u32[]{:S(2)}) collective-permute-start(f32[40,384]{1,0:T(8,128)} %get-tuple-element.18), channel_id=1, source_target_pairs={{0,2},{1,3},{2,0},{3,1},{4,6},{5,7},{6,4},{7,5},{8,10},{9,11},{10,... | collective-permute-start | bytes 184328 | tf_op jit(solution)/shard_map/ppermute | solution.py:279
  6.3 2.6 %collective-permute-start.4 = (f32[40,384]{1,0:T(8,128)}, f32[40,384]{1,0:T(8,128)S(1)}, u32[]{:S(2)}, u32[]{:S(2)}) collective-permute-start(f32[40,384]{1,0:T(8,128)} %get-tuple-element.18), channel_id=1, source_target_pairs={{0,4},{1,5},{2,6},{3,7},{4,0},{5,1},{6,2},{7,3},{8,12},{9,13},{10,... | collective-permute-start | bytes 184328 | tf_op jit(solution)/shard_map/ppermute | solution.py:279
  8.8 0.0 collective-permute-start.5
  8.8 0.9 %slice_dynamic-update-slice_fusion.3 = f32[136,384]{1,0:T(8,128)S(1)} fusion(f32[40,384]{1,0:T(8,128)} %get-tuple-element.18), kind=kLoop, calls=%fused_computation.11 | loop fusion | bytes 98304
  9.7 0.0 collective-permute-done.3
  9.7 3.1 %collective-permute-done.4 = f32[40,384]{1,0:T(8,128)S(1)} collective-permute-done((f32[40,384]{1,0:T(8,128)}, f32[40,384]{1,0:T(8,128)S(1)}, u32[]{:S(2)}, u32[]{:S(2)}) %collective-permute-start.4) | collective-permute-done | bytes 61472 | tf_op jit(solution)/shard_map/ppermute | solution.py:279
  12.8 2.2 %collective-permute-done.5 = f32[40,384]{1,0:T(8,128)S(1)} collective-permute-done((f32[40,384]{1,0:T(8,128)}, f32[40,384]{1,0:T(8,128)S(1)}, u32[]{:S(2)}, u32[]{:S(2)}) %collective-permute-start.5) | collective-permute-done | bytes 61472 | tf_op jit(solution)/shard_map/ppermute | solution.py:279
  15.1 0.7 fusion.2
  15.8 2.4 %collective-permute-start.8 = (f32[136,384]{1,0:T(8,128)S(1)}, f32[136,384]{1,0:T(8,128)S(1)}, u32[]{:S(2)}, u32[]{:S(2)}) collective-permute-start(f32[136,384]{1,0:T(8,128)S(1)} %fusion.2), channel_id=1, source_target_pairs={{0,17},{1,16},{2,19},{3,18},{4,21},{5,20},{6,23},{7,22},{8,25},{9,... | collective-permute-start | bytes 626696 | tf_op jit(solution)/shard_map/ppermute | solution.py:279
  18.2 0.5 collective-permute-start.7
  18.7 0.5 collective-permute-start.6
  19.3 5.2 %collective-permute-done.8 = f32[136,384]{1,0:T(8,128)S(1)} collective-permute-done((f32[136,384]{1,0:T(8,128)S(1)}, f32[136,384]{1,0:T(8,128)S(1)}, u32[]{:S(2)}, u32[]{:S(2)}) %collective-permute-start.8) | collective-permute-done | bytes 208928 | tf_op jit(solution)/shard_map/ppermute | solution.py:279
  24.4 2.0 %collective-permute-done.7 = f32[136,384]{1,0:T(8,128)S(1)} collective-permute-done((f32[136,384]{1,0:T(8,128)S(1)}, f32[136,384]{1,0:T(8,128)S(1)}, u32[]{:S(2)}, u32[]{:S(2)}) %collective-permute-start.7) | collective-permute-done | bytes 208928 | tf_op jit(solution)/shard_map/ppermute | solution.py:279
  26.5 0.1 collective-permute-done.6
  26.6 0.1 pad_maximum_fusion.near
  26.6 0.1 collective-permute-start.9
  26.7 1.5 %collective-permute-start.2 = (bf16[264,384]{1,0:T(8,128)(2,1)}, bf16[264,384]{1,0:T(8,128)(2,1)S(1)}, u32[]{:S(2)}, u32[]{:S(2)}) collective-permute-start(bf16[264,384]{1,0:T(8,128)(2,1)} %get-tuple-element.15), channel_id=1, source_target_pairs={{0,24},{1,25},{2,26},{3,27},{4,28},{5,29},{6,30},{7,31},{8,16},{9,... | collective-permute-start | bytes 608264 | tf_op jit(solution)/shard_map/ppermute | solution.py:279
  28.2 0.6 collective-permute-start.1
  28.8 0.0 collective-permute-start
  28.8 0.7 slice.48
  29.5 0.0 copy-done.1
  29.5 0.1 copy.12
  29.6 4.4 %collective-permute-done.2.refs_3_ = bf16[264,384]{1,0:T(8,128)(2,1)S(1)} collective-permute-done((bf16[264,384]{1,0:T(8,128)(2,1)}, bf16[264,384]{1,0:T(8,128)(2,1)S(1)}, u32[]{:S(2)}, u32[]{:S(2)}) %collective-permute-start.2) | collective-permute-done | bytes 202784 | tf_op jit(solution)/shard_map/ppermute | solution.py:279
  34.0 4.7 %collective-permute-done.1.refs_2_ = bf16[264,384]{1,0:T(8,128)(2,1)S(1)} collective-permute-done((bf16[264,384]{1,0:T(8,128)(2,1)}, bf16[264,384]{1,0:T(8,128)(2,1)S(1)}, u32[]{:S(2)}, u32[]{:S(2)}) %collective-permute-start.1) | collective-permute-done | bytes 202784 | tf_op jit(solution)/shard_map/ppermute | solution.py:279
  38.7 0.0 collective-permute-done.refs_1_
  38.7 0.4 plan.1
  39.1 0.0 copy-start
  39.1 0.9 %copy-done = bf16[264,384]{1,0:T(8,128)(2,1)S(1)} copy-done((bf16[264,384]{1,0:T(8,128)(2,1)S(1)}, bf16[264,384]{1,0:T(8,128)(2,1)}, u32[]{:S(2)}) %copy-start) | copy-done | bytes 202776
  40.0 4.6 %sort_bins.1.bins = bf16[14800,128]{1,0:T(8,128)(2,1)S(1)} custom-call(s32[32,128]{1,0:T(8,128)S(1)} %get-tuple-element.16.where, bf16[264,384]{1,0:T(8,128)(2,1)S(1)} %copy-done, bf16[264,384]{1,0:T(8,128)(2,1)S(1)} %collective-permute-done.refs_1_, bf16[264,384]{1,0:T(8,128)(2,1)S(1)} %collective-permute-done.1.refs_2_, ...), custom_call_target="tpu_custom_call" | custom-call | tf_op jit(solution)/shard_map/sort_bins/pallas_call | solution.py:343
  44.7 5.5 %near.1.near_grads = bf16[14800,256]{1,0:T(8,128)(2,1)S(1)} custom-call(s32[32,128]{1,0:T(8,128)S(1)} %get-tuple-element.16.where, f32[4,136,384]{2,1,0:T(8,128)S(1)} %pad_maximum_fusion.near, f32[32,384]{1,0:T(8,128)S(1)} %maximum_convert_fusion.parents, f32[32,384]{1,0:T(8,128)S(1)} %get-tuple-element.19.slots.refs_4_, f32[32,16]{1,0:T(8,128)S(1)} %bitcast.26), custom_call_target="tpu_custom_call" | custom-call | tf_op jit(solution)/shard_map/near/pallas_call | solution.py:357
  50.2 0.0 collective-permute-done.9.far
  50.2 25.3 %level.1 = (f32[4,4,2048]{2,1,0:T(4,128)S(1)}, f32[4,1,256]{2,1,0:T(1,128)S(1)}) custom-call(s32[32,128]{1,0:T(8,128)S(1)} %get-tuple-element.16.where, s32[8,128]{1,0:T(8,128)S(1)} %get-tuple-element.17.chunks, bf16[14800,256]{1,0:T(8,128)(2,1)S(1)} %near.1.near_grads, f32[4,136,384]{2,1,0:T(8,128)S(1)} %collective-permute-done.9.far, ...), custom_call_target="tpu_custom_call" | custom-call | tf_op jit(solution)/shard_map/level/pallas_call | solution.py:366
  75.6 0.1 fusion
  75.7 0.6 collective-permute-start.12
  76.3 1.0 %collective-permute-start.11 = (f32[4,2048]{1,0:T(4,128)S(1)}, f32[4,2048]{1,0:T(4,128)S(1)}, u32[]{:S(2)}, u32[]{:S(2)}) collective-permute-start(f32[4,2048]{1,0:T(4,128)S(1)} %get-tuple-element.26), channel_id=1, source_target_pairs={{0,16},{1,17},{2,18},{3,19},{4,20},{5,21},{6,22},{7,23},{8,24},{9,... | collective-permute-start | bytes 98312 | tf_op jit(solution)/shard_map/ppermute | solution.py:279
  77.3 0.3 collective-permute-start.10
  77.6 0.1 reshape.30
  77.7 0.7 reshape.31
  78.4 1.0 %collective-permute-done.12 = f32[4,2048]{1,0:T(4,128)S(1)} collective-permute-done((f32[4,2048]{1,0:T(4,128)S(1)}, f32[4,2048]{1,0:T(4,128)S(1)}, u32[]{:S(2)}, u32[]{:S(2)}) %collective-permute-start.12) | collective-permute-done | bytes 32800 | tf_op jit(solution)/shard_map/ppermute | solution.py:279
  79.4 1.1 %collective-permute-done.11 = f32[4,2048]{1,0:T(4,128)S(1)} collective-permute-done((f32[4,2048]{1,0:T(4,128)S(1)}, f32[4,2048]{1,0:T(4,128)S(1)}, u32[]{:S(2)}, u32[]{:S(2)}) %collective-permute-start.11) | collective-permute-done | bytes 32800 | tf_op jit(solution)/shard_map/ppermute | solution.py:279
  80.5 0.0 collective-permute-done.10
  80.6 0.2 reshape_reshape.11
  80.8 0.2 copy.13
  81.0 0.8 copy.15
  (14 shorter events, 0.2 us)
Async XLA Ops:
  0.6 28.9 %copy-start.1 = (f32[16,32]{1,0:T(8,128)S(1)}, f32[16,32]{1,0:T(8,128)}, u32[]{:S(2)}) copy-start(f32[16,32]{1,0:T(8,128)} %param.13) | copy-start | bytes 6148
  3.1 6.6 %collective-permute-start.3 = (f32[40,384]{1,0:T(8,128)}, f32[40,384]{1,0:T(8,128)S(1)}, u32[]{:S(2)}, u32[]{:S(2)}) collective-permute-start(f32[40,384]{1,0:T(8,128)} %get-tuple-element.18), channel_id=1, source_target_pairs={{0,2},{1,3},{2,0},{3,1},{4,6},{5,7},{6,4},{7,5},{8,10},{9,11},{10,... | collective-permute-start | bytes 184328 | tf_op jit(solution)/shard_map/ppermute | solution.py:279
  6.3 6.6 %collective-permute-start.4 = (f32[40,384]{1,0:T(8,128)}, f32[40,384]{1,0:T(8,128)S(1)}, u32[]{:S(2)}, u32[]{:S(2)}) collective-permute-start(f32[40,384]{1,0:T(8,128)} %get-tuple-element.18), channel_id=1, source_target_pairs={{0,4},{1,5},{2,6},{3,7},{4,0},{5,1},{6,2},{7,3},{8,12},{9,13},{10,... | collective-permute-start | bytes 184328 | tf_op jit(solution)/shard_map/ppermute | solution.py:279
  8.8 6.2 %collective-permute-start.5 = (f32[40,384]{1,0:T(8,128)}, f32[40,384]{1,0:T(8,128)S(1)}, u32[]{:S(2)}, u32[]{:S(2)}) collective-permute-start(f32[40,384]{1,0:T(8,128)} %get-tuple-element.18), channel_id=1, source_target_pairs={{0,6},{1,7},{2,4},{3,5},{4,2},{5,3},{6,0},{7,1},{8,14},{9,15},{10,... | collective-permute-start | bytes 184328 | tf_op jit(solution)/shard_map/ppermute | solution.py:279
  15.8 8.6 %collective-permute-start.8 = (f32[136,384]{1,0:T(8,128)S(1)}, f32[136,384]{1,0:T(8,128)S(1)}, u32[]{:S(2)}, u32[]{:S(2)}) collective-permute-start(f32[136,384]{1,0:T(8,128)S(1)} %fusion.2), channel_id=1, source_target_pairs={{0,17},{1,16},{2,19},{3,18},{4,21},{5,20},{6,23},{7,22},{8,25},{9,... | collective-permute-start | bytes 626696 | tf_op jit(solution)/shard_map/ppermute | solution.py:279
  18.2 8.2 %collective-permute-start.7 = (f32[136,384]{1,0:T(8,128)S(1)}, f32[136,384]{1,0:T(8,128)S(1)}, u32[]{:S(2)}, u32[]{:S(2)}) collective-permute-start(f32[136,384]{1,0:T(8,128)S(1)} %fusion.2), channel_id=1, source_target_pairs={{0,16},{1,17},{2,18},{3,19},{4,20},{5,21},{6,22},{7,23},{8,24},{9,... | collective-permute-start | bytes 626696 | tf_op jit(solution)/shard_map/ppermute | solution.py:279
  18.7 7.8 %collective-permute-start.6 = (f32[136,384]{1,0:T(8,128)S(1)}, f32[136,384]{1,0:T(8,128)S(1)}, u32[]{:S(2)}, u32[]{:S(2)}) collective-permute-start(f32[136,384]{1,0:T(8,128)S(1)} %fusion.2), channel_id=1, source_target_pairs={{0,1},{1,0},{2,3},{3,2},{4,5},{5,4},{6,7},{7,6},{8,9},{9,8},{10,11... | collective-permute-start | bytes 626696 | tf_op jit(solution)/shard_map/ppermute | solution.py:279
  26.6 23.6 %collective-permute-start.9 = (f32[4,136,384]{2,1,0:T(8,128)S(1)}, f32[4,136,384]{2,1,0:T(8,128)S(1)}, u32[]{:S(2)}, u32[]{:S(2)}) collective-permute-start(f32[4,136,384]{2,1,0:T(8,128)S(1)} %pad_maximum_fusion.near), channel_id=1, source_target_pairs={{0,8},{1,9},{2,10},{3,11},{4,12},{5,13},{6,14},{7,15},{8,0},{9,1},... | collective-permute-start | bytes 2506760 | tf_op jit(solution)/shard_map/ppermute | solution.py:279
  26.7 7.3 %collective-permute-start.2 = (bf16[264,384]{1,0:T(8,128)(2,1)}, bf16[264,384]{1,0:T(8,128)(2,1)S(1)}, u32[]{:S(2)}, u32[]{:S(2)}) collective-permute-start(bf16[264,384]{1,0:T(8,128)(2,1)} %get-tuple-element.15), channel_id=1, source_target_pairs={{0,24},{1,25},{2,26},{3,27},{4,28},{5,29},{6,30},{7,31},{8,16},{9,... | collective-permute-start | bytes 608264 | tf_op jit(solution)/shard_map/ppermute | solution.py:279
  28.2 10.4 %collective-permute-start.1 = (bf16[264,384]{1,0:T(8,128)(2,1)}, bf16[264,384]{1,0:T(8,128)(2,1)S(1)}, u32[]{:S(2)}, u32[]{:S(2)}) collective-permute-start(bf16[264,384]{1,0:T(8,128)(2,1)} %get-tuple-element.14), channel_id=1, source_target_pairs={{0,16},{1,17},{2,18},{3,19},{4,20},{5,21},{6,22},{7,23},{8,24},{9,... | collective-permute-start | bytes 608264 | tf_op jit(solution)/shard_map/ppermute | solution.py:279
  28.8 9.8 %collective-permute-start = (bf16[264,384]{1,0:T(8,128)(2,1)}, bf16[264,384]{1,0:T(8,128)(2,1)S(1)}, u32[]{:S(2)}, u32[]{:S(2)}) collective-permute-start(bf16[264,384]{1,0:T(8,128)(2,1)} %get-tuple-element.13), channel_id=1, source_target_pairs={{0,8},{1,9},{2,10},{3,11},{4,12},{5,13},{6,14},{7,15},{8,0},{9,1},... | collective-permute-start | bytes 608264 | tf_op jit(solution)/shard_map/ppermute | solution.py:279
  39.1 0.9 %copy-start = (bf16[264,384]{1,0:T(8,128)(2,1)S(1)}, bf16[264,384]{1,0:T(8,128)(2,1)}, u32[]{:S(2)}) copy-start(bf16[264,384]{1,0:T(8,128)(2,1)} %get-tuple-element.12.refs_0_) | copy-start | bytes 608260
  75.7 3.7 %collective-permute-start.12 = (f32[4,2048]{1,0:T(4,128)S(1)}, f32[4,2048]{1,0:T(4,128)S(1)}, u32[]{:S(2)}, u32[]{:S(2)}) collective-permute-start(f32[4,2048]{1,0:T(4,128)S(1)} %get-tuple-element.25), channel_id=1, source_target_pairs={{0,24},{1,25},{2,26},{3,27},{4,28},{5,29},{6,30},{7,31},{8,16},{9,... | collective-permute-start | bytes 98312 | tf_op jit(solution)/shard_map/ppermute | solution.py:279
  76.3 4.2 %collective-permute-start.11 = (f32[4,2048]{1,0:T(4,128)S(1)}, f32[4,2048]{1,0:T(4,128)S(1)}, u32[]{:S(2)}, u32[]{:S(2)}) collective-permute-start(f32[4,2048]{1,0:T(4,128)S(1)} %get-tuple-element.26), channel_id=1, source_target_pairs={{0,16},{1,17},{2,18},{3,19},{4,20},{5,21},{6,22},{7,23},{8,24},{9,... | collective-permute-start | bytes 98312 | tf_op jit(solution)/shard_map/ppermute | solution.py:279
  77.3 3.2 %collective-permute-start.10 = (f32[4,2048]{1,0:T(4,128)S(1)}, f32[4,2048]{1,0:T(4,128)S(1)}, u32[]{:S(2)}, u32[]{:S(2)}) collective-permute-start(f32[4,2048]{1,0:T(4,128)S(1)} %get-tuple-element.27), channel_id=1, source_target_pairs={{0,8},{1,9},{2,10},{3,11},{4,12},{5,13},{6,14},{7,15},{8,0},{9,1},... | collective-permute-start | bytes 98312 | tf_op jit(solution)/shard_map/ppermute | solution.py:279

commit v4 on v3

--- a/solution.py
+++ b/solution.py
@@ -13,6 +13,7 @@
 TILE = 16
 GROUP_NODES = 4
 CHUNK = 256
+SUB = 256
 PIECES = (2048, 1024, 512, 256)
 COLS = 256
 VMEM_SMALL = 12 * 2**20
@@ -34,12 +35,29 @@
     return lax.broadcasted_iota(I32, shape, dim)
 
 
+def put_bins(bins, parents, cuts, out):
+    own_feats = bins.shape[0]
+    for k, cut in enumerate(cuts):
+        out[k * own_feats : (k + 1) * own_feats, :] = bins[:, cut].astype(F32).astype(BF16)
+    out[len(cuts) * own_feats :, :] = jnp.concatenate([parents[:, cut] for cut in cuts], axis=0).astype(F32).astype(BF16)
+
+
+def own_kernel(nf, bins, parents, out, held, sem):
+    own_feats = held.shape[0]
+    own = held.shape[1] // nf
+    at = pl.multiple_of(lax.axis_index("rows") * own_feats, own_feats)
+    copy = pltpu.make_async_copy(bins.at[pl.ds(at, own_feats), :], held, sem)
+    copy.start()
+    copy.wait()
+    put_bins(held[...], parents[...], [slice(k * own, (k + 1) * own) for k in range(nf)], out)
+
+
 def first_kernel(nr, nf, *refs):
     sources = refs[:6]
     out = refs[6]
-    sent = refs[7 : 7 + nr]
-    held = refs[7 + nr : 13 + nr]
-    sems = refs[13 + nr]
+    sent = refs[7 : 6 + nr]
+    held = refs[6 + nr : 12 + nr]
+    sems = refs[12 + nr]
     copies = [pltpu.make_async_copy(source, here, sems.at[i]) for i, (source, here) in enumerate(zip(sources, held))]
     for copy in copies:
         copy.start()
@@ -54,13 +72,9 @@
         copy.wait()
     par = parents[...]
     cuts = [slice(k * own, (k + 1) * own) for k in range(nf)]
-    par_rows = jnp.concatenate([par[:, cut] for cut in cuts], axis=0).astype(F32).astype(BF16)
-    for j in range(nr):
-        first = pl.multiple_of(jnp.bitwise_xor(row, j) * own_feats, own_feats)
-        for k, cut in enumerate(cuts):
-            piece = bins[pl.ds(first, own_feats), cut]
-            sent[j][k * own_feats : (k + 1) * own_feats, :] = piece.astype(F32).astype(BF16)
-        sent[j][nf * own_feats :, :] = par_rows
+    for j in range(1, nr):
+        at = pl.multiple_of(jnp.bitwise_xor(row, j) * own_feats, own_feats)
+        put_bins(bins[pl.ds(at, own_feats), :], par, cuts, sent[j - 1])
     out[0:classes, :] = margins[...]
     right = jnp.zeros(par.shape, F32)
     for p in range(split_feature.shape[0]):
@@ -74,9 +88,21 @@
     out[classes:, :] = jnp.concatenate([right[:, cut] for cut in cuts], axis=0) + jnp.where(mine, label, 0.0)
 
 
-def plan_kernel(groups, parents_per_group, spare, parents, slots, where, chunks):
+def cut_pair(pair, sub):
+    joined = jnp.concatenate(pair, axis=1)
+    return [joined[:, at : at + sub] for at in range(0, joined.shape[1], sub)]
+
+
+def plan_kernel(groups, parents_per_group, spare, nr, nf, lo, sub, given, slots, where, chunks):
+    feat = lax.axis_index("feat")
+    parents = []
+    for j in range(nr):
+        for far in range(0, nf, lo):
+            pair = [given[pl.ds(j * nf + jnp.bitwise_xor(feat, far + x), 1), :] for x in range(lo)]
+            parents += cut_pair(pair, sub)
+    parents = jnp.concatenate(parents, axis=0)
     blocks, own = parents.shape
-    group = parents[...].astype(I32) // parents_per_group
+    group = parents.astype(I32) // parents_per_group
     hot = [(group == q).astype(F32) for q in range(groups)]
     earlier = (iota((own, own), 0) < iota((own, own), 1)).astype(F32).astype(BF16)
     ahead = jnp.dot(jnp.concatenate(hot, axis=0).astype(BF16), earlier, preferred_element_type=F32)
@@ -124,25 +150,31 @@
         out[pl.ds(to, TILE), :] = placed[t * TILE : (t + 1) * TILE]
 
 
-def sort_bins_kernel(nr, nf, tiles, unroll, where, *refs):
+def sort_bins_kernel(nr, nf, lo, sub, tiles, unroll, where, *refs):
     bins = refs[:nr]
     slots, out = refs[nr:]
     own_feats = (bins[0].shape[0] - nf) // nf
     copies = LANES // own_feats
+    cuts = slots.shape[0] * lo // (nr * nf)
+    feat = lax.axis_index("feat")
     for j in range(nr):
 
-        @pl.loop(0, nf // unroll)
+        @pl.loop(0, nf // (lo * unroll))
         def _(i):
             for u in range(unroll):
-                k = i * unroll + u
-                block = j * nf + k
-                values = bins[j][pl.ds(pl.multiple_of(k * own_feats, own_feats), own_feats), :]
-                values = jnp.concatenate([values] * copies, axis=0)
-                put_block(values, slots[pl.ds(block, 1), :], tiles, where, block, out)
+                jz = i * unroll + u
+                pair = []
+                for jx in range(lo):
+                    k = jnp.bitwise_xor(feat, jz * lo + jx)
+                    pair.append(bins[j][pl.ds(pl.multiple_of(k * own_feats, own_feats), own_feats), :])
+                for c, values in enumerate(cut_pair(pair, sub)):
+                    part = (j * (nf // lo) + jz) * cuts + c
+                    values = jnp.concatenate([values] * copies, axis=0)
+                    put_block(values, slots[pl.ds(part, 1), :], tiles, where, part, out)
 
 
 def put_grads(sizes, jc, where, source, parents, slots, leaf, grads):
-    _, nf, ny, lo, hi, own, _, classes, nodes, tiles = sizes
+    _, nf, ny, lo, hi, own, _, classes, nodes, tiles, sub = sizes
     me_feat = lax.axis_index("feat")
     code_row = hi * classes
     rest = leaf[...]
@@ -156,7 +188,8 @@
     @pl.loop(0, ny)
     def _(jy):
         j = jy * 2 + jc
-        for jx, jz in [(jx, jz) for jx in range(lo) for jz in range(hi)]:
+        pair = []
+        for jz, jx in [(jz, jx) for jz in range(hi) for jx in range(lo)]:
             yx = jy * lo + jx
             k = jnp.bitwise_xor(me_feat, jz * lo + jx)
             block = j * nf + k
@@ -177,8 +210,14 @@
             hessian = 2.0 * prob * (1.0 - prob)
             member = node - GROUP_NODES * jnp.floor(node * (1.0 / GROUP_NODES))
             parts = [jnp.where(member == n, v, 0.0) for v in (gradient, hessian) for n in range(GROUP_NODES)]
-            columns = jnp.concatenate(parts, axis=0).astype(BF16)
-            put_block(columns, slots[pl.ds(block, 1), :], tiles, where, block, grads)
+            pair.append(jnp.concatenate(parts, axis=0).astype(BF16))
+            if jx < lo - 1:
+                continue
+            cuts = cut_pair(pair, sub)
+            pair = []
+            for c, columns in enumerate(cuts):
+                part = (j * hi + jz) * len(cuts) + c
+                put_block(columns, slots[pl.ds(part, 1), :], tiles, where, part, grads)
 
 
 def near_kernel(sizes, where, near, parents, slots, leaf, grads):
@@ -186,7 +225,7 @@
 
 
 def level_kernel(sizes, where, chunks, near_grads, far, parents, slots, bins, leaf, gains, totals, grads, acc):
-    _, _, _, _, _, _, own_feats, classes, nodes, _ = sizes
+    _, _, _, _, _, _, own_feats, classes, nodes, _, _ = sizes
     groups = nodes // GROUP_NODES
     half = GROUP_NODES * classes
     width = BINS * own_feats
@@ -299,9 +338,9 @@
     first, *sent = pl.pallas_call(
         functools.partial(first_kernel, nr, nf),
         out_shape=[jax.ShapeDtypeStruct((classes + nf, own), F32)]
-        + [jax.ShapeDtypeStruct((message_rows, own), BF16)] * nr,
+        + [jax.ShapeDtypeStruct((message_rows, own), BF16)] * (nr - 1),
         in_specs=[pl.BlockSpec(memory_space=pltpu.HBM)] * 6,
-        out_specs=[VMEM] * (nr + 1),
+        out_specs=[VMEM] * nr,
         scratch_shapes=[pltpu.SMEM(x.shape, x.dtype) for x in first_inputs[:2]]
         + [pltpu.VMEM(x.shape, x.dtype) for x in first_inputs[2:]]
         + [pltpu.SemaphoreType.DMA((6,))],
@@ -309,9 +348,18 @@
         name="first",
     )(*first_inputs)
 
-    bins_by = [sent[0]]
+    own_bins = pl.pallas_call(
+        functools.partial(own_kernel, nf),
+        out_shape=jax.ShapeDtypeStruct((message_rows, own), BF16),
+        in_specs=[pl.BlockSpec(memory_space=pltpu.HBM), VMEM],
+        out_specs=VMEM,
+        scratch_shapes=[pltpu.VMEM((own_feats, group_rows), I32), pltpu.SemaphoreType.DMA],
+        compiler_params=pltpu.CompilerParams(vmem_limit_bytes=VMEM_SMALL),
+        name="own_bins",
+    )(row_bins, parents.reshape(1, group_rows))
+    bins_by = [own_bins]
     for j in range(1, nr):
-        bins_by.append(swap(sent[j], axes, sizes, (j, 0)))
+        bins_by.append(swap(sent[j - 1], axes, sizes, (j, 0)))
     along_z = [first] + [swap(first, axes, sizes, (0, lo * j)) for j in range(1, hi)]
 
     all_parents = jnp.concatenate([b[nf * own_feats :] for b in bins_by]).astype(F32)
@@ -324,14 +372,16 @@
     near = jnp.stack(plane)
     far = swap(near, axes, sizes, (1, 0))
 
-    tiles = own // TILE + groups * (TILE - 1) // TILE
-    spare = blocks * tiles + groups * (CHUNK // TILE - 1)
+    sub = SUB if lo * own % SUB == 0 else own
+    parts = blocks * own // sub
+    tiles = sub // TILE + groups * (TILE - 1) // TILE
+    spare = parts * tiles + groups * (CHUNK // TILE - 1)
     ordered_rows = (spare + 1) * TILE
     slots, where, chunks = pl.pallas_call(
-        functools.partial(plan_kernel, groups, parent_count // groups, spare),
+        functools.partial(plan_kernel, groups, parent_count // groups, spare, nr, nf, lo, sub),
         out_shape=(
-            jax.ShapeDtypeStruct((blocks, own), F32),
-            jax.ShapeDtypeStruct((blocks, LANES), I32),
+            jax.ShapeDtypeStruct((parts, sub), F32),
+            jax.ShapeDtypeStruct((parts, LANES), I32),
             jax.ShapeDtypeStruct((8, LANES), I32),
         ),
         in_specs=[VMEM],
@@ -341,7 +391,7 @@
     )(all_parents)
 
     ordered_bins = pl.pallas_call(
-        functools.partial(sort_bins_kernel, nr, nf, tiles, 8),
+        functools.partial(sort_bins_kernel, nr, nf, lo, sub, tiles, 2),
         out_shape=jax.ShapeDtypeStruct((ordered_rows, LANES), BF16),
         in_specs=[SMEM] + [VMEM] * (nr + 1),
         out_specs=VMEM,
@@ -352,7 +402,7 @@
     columns = 2 * GROUP_NODES * classes
     level_bytes = ordered_rows * 2 * (2 * columns + LANES) + groups * width * columns * 4 + VMEM_MORE
     near_bytes = ordered_rows * 2 * columns + VMEM_MORE
-    shape = (nr, nf, ny, lo, hi, own, own_feats, classes, nodes, tiles)
+    shape = (nr, nf, ny, lo, hi, own, own_feats, classes, nodes, tiles, sub)
     leaf_t = leaf_values.T
     near_grads = pl.pallas_call(
         functools.partial(near_kernel, shape),

time: 82.1 us -> 80.5 us (0.981)
  local copies, waits for them, and re-layouts: 4.52 us -> 3.62 us
    pallas_call x1 -> x2, Pallas kernels: 4.64 us -> 4.92 us  [the longest x1 4.69 us: body(): pl.pallas_call(functools.partial(sort_bins_kernel, nr, nf, lo, sub, tiles...]
    unnamed x10 -> x12, local copies, waits for them, and re-layouts: 2.66 us -> 2.45 us
  transfers between devices with their start and end apart: 13 -> 13, of which waited for: 9 -> 9; matrix products, arithmetic and copies ran while one was open for 3% -> 2% of each run, Pallas kernels for 13% -> 13%
where the time goes in v4:
time: 80.5 us; the launch traced here: 80.2 us
  Pallas kernels  38 us (47%)
  waiting for transfers between devices  23.5 us (29%)
  starting transfers between devices  13.3 us (17%)
  local copies, waits for them, and re-layouts  3.62 us (4%)
  other arithmetic  0.97 us (1%)
  between operations  0.82 us (1%)
    pallas_call x1, Pallas kernels, body(): pl.pallas_call(functools.partial(level_kernel, shape), out_shape=(jax.Sha...  25.4 us
    ppermute x13, waiting for transfers between devices, swap(): return lax.ppermute(value, axes, [(i, i ^ flat) for i in range(total)])  23.5 us
    ppermute x13, starting transfers between devices, swap(): return lax.ppermute(value, axes, [(i, i ^ flat) for i in range(total)])  13.3 us
    pallas_call x1, Pallas kernels, body(): pl.pallas_call(functools.partial(near_kernel, shape), out_shape=jax.Shape...  4.75 us
    pallas_call x1, Pallas kernels, body(): pl.pallas_call(functools.partial(sort_bins_kernel, nr, nf, lo, sub, tiles...  4.69 us
    pallas_call x1, Pallas kernels, body(): pl.pallas_call(functools.partial(first_kernel, nr, nf), out_shape=[jax.Sh...  2.53 us
    unnamed x12, local copies, waits for them, and re-layouts  2.45 us
  transfers between devices with their start and end apart: 13, of which 9 were waited for; matrix products, arithmetic and copies ran while one was open for 2% of the time, Pallas kernels for 13%

profile of v4, /device:TPU:0, one launch (start us, length us, event | category | flops | bytes accessed | tf_op | source)
XLA Modules:
  0.0 80.2 jit_solution(5365305733289903239)
XLA Ops:
  0.6 0.0 copy-start
  0.6 0.0 copy-start.2
  0.7 2.5 %first.1 = (f32[40,384]{1,0:T(8,128)}, bf16[264,384]{1,0:T(8,128)(2,1)}, bf16[264,384]{1,0:T(8,128)(2,1)}, bf16[264,384]{1,0:T(8,128)(2,1)}) custom-call(s32[8]{0:T(128)} %refs_0_.1, s32[8]{0:T(128)} %refs_1_.1, f32[32,384]{1,0:T(8,128)} %bitcast.40, s32[384]{0:T(512)} %refs_3_.1, s32[128,3072]{1,0:T(8,128)} %refs_4_.1, s32[1,3072]{1,0:T(1,128)} %bitcast.29), custom_call_target="tpu_custom_call" | custom-call | tf_op jit(solution)/shard_map/first/pallas_call | solution.py:338
  3.2 3.1 %collective-permute-start.3 = (f32[40,384]{1,0:T(8,128)}, f32[40,384]{1,0:T(8,128)S(1)}, u32[]{:S(2)}, u32[]{:S(2)}) collective-permute-start(f32[40,384]{1,0:T(8,128)} %get-tuple-element.16), channel_id=1, source_target_pairs={{0,2},{1,3},{2,0},{3,1},{4,6},{5,7},{6,4},{7,5},{8,10},{9,11},{10,... | collective-permute-start | bytes 184328 | tf_op jit(solution)/shard_map/ppermute | solution.py:318
  6.3 2.6 %collective-permute-start.4 = (f32[40,384]{1,0:T(8,128)}, f32[40,384]{1,0:T(8,128)S(1)}, u32[]{:S(2)}, u32[]{:S(2)}) collective-permute-start(f32[40,384]{1,0:T(8,128)} %get-tuple-element.16), channel_id=1, source_target_pairs={{0,4},{1,5},{2,6},{3,7},{4,0},{5,1},{6,2},{7,3},{8,12},{9,13},{10,... | collective-permute-start | bytes 184328 | tf_op jit(solution)/shard_map/ppermute | solution.py:318
  8.9 0.0 collective-permute-start.5
  8.9 0.9 %slice_dynamic-update-slice_fusion.3 = f32[136,384]{1,0:T(8,128)S(1)} fusion(f32[40,384]{1,0:T(8,128)} %get-tuple-element.16), kind=kLoop, calls=%fused_computation.11 | loop fusion | bytes 98304
  9.8 0.0 collective-permute-done.3
  9.8 3.1 %collective-permute-done.4 = f32[40,384]{1,0:T(8,128)S(1)} collective-permute-done((f32[40,384]{1,0:T(8,128)}, f32[40,384]{1,0:T(8,128)S(1)}, u32[]{:S(2)}, u32[]{:S(2)}) %collective-permute-start.4) | collective-permute-done | bytes 61472 | tf_op jit(solution)/shard_map/ppermute | solution.py:318
  12.9 2.2 %collective-permute-done.5 = f32[40,384]{1,0:T(8,128)S(1)} collective-permute-done((f32[40,384]{1,0:T(8,128)}, f32[40,384]{1,0:T(8,128)S(1)}, u32[]{:S(2)}, u32[]{:S(2)}) %collective-permute-start.5) | collective-permute-done | bytes 61472 | tf_op jit(solution)/shard_map/ppermute | solution.py:318
  15.1 0.7 fusion.2
  15.8 2.4 %collective-permute-start.8 = (f32[136,384]{1,0:T(8,128)S(1)}, f32[136,384]{1,0:T(8,128)S(1)}, u32[]{:S(2)}, u32[]{:S(2)}) collective-permute-start(f32[136,384]{1,0:T(8,128)S(1)} %fusion.2), channel_id=1, source_target_pairs={{0,17},{1,16},{2,19},{3,18},{4,21},{5,20},{6,23},{7,22},{8,25},{9,... | collective-permute-start | bytes 626696 | tf_op jit(solution)/shard_map/ppermute | solution.py:318
  18.3 0.5 collective-permute-start.7
  18.8 0.5 collective-permute-start.6
  19.3 5.2 %collective-permute-done.8 = f32[136,384]{1,0:T(8,128)S(1)} collective-permute-done((f32[136,384]{1,0:T(8,128)S(1)}, f32[136,384]{1,0:T(8,128)S(1)}, u32[]{:S(2)}, u32[]{:S(2)}) %collective-permute-start.8) | collective-permute-done | bytes 208928 | tf_op jit(solution)/shard_map/ppermute | solution.py:318
  24.5 2.0 %collective-permute-done.7 = f32[136,384]{1,0:T(8,128)S(1)} collective-permute-done((f32[136,384]{1,0:T(8,128)S(1)}, f32[136,384]{1,0:T(8,128)S(1)}, u32[]{:S(2)}, u32[]{:S(2)}) %collective-permute-start.7) | collective-permute-done | bytes 208928 | tf_op jit(solution)/shard_map/ppermute | solution.py:318
  26.5 0.1 collective-permute-done.6
  26.6 0.1 pad_maximum_fusion.near
  26.7 0.1 collective-permute-start.9
  26.8 1.5 %collective-permute-start.2 = (bf16[264,384]{1,0:T(8,128)(2,1)}, bf16[264,384]{1,0:T(8,128)(2,1)S(1)}, u32[]{:S(2)}, u32[]{:S(2)}) collective-permute-start(bf16[264,384]{1,0:T(8,128)(2,1)} %get-tuple-element.13), channel_id=1, source_target_pairs={{0,24},{1,25},{2,26},{3,27},{4,28},{5,29},{6,30},{7,31},{8,16},{9,... | collective-permute-start | bytes 608264 | tf_op jit(solution)/shard_map/ppermute | solution.py:318
  28.3 0.6 collective-permute-start.1
  28.9 0.0 collective-permute-start
  28.9 0.0 copy-done
  28.9 0.0 copy-start.1
  28.9 0.7 copy-done.1
  29.6 0.2 own_bins.1.refs_0_
  29.9 0.0 copy-done.2
  29.9 0.1 copy.12
  30.0 4.1 %collective-permute-done.2.refs_3_ = bf16[264,384]{1,0:T(8,128)(2,1)S(1)} collective-permute-done((bf16[264,384]{1,0:T(8,128)(2,1)}, bf16[264,384]{1,0:T(8,128)(2,1)S(1)}, u32[]{:S(2)}, u32[]{:S(2)}) %collective-permute-start.2) | collective-permute-done | bytes 202784 | tf_op jit(solution)/shard_map/ppermute | solution.py:318
  34.0 4.7 %collective-permute-done.1.refs_2_ = bf16[264,384]{1,0:T(8,128)(2,1)S(1)} collective-permute-done((bf16[264,384]{1,0:T(8,128)(2,1)}, bf16[264,384]{1,0:T(8,128)(2,1)S(1)}, u32[]{:S(2)}, u32[]{:S(2)}) %collective-permute-start.1) | collective-permute-done | bytes 202784 | tf_op jit(solution)/shard_map/ppermute | solution.py:318
  38.7 0.0 collective-permute-done.refs_1_
  38.7 0.5 plan.1
  39.2 4.7 %sort_bins.1.bins = bf16[15568,128]{1,0:T(8,128)(2,1)S(1)} custom-call(s32[48,128]{1,0:T(8,128)S(1)} %get-tuple-element.14.where, bf16[264,384]{1,0:T(8,128)(2,1)S(1)} %own_bins.1.refs_0_, bf16[264,384]{1,0:T(8,128)(2,1)S(1)} %collective-permute-done.refs_1_, bf16[264,384]{1,0:T(8,128)(2,1)S(1)} %collective-permute-done.1.refs_2_, ...), custom_call_target="tpu_custom_call" | custom-call | tf_op jit(solution)/shard_map/sort_bins/pallas_call | solution.py:393
  43.9 4.8 %near.1.near_grads = bf16[15568,256]{1,0:T(8,128)(2,1)S(1)} custom-call(s32[48,128]{1,0:T(8,128)S(1)} %get-tuple-element.14.where, f32[4,136,384]{2,1,0:T(8,128)S(1)} %pad_maximum_fusion.near, f32[32,384]{1,0:T(8,128)S(1)} %maximum_convert_fusion.given.parents, f32[48,256]{1,0:T(8,128)S(1)} %get-tuple-element.17.slots.refs_4_, f32[32,16]{1,0:T(8,128)S(1)} %bitcast.26), custom_call_target="tpu_custom_call" | custom-call | tf_op jit(solution)/shard_map/near/pallas_call | solution.py:407
  48.7 0.0 collective-permute-done.9.far
  48.7 25.4 %level.1 = (f32[4,4,2048]{2,1,0:T(4,128)S(1)}, f32[4,1,256]{2,1,0:T(1,128)S(1)}) custom-call(s32[48,128]{1,0:T(8,128)S(1)} %get-tuple-element.14.where, s32[8,128]{1,0:T(8,128)S(1)} %get-tuple-element.15.chunks, bf16[15568,256]{1,0:T(8,128)(2,1)S(1)} %near.1.near_grads, f32[4,136,384]{2,1,0:T(8,128)S(1)} %collective-permute-done.9.far, ...), custom_call_target="tpu_custom_call" | custom-call | tf_op jit(solution)/shard_map/level/pallas_call | solution.py:416
  74.0 0.1 fusion
  74.2 0.6 collective-permute-start.12
  74.7 1.0 %collective-permute-start.11 = (f32[4,2048]{1,0:T(4,128)S(1)}, f32[4,2048]{1,0:T(4,128)S(1)}, u32[]{:S(2)}, u32[]{:S(2)}) collective-permute-start(f32[4,2048]{1,0:T(4,128)S(1)} %get-tuple-element.24), channel_id=1, source_target_pairs={{0,16},{1,17},{2,18},{3,19},{4,20},{5,21},{6,22},{7,23},{8,24},{9,... | collective-permute-start | bytes 98312 | tf_op jit(solution)/shard_map/ppermute | solution.py:318
  75.7 0.4 collective-permute-start.10
  76.1 0.1 reshape.31
  76.2 0.7 reshape.32
  76.9 1.0 %collective-permute-done.12 = f32[4,2048]{1,0:T(4,128)S(1)} collective-permute-done((f32[4,2048]{1,0:T(4,128)S(1)}, f32[4,2048]{1,0:T(4,128)S(1)}, u32[]{:S(2)}, u32[]{:S(2)}) %collective-permute-start.12) | collective-permute-done | bytes 32800 | tf_op jit(solution)/shard_map/ppermute | solution.py:318
  77.9 1.1 %collective-permute-done.11 = f32[4,2048]{1,0:T(4,128)S(1)} collective-permute-done((f32[4,2048]{1,0:T(4,128)S(1)}, f32[4,2048]{1,0:T(4,128)S(1)}, u32[]{:S(2)}, u32[]{:S(2)}) %collective-permute-start.11) | collective-permute-done | bytes 32800 | tf_op jit(solution)/shard_map/ppermute | solution.py:318
  79.0 0.0 collective-permute-done.10
  79.1 0.2 reshape_reshape.11
  79.3 0.2 copy.13
  79.4 0.8 copy.15
  (15 shorter events, 0.2 us)
Async XLA Ops:
  0.6 28.3 %copy-start = (s32[128,3072]{1,0:T(8,128)S(1)}, s32[128,3072]{1,0:T(8,128)}, u32[]{:S(2)}) copy-start(s32[128,3072]{1,0:T(8,128)} %refs_4_.1) | copy-start | bytes 4718596
  0.6 29.2 %copy-start.2 = (f32[16,32]{1,0:T(8,128)S(1)}, f32[16,32]{1,0:T(8,128)}, u32[]{:S(2)}) copy-start(f32[16,32]{1,0:T(8,128)} %param.13) | copy-start | bytes 6148
  3.2 6.6 %collective-permute-start.3 = (f32[40,384]{1,0:T(8,128)}, f32[40,384]{1,0:T(8,128)S(1)}, u32[]{:S(2)}, u32[]{:S(2)}) collective-permute-start(f32[40,384]{1,0:T(8,128)} %get-tuple-element.16), channel_id=1, source_target_pairs={{0,2},{1,3},{2,0},{3,1},{4,6},{5,7},{6,4},{7,5},{8,10},{9,11},{10,... | collective-permute-start | bytes 184328 | tf_op jit(solution)/shard_map/ppermute | solution.py:318
  6.3 6.6 %collective-permute-start.4 = (f32[40,384]{1,0:T(8,128)}, f32[40,384]{1,0:T(8,128)S(1)}, u32[]{:S(2)}, u32[]{:S(2)}) collective-permute-start(f32[40,384]{1,0:T(8,128)} %get-tuple-element.16), channel_id=1, source_target_pairs={{0,4},{1,5},{2,6},{3,7},{4,0},{5,1},{6,2},{7,3},{8,12},{9,13},{10,... | collective-permute-start | bytes 184328 | tf_op jit(solution)/shard_map/ppermute | solution.py:318
  8.9 6.2 %collective-permute-start.5 = (f32[40,384]{1,0:T(8,128)}, f32[40,384]{1,0:T(8,128)S(1)}, u32[]{:S(2)}, u32[]{:S(2)}) collective-permute-start(f32[40,384]{1,0:T(8,128)} %get-tuple-element.16), channel_id=1, source_target_pairs={{0,6},{1,7},{2,4},{3,5},{4,2},{5,3},{6,0},{7,1},{8,14},{9,15},{10,... | collective-permute-start | bytes 184328 | tf_op jit(solution)/shard_map/ppermute | solution.py:318
  15.8 8.6 %collective-permute-start.8 = (f32[136,384]{1,0:T(8,128)S(1)}, f32[136,384]{1,0:T(8,128)S(1)}, u32[]{:S(2)}, u32[]{:S(2)}) collective-permute-start(f32[136,384]{1,0:T(8,128)S(1)} %fusion.2), channel_id=1, source_target_pairs={{0,17},{1,16},{2,19},{3,18},{4,21},{5,20},{6,23},{7,22},{8,25},{9,... | collective-permute-start | bytes 626696 | tf_op jit(solution)/shard_map/ppermute | solution.py:318
  18.3 8.2 %collective-permute-start.7 = (f32[136,384]{1,0:T(8,128)S(1)}, f32[136,384]{1,0:T(8,128)S(1)}, u32[]{:S(2)}, u32[]{:S(2)}) collective-permute-start(f32[136,384]{1,0:T(8,128)S(1)} %fusion.2), channel_id=1, source_target_pairs={{0,16},{1,17},{2,18},{3,19},{4,20},{5,21},{6,22},{7,23},{8,24},{9,... | collective-permute-start | bytes 626696 | tf_op jit(solution)/shard_map/ppermute | solution.py:318
  18.8 7.8 %collective-permute-start.6 = (f32[136,384]{1,0:T(8,128)S(1)}, f32[136,384]{1,0:T(8,128)S(1)}, u32[]{:S(2)}, u32[]{:S(2)}) collective-permute-start(f32[136,384]{1,0:T(8,128)S(1)} %fusion.2), channel_id=1, source_target_pairs={{0,1},{1,0},{2,3},{3,2},{4,5},{5,4},{6,7},{7,6},{8,9},{9,8},{10,11... | collective-permute-start | bytes 626696 | tf_op jit(solution)/shard_map/ppermute | solution.py:318
  26.7 22.0 %collective-permute-start.9 = (f32[4,136,384]{2,1,0:T(8,128)S(1)}, f32[4,136,384]{2,1,0:T(8,128)S(1)}, u32[]{:S(2)}, u32[]{:S(2)}) collective-permute-start(f32[4,136,384]{2,1,0:T(8,128)S(1)} %pad_maximum_fusion.near), channel_id=1, source_target_pairs={{0,8},{1,9},{2,10},{3,11},{4,12},{5,13},{6,14},{7,15},{8,0},{9,1},... | collective-permute-start | bytes 2506760 | tf_op jit(solution)/shard_map/ppermute | solution.py:318
  26.8 7.3 %collective-permute-start.2 = (bf16[264,384]{1,0:T(8,128)(2,1)}, bf16[264,384]{1,0:T(8,128)(2,1)S(1)}, u32[]{:S(2)}, u32[]{:S(2)}) collective-permute-start(bf16[264,384]{1,0:T(8,128)(2,1)} %get-tuple-element.13), channel_id=1, source_target_pairs={{0,24},{1,25},{2,26},{3,27},{4,28},{5,29},{6,30},{7,31},{8,16},{9,... | collective-permute-start | bytes 608264 | tf_op jit(solution)/shard_map/ppermute | solution.py:318
  28.3 10.4 %collective-permute-start.1 = (bf16[264,384]{1,0:T(8,128)(2,1)}, bf16[264,384]{1,0:T(8,128)(2,1)S(1)}, u32[]{:S(2)}, u32[]{:S(2)}) collective-permute-start(bf16[264,384]{1,0:T(8,128)(2,1)} %get-tuple-element.12), channel_id=1, source_target_pairs={{0,16},{1,17},{2,18},{3,19},{4,20},{5,21},{6,22},{7,23},{8,24},{9,... | collective-permute-start | bytes 608264 | tf_op jit(solution)/shard_map/ppermute | solution.py:318
  28.9 9.8 %collective-permute-start = (bf16[264,384]{1,0:T(8,128)(2,1)}, bf16[264,384]{1,0:T(8,128)(2,1)S(1)}, u32[]{:S(2)}, u32[]{:S(2)}) collective-permute-start(bf16[264,384]{1,0:T(8,128)(2,1)} %get-tuple-element.11), channel_id=1, source_target_pairs={{0,8},{1,9},{2,10},{3,11},{4,12},{5,13},{6,14},{7,15},{8,0},{9,1},... | collective-permute-start | bytes 608264 | tf_op jit(solution)/shard_map/ppermute | solution.py:318
  28.9 0.7 copy-start.1
  74.2 3.7 %collective-permute-start.12 = (f32[4,2048]{1,0:T(4,128)S(1)}, f32[4,2048]{1,0:T(4,128)S(1)}, u32[]{:S(2)}, u32[]{:S(2)}) collective-permute-start(f32[4,2048]{1,0:T(4,128)S(1)} %get-tuple-element.23), channel_id=1, source_target_pairs={{0,24},{1,25},{2,26},{3,27},{4,28},{5,29},{6,30},{7,31},{8,16},{9,... | collective-permute-start | bytes 98312 | tf_op jit(solution)/shard_map/ppermute | solution.py:318
  74.7 4.2 %collective-permute-start.11 = (f32[4,2048]{1,0:T(4,128)S(1)}, f32[4,2048]{1,0:T(4,128)S(1)}, u32[]{:S(2)}, u32[]{:S(2)}) collective-permute-start(f32[4,2048]{1,0:T(4,128)S(1)} %get-tuple-element.24), channel_id=1, source_target_pairs={{0,16},{1,17},{2,18},{3,19},{4,20},{5,21},{6,22},{7,23},{8,24},{9,... | collective-permute-start | bytes 98312 | tf_op jit(solution)/shard_map/ppermute | solution.py:318
  75.7 3.2 %collective-permute-start.10 = (f32[4,2048]{1,0:T(4,128)S(1)}, f32[4,2048]{1,0:T(4,128)S(1)}, u32[]{:S(2)}, u32[]{:S(2)}) collective-permute-start(f32[4,2048]{1,0:T(4,128)S(1)} %get-tuple-element.25), channel_id=1, source_target_pairs={{0,8},{1,9},{2,10},{3,11},{4,12},{5,13},{6,14},{7,15},{8,0},{9,1},... | collective-permute-start | bytes 98312 | tf_op jit(solution)/shard_map/ppermute | solution.py:318

commit v5 on v4

--- a/solution.py
+++ b/solution.py
@@ -86,6 +86,14 @@
     label = 2.0 * labels[...].astype(F32).reshape(1, own)
     mine = iota((nf, own), 0) == feat
     out[classes:, :] = jnp.concatenate([right[:, cut] for cut in cuts], axis=0) + jnp.where(mine, label, 0.0)
+
+
+def each(count, limit, step):
+    if count <= limit:
+        for i in range(count):
+            step(i)
+    else:
+        pl.loop(0, count)(step)
 
 
 def cut_pair(pair, sub):
@@ -137,20 +145,24 @@
         spans = spans + jnp.where((lane8 == q) & (row8 == 0), region, 0)
         spans = spans + jnp.where((lane8 == q) & (row8 == 1), length, 0)
         region = region + length
-    where[...] = place
+    where[...] = place * TILE
     chunks[...] = spans
 
 
 def put_block(values, slot, tiles, where, block, out):
     own = values.shape[1]
-    hot = (iota((tiles * TILE, own), 0) == slot.astype(I32)).astype(F32).astype(BF16)
+    middle = tiles * TILE // 2
+    line = (iota((tiles * TILE, own), 0) - middle).astype(F32).astype(BF16)
+    wanted = jnp.broadcast_to(slot - middle, (tiles * TILE, own)).astype(BF16)
+    hot = jnp.where(line == wanted, jnp.asarray(1, BF16), jnp.asarray(0, BF16))
     placed = lax.dot_general(hot, values, NT, preferred_element_type=F32).astype(BF16)
+    places = [where[block, t] for t in range(tiles)]
     for t in range(tiles):
-        to = pl.multiple_of(where[block, t] * TILE, TILE)
+        to = pl.multiple_of(places[t], TILE)
         out[pl.ds(to, TILE), :] = placed[t * TILE : (t + 1) * TILE]
 
 
-def sort_bins_kernel(nr, nf, lo, sub, tiles, unroll, where, *refs):
+def sort_bins_kernel(nr, nf, lo, sub, tiles, where, *refs):
     bins = refs[:nr]
     slots, out = refs[nr:]
     own_feats = (bins[0].shape[0] - nf) // nf
@@ -159,18 +171,17 @@
     feat = lax.axis_index("feat")
     for j in range(nr):
 
-        @pl.loop(0, nf // (lo * unroll))
-        def _(i):
-            for u in range(unroll):
-                jz = i * unroll + u
-                pair = []
-                for jx in range(lo):
-                    k = jnp.bitwise_xor(feat, jz * lo + jx)
-                    pair.append(bins[j][pl.ds(pl.multiple_of(k * own_feats, own_feats), own_feats), :])
-                for c, values in enumerate(cut_pair(pair, sub)):
-                    part = (j * (nf // lo) + jz) * cuts + c
-                    values = jnp.concatenate([values] * copies, axis=0)
-                    put_block(values, slots[pl.ds(part, 1), :], tiles, where, part, out)
+        def sort_pair(jz):
+            pair = []
+            for jx in range(lo):
+                k = jnp.bitwise_xor(feat, jz * lo + jx)
+                pair.append(bins[j][pl.ds(pl.multiple_of(k * own_feats, own_feats), own_feats), :])
+            for c, values in enumerate(cut_pair(pair, sub)):
+                part = (j * (nf // lo) + jz) * cuts + c
+                values = jnp.concatenate([values] * copies, axis=0)
+                put_block(values, slots[pl.ds(part, 1), :], tiles, where, part, out)
+
+        each(nf // lo, 4, sort_pair)
 
 
 def put_grads(sizes, jc, where, source, parents, slots, leaf, grads):
@@ -185,8 +196,7 @@
     leaf_parts = jnp.concatenate(leaf_parts, axis=1)
     grads[...] = jnp.zeros(grads.shape, BF16)
 
-    @pl.loop(0, ny)
-    def _(jy):
+    def put_rows(jy):
         j = jy * 2 + jc
         pair = []
         for jz, jx in [(jz, jx) for jz in range(hi) for jx in range(lo)]:
@@ -204,13 +214,17 @@
             moved = jnp.dot(leaf_parts, jnp.concatenate([node_hot] * 3, axis=0), preferred_element_type=F32)
             logits = margins + moved
             powers = jnp.exp(logits - jnp.max(logits, axis=0, keepdims=True))
-            prob = powers / jnp.sum(powers, axis=0, keepdims=True)
+            prob = powers * (1.0 / jnp.sum(powers, axis=0, keepdims=True))
             hot = label == iota((classes, own), 0).astype(F32)
             gradient = prob - jnp.where(hot, 1.0, 0.0)
             hessian = 2.0 * prob * (1.0 - prob)
             member = node - GROUP_NODES * jnp.floor(node * (1.0 / GROUP_NODES))
-            parts = [jnp.where(member == n, v, 0.0) for v in (gradient, hessian) for n in range(GROUP_NODES)]
-            pair.append(jnp.concatenate(parts, axis=0).astype(BF16))
+            member = jnp.broadcast_to(member, (classes, own)).astype(BF16)
+            none = jnp.zeros((classes, own), BF16)
+            parts = []
+            for value in (gradient.astype(BF16), hessian.astype(BF16)):
+                parts += [jnp.where(member == jnp.asarray(n, BF16), value, none) for n in range(GROUP_NODES)]
+            pair.append(jnp.concatenate(parts, axis=0))
             if jx < lo - 1:
                 continue
             cuts = cut_pair(pair, sub)
@@ -218,6 +232,8 @@
             for c, columns in enumerate(cuts):
                 part = (j * hi + jz) * len(cuts) + c
                 put_block(columns, slots[pl.ds(part, 1), :], tiles, where, part, grads)
+
+    each(ny, 2, put_rows)
 
 
 def near_kernel(sizes, where, near, parents, slots, leaf, grads):
@@ -391,7 +407,7 @@
     )(all_parents)
 
     ordered_bins = pl.pallas_call(
-        functools.partial(sort_bins_kernel, nr, nf, lo, sub, tiles, 2),
+        functools.partial(sort_bins_kernel, nr, nf, lo, sub, tiles),
         out_shape=jax.ShapeDtypeStruct((ordered_rows, LANES), BF16),
         in_specs=[SMEM] + [VMEM] * (nr + 1),
         out_specs=VMEM,

time: 80.5 us -> 78.2 us (0.971)
  Pallas kernels: 38 us -> 35.7 us
    pallas_call x1, Pallas kernels: 4.69 us -> 3.07 us  [body(): pl.pallas_call(functools.partial(sort_bins_kernel, nr, nf, lo, sub, tiles...]
  transfers between devices with their start and end apart: 13 -> 13, of which waited for: 9 -> 9; matrix products, arithmetic and copies ran while one was open for 2% -> 2% of each run, Pallas kernels for 13% -> 10%
where the time goes in v5:
time: 78.2 us; the launch traced here: 77.9 us
  Pallas kernels  35.7 us (46%)
  waiting for transfers between devices  23.5 us (30%)
  starting transfers between devices  13.3 us (17%)
  local copies, waits for them, and re-layouts  3.62 us (5%)
  other arithmetic  0.97 us (1%)
  between operations  0.83 us (1%)
    pallas_call x1, Pallas kernels, body(): pl.pallas_call(functools.partial(level_kernel, shape), out_shape=(jax.Sha...  25.1 us
    ppermute x13, waiting for transfers between devices, swap(): return lax.ppermute(value, axes, [(i, i ^ flat) for i in range(total)])  23.5 us
    ppermute x13, starting transfers between devices, swap(): return lax.ppermute(value, axes, [(i, i ^ flat) for i in range(total)])  13.3 us
    pallas_call x1, Pallas kernels, body(): pl.pallas_call(functools.partial(near_kernel, shape), out_shape=jax.Shape...  4.3 us
    pallas_call x1, Pallas kernels, body(): pl.pallas_call(functools.partial(sort_bins_kernel, nr, nf, lo, sub, tiles...  3.07 us
    pallas_call x1, Pallas kernels, body(): pl.pallas_call(functools.partial(first_kernel, nr, nf), out_shape=[jax.Sh...  2.53 us
    unnamed x12, local copies, waits for them, and re-layouts  2.45 us
  transfers between devices with their start and end apart: 13, of which 9 were waited for; matrix products, arithmetic and copies ran while one was open for 2% of the time, Pallas kernels for 10%

profile of v5, /device:TPU:0, one launch (start us, length us, event | category | flops | bytes accessed | tf_op | source)
XLA Modules:
  0.0 77.9 jit_solution(9399201183050570168)
XLA Ops:
  0.6 0.0 copy-start
  0.6 0.0 copy-start.2
  0.7 2.5 %first.1 = (f32[40,384]{1,0:T(8,128)}, bf16[264,384]{1,0:T(8,128)(2,1)}, bf16[264,384]{1,0:T(8,128)(2,1)}, bf16[264,384]{1,0:T(8,128)(2,1)}) custom-call(s32[8]{0:T(128)} %refs_0_.1, s32[8]{0:T(128)} %refs_1_.1, f32[32,384]{1,0:T(8,128)} %bitcast.40, s32[384]{0:T(512)} %refs_3_.1, s32[128,3072]{1,0:T(8,128)} %refs_4_.1, s32[1,3072]{1,0:T(1,128)} %bitcast.29), custom_call_target="tpu_custom_call" | custom-call | tf_op jit(solution)/shard_map/first/pallas_call | solution.py:354
  3.2 3.1 %collective-permute-start.3 = (f32[40,384]{1,0:T(8,128)}, f32[40,384]{1,0:T(8,128)S(1)}, u32[]{:S(2)}, u32[]{:S(2)}) collective-permute-start(f32[40,384]{1,0:T(8,128)} %get-tuple-element.16), channel_id=1, source_target_pairs={{0,2},{1,3},{2,0},{3,1},{4,6},{5,7},{6,4},{7,5},{8,10},{9,11},{10,... | collective-permute-start | bytes 184328 | tf_op jit(solution)/shard_map/ppermute | solution.py:334
  6.3 2.6 %collective-permute-start.4 = (f32[40,384]{1,0:T(8,128)}, f32[40,384]{1,0:T(8,128)S(1)}, u32[]{:S(2)}, u32[]{:S(2)}) collective-permute-start(f32[40,384]{1,0:T(8,128)} %get-tuple-element.16), channel_id=1, source_target_pairs={{0,4},{1,5},{2,6},{3,7},{4,0},{5,1},{6,2},{7,3},{8,12},{9,13},{10,... | collective-permute-start | bytes 184328 | tf_op jit(solution)/shard_map/ppermute | solution.py:334
  8.9 0.0 collective-permute-start.5
  8.9 0.9 %slice_dynamic-update-slice_fusion.3 = f32[136,384]{1,0:T(8,128)S(1)} fusion(f32[40,384]{1,0:T(8,128)} %get-tuple-element.16), kind=kLoop, calls=%fused_computation.11 | loop fusion | bytes 98304
  9.8 0.0 collective-permute-done.3
  9.8 3.1 %collective-permute-done.4 = f32[40,384]{1,0:T(8,128)S(1)} collective-permute-done((f32[40,384]{1,0:T(8,128)}, f32[40,384]{1,0:T(8,128)S(1)}, u32[]{:S(2)}, u32[]{:S(2)}) %collective-permute-start.4) | collective-permute-done | bytes 61472 | tf_op jit(solution)/shard_map/ppermute | solution.py:334
  12.9 2.2 %collective-permute-done.5 = f32[40,384]{1,0:T(8,128)S(1)} collective-permute-done((f32[40,384]{1,0:T(8,128)}, f32[40,384]{1,0:T(8,128)S(1)}, u32[]{:S(2)}, u32[]{:S(2)}) %collective-permute-start.5) | collective-permute-done | bytes 61472 | tf_op jit(solution)/shard_map/ppermute | solution.py:334
  15.1 0.7 fusion.2
  15.8 2.4 %collective-permute-start.8 = (f32[136,384]{1,0:T(8,128)S(1)}, f32[136,384]{1,0:T(8,128)S(1)}, u32[]{:S(2)}, u32[]{:S(2)}) collective-permute-start(f32[136,384]{1,0:T(8,128)S(1)} %fusion.2), channel_id=1, source_target_pairs={{0,17},{1,16},{2,19},{3,18},{4,21},{5,20},{6,23},{7,22},{8,25},{9,... | collective-permute-start | bytes 626696 | tf_op jit(solution)/shard_map/ppermute | solution.py:334
  18.3 0.5 collective-permute-start.7
  18.8 0.5 collective-permute-start.6
  19.3 5.2 %collective-permute-done.8 = f32[136,384]{1,0:T(8,128)S(1)} collective-permute-done((f32[136,384]{1,0:T(8,128)S(1)}, f32[136,384]{1,0:T(8,128)S(1)}, u32[]{:S(2)}, u32[]{:S(2)}) %collective-permute-start.8) | collective-permute-done | bytes 208928 | tf_op jit(solution)/shard_map/ppermute | solution.py:334
  24.5 2.0 %collective-permute-done.7 = f32[136,384]{1,0:T(8,128)S(1)} collective-permute-done((f32[136,384]{1,0:T(8,128)S(1)}, f32[136,384]{1,0:T(8,128)S(1)}, u32[]{:S(2)}, u32[]{:S(2)}) %collective-permute-start.7) | collective-permute-done | bytes 208928 | tf_op jit(solution)/shard_map/ppermute | solution.py:334
  26.5 0.1 collective-permute-done.6
  26.6 0.1 pad_maximum_fusion.near
  26.7 0.1 collective-permute-start.9
  26.8 1.5 %collective-permute-start.2 = (bf16[264,384]{1,0:T(8,128)(2,1)}, bf16[264,384]{1,0:T(8,128)(2,1)S(1)}, u32[]{:S(2)}, u32[]{:S(2)}) collective-permute-start(bf16[264,384]{1,0:T(8,128)(2,1)} %get-tuple-element.13), channel_id=1, source_target_pairs={{0,24},{1,25},{2,26},{3,27},{4,28},{5,29},{6,30},{7,31},{8,16},{9,... | collective-permute-start | bytes 608264 | tf_op jit(solution)/shard_map/ppermute | solution.py:334
  28.3 0.6 collective-permute-start.1
  28.9 0.0 collective-permute-start
  28.9 0.0 copy-done
  28.9 0.0 copy-start.1
  28.9 0.7 copy-done.1
  29.6 0.2 own_bins.1.refs_0_
  29.9 0.0 copy-done.2
  29.9 0.1 copy.12
  30.0 4.1 %collective-permute-done.2.refs_3_ = bf16[264,384]{1,0:T(8,128)(2,1)S(1)} collective-permute-done((bf16[264,384]{1,0:T(8,128)(2,1)}, bf16[264,384]{1,0:T(8,128)(2,1)S(1)}, u32[]{:S(2)}, u32[]{:S(2)}) %collective-permute-start.2) | collective-permute-done | bytes 202784 | tf_op jit(solution)/shard_map/ppermute | solution.py:334
  34.0 4.7 %collective-permute-done.1.refs_2_ = bf16[264,384]{1,0:T(8,128)(2,1)S(1)} collective-permute-done((bf16[264,384]{1,0:T(8,128)(2,1)}, bf16[264,384]{1,0:T(8,128)(2,1)S(1)}, u32[]{:S(2)}, u32[]{:S(2)}) %collective-permute-start.1) | collective-permute-done | bytes 202784 | tf_op jit(solution)/shard_map/ppermute | solution.py:334
  38.7 0.0 collective-permute-done.refs_1_
  38.7 0.5 plan.1
  39.2 3.1 %sort_bins.1.bins = bf16[15568,128]{1,0:T(8,128)(2,1)S(1)} custom-call(s32[48,128]{1,0:T(8,128)S(1)} %get-tuple-element.14.where, bf16[264,384]{1,0:T(8,128)(2,1)S(1)} %own_bins.1.refs_0_, bf16[264,384]{1,0:T(8,128)(2,1)S(1)} %collective-permute-done.refs_1_, bf16[264,384]{1,0:T(8,128)(2,1)S(1)} %collective-permute-done.1.refs_2_, ...), custom_call_target="tpu_custom_call" | custom-call | tf_op jit(solution)/shard_map/sort_bins/pallas_call | solution.py:409
  42.3 4.3 %near.1.near_grads = bf16[15568,256]{1,0:T(8,128)(2,1)S(1)} custom-call(s32[48,128]{1,0:T(8,128)S(1)} %get-tuple-element.14.where, f32[4,136,384]{2,1,0:T(8,128)S(1)} %pad_maximum_fusion.near, f32[32,384]{1,0:T(8,128)S(1)} %maximum_convert_fusion.given.parents, f32[48,256]{1,0:T(8,128)S(1)} %get-tuple-element.17.slots.refs_4_, f32[32,16]{1,0:T(8,128)S(1)} %bitcast.26), custom_call_target="tpu_custom_call" | custom-call | tf_op jit(solution)/shard_map/near/pallas_call | solution.py:423
  46.6 0.0 collective-permute-done.9.far
  46.6 25.1 %level.1 = (f32[4,4,2048]{2,1,0:T(4,128)S(1)}, f32[4,1,256]{2,1,0:T(1,128)S(1)}) custom-call(s32[48,128]{1,0:T(8,128)S(1)} %get-tuple-element.14.where, s32[8,128]{1,0:T(8,128)S(1)} %get-tuple-element.15.chunks, bf16[15568,256]{1,0:T(8,128)(2,1)S(1)} %near.1.near_grads, f32[4,136,384]{2,1,0:T(8,128)S(1)} %collective-permute-done.9.far, ...), custom_call_target="tpu_custom_call" | custom-call | tf_op jit(solution)/shard_map/level/pallas_call | solution.py:432
  71.7 0.1 fusion
  71.8 0.6 collective-permute-start.12
  72.4 1.0 %collective-permute-start.11 = (f32[4,2048]{1,0:T(4,128)S(1)}, f32[4,2048]{1,0:T(4,128)S(1)}, u32[]{:S(2)}, u32[]{:S(2)}) collective-permute-start(f32[4,2048]{1,0:T(4,128)S(1)} %get-tuple-element.24), channel_id=1, source_target_pairs={{0,16},{1,17},{2,18},{3,19},{4,20},{5,21},{6,22},{7,23},{8,24},{9,... | collective-permute-start | bytes 98312 | tf_op jit(solution)/shard_map/ppermute | solution.py:334
  73.4 0.4 collective-permute-start.10
  73.8 0.1 reshape.31
  73.9 0.7 reshape.32
  74.5 1.0 %collective-permute-done.12 = f32[4,2048]{1,0:T(4,128)S(1)} collective-permute-done((f32[4,2048]{1,0:T(4,128)S(1)}, f32[4,2048]{1,0:T(4,128)S(1)}, u32[]{:S(2)}, u32[]{:S(2)}) %collective-permute-start.12) | collective-permute-done | bytes 32800 | tf_op jit(solution)/shard_map/ppermute | solution.py:334
  75.5 1.1 %collective-permute-done.11 = f32[4,2048]{1,0:T(4,128)S(1)} collective-permute-done((f32[4,2048]{1,0:T(4,128)S(1)}, f32[4,2048]{1,0:T(4,128)S(1)}, u32[]{:S(2)}, u32[]{:S(2)}) %collective-permute-start.11) | collective-permute-done | bytes 32800 | tf_op jit(solution)/shard_map/ppermute | solution.py:334
  76.6 0.0 collective-permute-done.10
  76.7 0.2 reshape_reshape.11
  76.9 0.2 copy.13
  77.1 0.8 %copy.15 = f32[4,128,64]{1,2,0:T(8,128)} copy(f32[4,128,64]{2,1,0:T(8,128)S(1)} %bitcast.32) | data formatting | bytes 262144
  (15 shorter events, 0.2 us)
Async XLA Ops:
  0.6 28.3 %copy-start = (s32[128,3072]{1,0:T(8,128)S(1)}, s32[128,3072]{1,0:T(8,128)}, u32[]{:S(2)}) copy-start(s32[128,3072]{1,0:T(8,128)} %refs_4_.1) | copy-start | bytes 4718596
  0.6 29.2 %copy-start.2 = (f32[16,32]{1,0:T(8,128)S(1)}, f32[16,32]{1,0:T(8,128)}, u32[]{:S(2)}) copy-start(f32[16,32]{1,0:T(8,128)} %param.13) | copy-start | bytes 6148
  3.2 6.6 %collective-permute-start.3 = (f32[40,384]{1,0:T(8,128)}, f32[40,384]{1,0:T(8,128)S(1)}, u32[]{:S(2)}, u32[]{:S(2)}) collective-permute-start(f32[40,384]{1,0:T(8,128)} %get-tuple-element.16), channel_id=1, source_target_pairs={{0,2},{1,3},{2,0},{3,1},{4,6},{5,7},{6,4},{7,5},{8,10},{9,11},{10,... | collective-permute-start | bytes 184328 | tf_op jit(solution)/shard_map/ppermute | solution.py:334
  6.3 6.6 %collective-permute-start.4 = (f32[40,384]{1,0:T(8,128)}, f32[40,384]{1,0:T(8,128)S(1)}, u32[]{:S(2)}, u32[]{:S(2)}) collective-permute-start(f32[40,384]{1,0:T(8,128)} %get-tuple-element.16), channel_id=1, source_target_pairs={{0,4},{1,5},{2,6},{3,7},{4,0},{5,1},{6,2},{7,3},{8,12},{9,13},{10,... | collective-permute-start | bytes 184328 | tf_op jit(solution)/shard_map/ppermute | solution.py:334
  8.9 6.2 %collective-permute-start.5 = (f32[40,384]{1,0:T(8,128)}, f32[40,384]{1,0:T(8,128)S(1)}, u32[]{:S(2)}, u32[]{:S(2)}) collective-permute-start(f32[40,384]{1,0:T(8,128)} %get-tuple-element.16), channel_id=1, source_target_pairs={{0,6},{1,7},{2,4},{3,5},{4,2},{5,3},{6,0},{7,1},{8,14},{9,15},{10,... | collective-permute-start | bytes 184328 | tf_op jit(solution)/shard_map/ppermute | solution.py:334
  15.8 8.6 %collective-permute-start.8 = (f32[136,384]{1,0:T(8,128)S(1)}, f32[136,384]{1,0:T(8,128)S(1)}, u32[]{:S(2)}, u32[]{:S(2)}) collective-permute-start(f32[136,384]{1,0:T(8,128)S(1)} %fusion.2), channel_id=1, source_target_pairs={{0,17},{1,16},{2,19},{3,18},{4,21},{5,20},{6,23},{7,22},{8,25},{9,... | collective-permute-start | bytes 626696 | tf_op jit(solution)/shard_map/ppermute | solution.py:334
  18.3 8.2 %collective-permute-start.7 = (f32[136,384]{1,0:T(8,128)S(1)}, f32[136,384]{1,0:T(8,128)S(1)}, u32[]{:S(2)}, u32[]{:S(2)}) collective-permute-start(f32[136,384]{1,0:T(8,128)S(1)} %fusion.2), channel_id=1, source_target_pairs={{0,16},{1,17},{2,18},{3,19},{4,20},{5,21},{6,22},{7,23},{8,24},{9,... | collective-permute-start | bytes 626696 | tf_op jit(solution)/shard_map/ppermute | solution.py:334
  18.8 7.8 %collective-permute-start.6 = (f32[136,384]{1,0:T(8,128)S(1)}, f32[136,384]{1,0:T(8,128)S(1)}, u32[]{:S(2)}, u32[]{:S(2)}) collective-permute-start(f32[136,384]{1,0:T(8,128)S(1)} %fusion.2), channel_id=1, source_target_pairs={{0,1},{1,0},{2,3},{3,2},{4,5},{5,4},{6,7},{7,6},{8,9},{9,8},{10,11... | collective-permute-start | bytes 626696 | tf_op jit(solution)/shard_map/ppermute | solution.py:334
  26.7 19.9 %collective-permute-start.9 = (f32[4,136,384]{2,1,0:T(8,128)S(1)}, f32[4,136,384]{2,1,0:T(8,128)S(1)}, u32[]{:S(2)}, u32[]{:S(2)}) collective-permute-start(f32[4,136,384]{2,1,0:T(8,128)S(1)} %pad_maximum_fusion.near), channel_id=1, source_target_pairs={{0,8},{1,9},{2,10},{3,11},{4,12},{5,13},{6,14},{7,15},{8,0},{9,1},... | collective-permute-start | bytes 2506760 | tf_op jit(solution)/shard_map/ppermute | solution.py:334
  26.8 7.3 %collective-permute-start.2 = (bf16[264,384]{1,0:T(8,128)(2,1)}, bf16[264,384]{1,0:T(8,128)(2,1)S(1)}, u32[]{:S(2)}, u32[]{:S(2)}) collective-permute-start(bf16[264,384]{1,0:T(8,128)(2,1)} %get-tuple-element.13), channel_id=1, source_target_pairs={{0,24},{1,25},{2,26},{3,27},{4,28},{5,29},{6,30},{7,31},{8,16},{9,... | collective-permute-start | bytes 608264 | tf_op jit(solution)/shard_map/ppermute | solution.py:334
  28.3 10.4 %collective-permute-start.1 = (bf16[264,384]{1,0:T(8,128)(2,1)}, bf16[264,384]{1,0:T(8,128)(2,1)S(1)}, u32[]{:S(2)}, u32[]{:S(2)}) collective-permute-start(bf16[264,384]{1,0:T(8,128)(2,1)} %get-tuple-element.12), channel_id=1, source_target_pairs={{0,16},{1,17},{2,18},{3,19},{4,20},{5,21},{6,22},{7,23},{8,24},{9,... | collective-permute-start | bytes 608264 | tf_op jit(solution)/shard_map/ppermute | solution.py:334
  28.9 9.8 %collective-permute-start = (bf16[264,384]{1,0:T(8,128)(2,1)}, bf16[264,384]{1,0:T(8,128)(2,1)S(1)}, u32[]{:S(2)}, u32[]{:S(2)}) collective-permute-start(bf16[264,384]{1,0:T(8,128)(2,1)} %get-tuple-element.11), channel_id=1, source_target_pairs={{0,8},{1,9},{2,10},{3,11},{4,12},{5,13},{6,14},{7,15},{8,0},{9,1},... | collective-permute-start | bytes 608264 | tf_op jit(solution)/shard_map/ppermute | solution.py:334
  28.9 0.7 copy-start.1
  71.8 3.7 %collective-permute-start.12 = (f32[4,2048]{1,0:T(4,128)S(1)}, f32[4,2048]{1,0:T(4,128)S(1)}, u32[]{:S(2)}, u32[]{:S(2)}) collective-permute-start(f32[4,2048]{1,0:T(4,128)S(1)} %get-tuple-element.23), channel_id=1, source_target_pairs={{0,24},{1,25},{2,26},{3,27},{4,28},{5,29},{6,30},{7,31},{8,16},{9,... | collective-permute-start | bytes 98312 | tf_op jit(solution)/shard_map/ppermute | solution.py:334
  72.4 4.2 %collective-permute-start.11 = (f32[4,2048]{1,0:T(4,128)S(1)}, f32[4,2048]{1,0:T(4,128)S(1)}, u32[]{:S(2)}, u32[]{:S(2)}) collective-permute-start(f32[4,2048]{1,0:T(4,128)S(1)} %get-tuple-element.24), channel_id=1, source_target_pairs={{0,16},{1,17},{2,18},{3,19},{4,20},{5,21},{6,22},{7,23},{8,24},{9,... | collective-permute-start | bytes 98312 | tf_op jit(solution)/shard_map/ppermute | solution.py:334
  73.4 3.2 %collective-permute-start.10 = (f32[4,2048]{1,0:T(4,128)S(1)}, f32[4,2048]{1,0:T(4,128)S(1)}, u32[]{:S(2)}, u32[]{:S(2)}) collective-permute-start(f32[4,2048]{1,0:T(4,128)S(1)} %get-tuple-element.25), channel_id=1, source_target_pairs={{0,8},{1,9},{2,10},{3,11},{4,12},{5,13},{6,14},{7,15},{8,0},{9,1},... | collective-permute-start | bytes 98312 | tf_op jit(solution)/shard_map/ppermute | solution.py:334

commit v6 on v5

--- a/solution.py
+++ b/solution.py
@@ -198,7 +198,7 @@
 
     def put_rows(jy):
         j = jy * 2 + jc
-        pair = []
+        pair, ready = [], []
         for jz, jx in [(jz, jx) for jz in range(hi) for jx in range(lo)]:
             yx = jy * lo + jx
             k = jnp.bitwise_xor(me_feat, jz * lo + jx)
@@ -227,8 +227,9 @@
             pair.append(jnp.concatenate(parts, axis=0))
             if jx < lo - 1:
                 continue
-            cuts = cut_pair(pair, sub)
+            ready.append((jz, cut_pair(pair, sub)))
             pair = []
+        for jz, cuts in ready:
             for c, columns in enumerate(cuts):
                 part = (j * hi + jz) * len(cuts) + c
                 put_block(columns, slots[pl.ds(part, 1), :], tiles, where, part, grads)

time: 78.2 us -> 75.8 us (0.969)
  Pallas kernels: 35.7 us -> 33.3 us
    pallas_call x1, Pallas kernels: 25.1 us -> 23.8 us  [body(): pl.pallas_call(functools.partial(level_kernel, shape), out_shape=(jax.Sha...]
    pallas_call x1, Pallas kernels: 4.3 us -> 3.2 us  [body(): pl.pallas_call(functools.partial(near_kernel, shape), out_shape=jax.Shape...]
  transfers between devices with their start and end apart: 13 -> 13, of which waited for: 9 -> 9; matrix products, arithmetic and copies ran while one was open for 2% -> 2% of each run, Pallas kernels for 10% -> 9%
where the time goes in v6:
time: 75.8 us; the launch traced here: 75.5 us
  Pallas kernels  33.3 us (44%)
  waiting for transfers between devices  23.5 us (31%)
  starting transfers between devices  13.3 us (18%)
  local copies, waits for them, and re-layouts  3.62 us (5%)
  other arithmetic  0.97 us (1%)
  between operations  0.83 us (1%)
    pallas_call x1, Pallas kernels, body(): pl.pallas_call(functools.partial(level_kernel, shape), out_shape=(jax.Sha...  23.8 us
    ppermute x13, waiting for transfers between devices, swap(): return lax.ppermute(value, axes, [(i, i ^ flat) for i in range(total)])  23.5 us
    ppermute x13, starting transfers between devices, swap(): return lax.ppermute(value, axes, [(i, i ^ flat) for i in range(total)])  13.3 us
    pallas_call x1, Pallas kernels, body(): pl.pallas_call(functools.partial(near_kernel, shape), out_shape=jax.Shape...  3.2 us
    pallas_call x1, Pallas kernels, body(): pl.pallas_call(functools.partial(sort_bins_kernel, nr, nf, lo, sub, tiles...  3.07 us
    pallas_call x1, Pallas kernels, body(): pl.pallas_call(functools.partial(first_kernel, nr, nf), out_shape=[jax.Sh...  2.53 us
    unnamed x12, local copies, waits for them, and re-layouts  2.45 us
  transfers between devices with their start and end apart: 13, of which 9 were waited for; matrix products, arithmetic and copies ran while one was open for 2% of the time, Pallas kernels for 9%

profile of v6, /device:TPU:0, one launch (start us, length us, event | category | flops | bytes accessed | tf_op | source)
XLA Modules:
  0.0 75.5 jit_solution(13959214864631294212)
XLA Ops:
  0.6 0.0 copy-start
  0.6 0.0 copy-start.2
  0.7 2.5 %first.1 = (f32[40,384]{1,0:T(8,128)}, bf16[264,384]{1,0:T(8,128)(2,1)}, bf16[264,384]{1,0:T(8,128)(2,1)}, bf16[264,384]{1,0:T(8,128)(2,1)}) custom-call(s32[8]{0:T(128)} %refs_0_.1, s32[8]{0:T(128)} %refs_1_.1, f32[32,384]{1,0:T(8,128)} %bitcast.40, s32[384]{0:T(512)} %refs_3_.1, s32[128,3072]{1,0:T(8,128)} %refs_4_.1, s32[1,3072]{1,0:T(1,128)} %bitcast.29), custom_call_target="tpu_custom_call" | custom-call | tf_op jit(solution)/shard_map/first/pallas_call | solution.py:355
  3.2 3.1 %collective-permute-start.3 = (f32[40,384]{1,0:T(8,128)}, f32[40,384]{1,0:T(8,128)S(1)}, u32[]{:S(2)}, u32[]{:S(2)}) collective-permute-start(f32[40,384]{1,0:T(8,128)} %get-tuple-element.16), channel_id=1, source_target_pairs={{0,2},{1,3},{2,0},{3,1},{4,6},{5,7},{6,4},{7,5},{8,10},{9,11},{10,... | collective-permute-start | bytes 184328 | tf_op jit(solution)/shard_map/ppermute | solution.py:335
  6.3 2.6 %collective-permute-start.4 = (f32[40,384]{1,0:T(8,128)}, f32[40,384]{1,0:T(8,128)S(1)}, u32[]{:S(2)}, u32[]{:S(2)}) collective-permute-start(f32[40,384]{1,0:T(8,128)} %get-tuple-element.16), channel_id=1, source_target_pairs={{0,4},{1,5},{2,6},{3,7},{4,0},{5,1},{6,2},{7,3},{8,12},{9,13},{10,... | collective-permute-start | bytes 184328 | tf_op jit(solution)/shard_map/ppermute | solution.py:335
  8.9 0.0 collective-permute-start.5
  8.9 0.9 %slice_dynamic-update-slice_fusion.3 = f32[136,384]{1,0:T(8,128)S(1)} fusion(f32[40,384]{1,0:T(8,128)} %get-tuple-element.16), kind=kLoop, calls=%fused_computation.11 | loop fusion | bytes 98304
  9.8 0.0 collective-permute-done.3
  9.8 3.1 %collective-permute-done.4 = f32[40,384]{1,0:T(8,128)S(1)} collective-permute-done((f32[40,384]{1,0:T(8,128)}, f32[40,384]{1,0:T(8,128)S(1)}, u32[]{:S(2)}, u32[]{:S(2)}) %collective-permute-start.4) | collective-permute-done | bytes 61472 | tf_op jit(solution)/shard_map/ppermute | solution.py:335
  12.9 2.2 %collective-permute-done.5 = f32[40,384]{1,0:T(8,128)S(1)} collective-permute-done((f32[40,384]{1,0:T(8,128)}, f32[40,384]{1,0:T(8,128)S(1)}, u32[]{:S(2)}, u32[]{:S(2)}) %collective-permute-start.5) | collective-permute-done | bytes 61472 | tf_op jit(solution)/shard_map/ppermute | solution.py:335
  15.1 0.7 fusion.2
  15.8 2.4 %collective-permute-start.8 = (f32[136,384]{1,0:T(8,128)S(1)}, f32[136,384]{1,0:T(8,128)S(1)}, u32[]{:S(2)}, u32[]{:S(2)}) collective-permute-start(f32[136,384]{1,0:T(8,128)S(1)} %fusion.2), channel_id=1, source_target_pairs={{0,17},{1,16},{2,19},{3,18},{4,21},{5,20},{6,23},{7,22},{8,25},{9,... | collective-permute-start | bytes 626696 | tf_op jit(solution)/shard_map/ppermute | solution.py:335
  18.3 0.5 collective-permute-start.7
  18.8 0.5 collective-permute-start.6
  19.3 5.2 %collective-permute-done.8 = f32[136,384]{1,0:T(8,128)S(1)} collective-permute-done((f32[136,384]{1,0:T(8,128)S(1)}, f32[136,384]{1,0:T(8,128)S(1)}, u32[]{:S(2)}, u32[]{:S(2)}) %collective-permute-start.8) | collective-permute-done | bytes 208928 | tf_op jit(solution)/shard_map/ppermute | solution.py:335
  24.5 2.0 %collective-permute-done.7 = f32[136,384]{1,0:T(8,128)S(1)} collective-permute-done((f32[136,384]{1,0:T(8,128)S(1)}, f32[136,384]{1,0:T(8,128)S(1)}, u32[]{:S(2)}, u32[]{:S(2)}) %collective-permute-start.7) | collective-permute-done | bytes 208928 | tf_op jit(solution)/shard_map/ppermute | solution.py:335
  26.5 0.1 collective-permute-done.6
  26.6 0.1 pad_maximum_fusion.near
  26.7 0.1 collective-permute-start.9
  26.8 1.5 %collective-permute-start.2 = (bf16[264,384]{1,0:T(8,128)(2,1)}, bf16[264,384]{1,0:T(8,128)(2,1)S(1)}, u32[]{:S(2)}, u32[]{:S(2)}) collective-permute-start(bf16[264,384]{1,0:T(8,128)(2,1)} %get-tuple-element.13), channel_id=1, source_target_pairs={{0,24},{1,25},{2,26},{3,27},{4,28},{5,29},{6,30},{7,31},{8,16},{9,... | collective-permute-start | bytes 608264 | tf_op jit(solution)/shard_map/ppermute | solution.py:335
  28.3 0.6 collective-permute-start.1
  28.9 0.0 collective-permute-start
  28.9 0.0 copy-done
  28.9 0.0 copy-start.1
  28.9 0.7 copy-done.1
  29.6 0.2 own_bins.1.refs_0_
  29.9 0.0 copy-done.2
  29.9 0.1 copy.12
  30.0 4.1 %collective-permute-done.2.refs_3_ = bf16[264,384]{1,0:T(8,128)(2,1)S(1)} collective-permute-done((bf16[264,384]{1,0:T(8,128)(2,1)}, bf16[264,384]{1,0:T(8,128)(2,1)S(1)}, u32[]{:S(2)}, u32[]{:S(2)}) %collective-permute-start.2) | collective-permute-done | bytes 202784 | tf_op jit(solution)/shard_map/ppermute | solution.py:335
  34.0 4.7 %collective-permute-done.1.refs_2_ = bf16[264,384]{1,0:T(8,128)(2,1)S(1)} collective-permute-done((bf16[264,384]{1,0:T(8,128)(2,1)}, bf16[264,384]{1,0:T(8,128)(2,1)S(1)}, u32[]{:S(2)}, u32[]{:S(2)}) %collective-permute-start.1) | collective-permute-done | bytes 202784 | tf_op jit(solution)/shard_map/ppermute | solution.py:335
  38.7 0.0 collective-permute-done.refs_1_
  38.7 0.5 plan.1
  39.2 3.1 %sort_bins.1.bins = bf16[15568,128]{1,0:T(8,128)(2,1)S(1)} custom-call(s32[48,128]{1,0:T(8,128)S(1)} %get-tuple-element.14.where, bf16[264,384]{1,0:T(8,128)(2,1)S(1)} %own_bins.1.refs_0_, bf16[264,384]{1,0:T(8,128)(2,1)S(1)} %collective-permute-done.refs_1_, bf16[264,384]{1,0:T(8,128)(2,1)S(1)} %collective-permute-done.1.refs_2_, ...), custom_call_target="tpu_custom_call" | custom-call | tf_op jit(solution)/shard_map/sort_bins/pallas_call | solution.py:410
  42.3 3.2 %near.1.near_grads = bf16[15568,256]{1,0:T(8,128)(2,1)S(1)} custom-call(s32[48,128]{1,0:T(8,128)S(1)} %get-tuple-element.14.where, f32[4,136,384]{2,1,0:T(8,128)S(1)} %pad_maximum_fusion.near, f32[32,384]{1,0:T(8,128)S(1)} %maximum_convert_fusion.given.parents, f32[48,256]{1,0:T(8,128)S(1)} %get-tuple-element.17.slots.refs_4_, f32[32,16]{1,0:T(8,128)S(1)} %bitcast.26), custom_call_target="tpu_custom_call" | custom-call | tf_op jit(solution)/shard_map/near/pallas_call | solution.py:424
  45.5 0.0 collective-permute-done.9.far
  45.5 23.8 %level.1 = (f32[4,4,2048]{2,1,0:T(4,128)S(1)}, f32[4,1,256]{2,1,0:T(1,128)S(1)}) custom-call(s32[48,128]{1,0:T(8,128)S(1)} %get-tuple-element.14.where, s32[8,128]{1,0:T(8,128)S(1)} %get-tuple-element.15.chunks, bf16[15568,256]{1,0:T(8,128)(2,1)S(1)} %near.1.near_grads, f32[4,136,384]{2,1,0:T(8,128)S(1)} %collective-permute-done.9.far, ...), custom_call_target="tpu_custom_call" | custom-call | tf_op jit(solution)/shard_map/level/pallas_call | solution.py:433
  69.3 0.1 fusion
  69.4 0.6 collective-permute-start.12
  70.0 1.0 %collective-permute-start.11 = (f32[4,2048]{1,0:T(4,128)S(1)}, f32[4,2048]{1,0:T(4,128)S(1)}, u32[]{:S(2)}, u32[]{:S(2)}) collective-permute-start(f32[4,2048]{1,0:T(4,128)S(1)} %get-tuple-element.24), channel_id=1, source_target_pairs={{0,16},{1,17},{2,18},{3,19},{4,20},{5,21},{6,22},{7,23},{8,24},{9,... | collective-permute-start | bytes 98312 | tf_op jit(solution)/shard_map/ppermute | solution.py:335
  71.0 0.4 collective-permute-start.10
  71.4 0.1 reshape.31
  71.5 0.7 reshape.32
  72.2 1.0 %collective-permute-done.12 = f32[4,2048]{1,0:T(4,128)S(1)} collective-permute-done((f32[4,2048]{1,0:T(4,128)S(1)}, f32[4,2048]{1,0:T(4,128)S(1)}, u32[]{:S(2)}, u32[]{:S(2)}) %collective-permute-start.12) | collective-permute-done | bytes 32800 | tf_op jit(solution)/shard_map/ppermute | solution.py:335
  73.2 1.1 %collective-permute-done.11 = f32[4,2048]{1,0:T(4,128)S(1)} collective-permute-done((f32[4,2048]{1,0:T(4,128)S(1)}, f32[4,2048]{1,0:T(4,128)S(1)}, u32[]{:S(2)}, u32[]{:S(2)}) %collective-permute-start.11) | collective-permute-done | bytes 32800 | tf_op jit(solution)/shard_map/ppermute | solution.py:335
  74.3 0.0 collective-permute-done.10
  74.4 0.2 reshape_reshape.11
  74.5 0.2 copy.13
  74.7 0.8 %copy.15 = f32[4,128,64]{1,2,0:T(8,128)} copy(f32[4,128,64]{2,1,0:T(8,128)S(1)} %bitcast.32) | data formatting | bytes 262144
  (15 shorter events, 0.2 us)
Async XLA Ops:
  0.6 28.3 %copy-start = (s32[128,3072]{1,0:T(8,128)S(1)}, s32[128,3072]{1,0:T(8,128)}, u32[]{:S(2)}) copy-start(s32[128,3072]{1,0:T(8,128)} %refs_4_.1) | copy-start | bytes 4718596
  0.6 29.2 %copy-start.2 = (f32[16,32]{1,0:T(8,128)S(1)}, f32[16,32]{1,0:T(8,128)}, u32[]{:S(2)}) copy-start(f32[16,32]{1,0:T(8,128)} %param.13) | copy-start | bytes 6148
  3.2 6.6 %collective-permute-start.3 = (f32[40,384]{1,0:T(8,128)}, f32[40,384]{1,0:T(8,128)S(1)}, u32[]{:S(2)}, u32[]{:S(2)}) collective-permute-start(f32[40,384]{1,0:T(8,128)} %get-tuple-element.16), channel_id=1, source_target_pairs={{0,2},{1,3},{2,0},{3,1},{4,6},{5,7},{6,4},{7,5},{8,10},{9,11},{10,... | collective-permute-start | bytes 184328 | tf_op jit(solution)/shard_map/ppermute | solution.py:335
  6.3 6.6 %collective-permute-start.4 = (f32[40,384]{1,0:T(8,128)}, f32[40,384]{1,0:T(8,128)S(1)}, u32[]{:S(2)}, u32[]{:S(2)}) collective-permute-start(f32[40,384]{1,0:T(8,128)} %get-tuple-element.16), channel_id=1, source_target_pairs={{0,4},{1,5},{2,6},{3,7},{4,0},{5,1},{6,2},{7,3},{8,12},{9,13},{10,... | collective-permute-start | bytes 184328 | tf_op jit(solution)/shard_map/ppermute | solution.py:335
  8.9 6.2 %collective-permute-start.5 = (f32[40,384]{1,0:T(8,128)}, f32[40,384]{1,0:T(8,128)S(1)}, u32[]{:S(2)}, u32[]{:S(2)}) collective-permute-start(f32[40,384]{1,0:T(8,128)} %get-tuple-element.16), channel_id=1, source_target_pairs={{0,6},{1,7},{2,4},{3,5},{4,2},{5,3},{6,0},{7,1},{8,14},{9,15},{10,... | collective-permute-start | bytes 184328 | tf_op jit(solution)/shard_map/ppermute | solution.py:335
  15.8 8.6 %collective-permute-start.8 = (f32[136,384]{1,0:T(8,128)S(1)}, f32[136,384]{1,0:T(8,128)S(1)}, u32[]{:S(2)}, u32[]{:S(2)}) collective-permute-start(f32[136,384]{1,0:T(8,128)S(1)} %fusion.2), channel_id=1, source_target_pairs={{0,17},{1,16},{2,19},{3,18},{4,21},{5,20},{6,23},{7,22},{8,25},{9,... | collective-permute-start | bytes 626696 | tf_op jit(solution)/shard_map/ppermute | solution.py:335
  18.3 8.2 %collective-permute-start.7 = (f32[136,384]{1,0:T(8,128)S(1)}, f32[136,384]{1,0:T(8,128)S(1)}, u32[]{:S(2)}, u32[]{:S(2)}) collective-permute-start(f32[136,384]{1,0:T(8,128)S(1)} %fusion.2), channel_id=1, source_target_pairs={{0,16},{1,17},{2,18},{3,19},{4,20},{5,21},{6,22},{7,23},{8,24},{9,... | collective-permute-start | bytes 626696 | tf_op jit(solution)/shard_map/ppermute | solution.py:335
  18.8 7.8 %collective-permute-start.6 = (f32[136,384]{1,0:T(8,128)S(1)}, f32[136,384]{1,0:T(8,128)S(1)}, u32[]{:S(2)}, u32[]{:S(2)}) collective-permute-start(f32[136,384]{1,0:T(8,128)S(1)} %fusion.2), channel_id=1, source_target_pairs={{0,1},{1,0},{2,3},{3,2},{4,5},{5,4},{6,7},{7,6},{8,9},{9,8},{10,11... | collective-permute-start | bytes 626696 | tf_op jit(solution)/shard_map/ppermute | solution.py:335
  26.7 18.8 %collective-permute-start.9 = (f32[4,136,384]{2,1,0:T(8,128)S(1)}, f32[4,136,384]{2,1,0:T(8,128)S(1)}, u32[]{:S(2)}, u32[]{:S(2)}) collective-permute-start(f32[4,136,384]{2,1,0:T(8,128)S(1)} %pad_maximum_fusion.near), channel_id=1, source_target_pairs={{0,8},{1,9},{2,10},{3,11},{4,12},{5,13},{6,14},{7,15},{8,0},{9,1},... | collective-permute-start | bytes 2506760 | tf_op jit(solution)/shard_map/ppermute | solution.py:335
  26.8 7.3 %collective-permute-start.2 = (bf16[264,384]{1,0:T(8,128)(2,1)}, bf16[264,384]{1,0:T(8,128)(2,1)S(1)}, u32[]{:S(2)}, u32[]{:S(2)}) collective-permute-start(bf16[264,384]{1,0:T(8,128)(2,1)} %get-tuple-element.13), channel_id=1, source_target_pairs={{0,24},{1,25},{2,26},{3,27},{4,28},{5,29},{6,30},{7,31},{8,16},{9,... | collective-permute-start | bytes 608264 | tf_op jit(solution)/shard_map/ppermute | solution.py:335
  28.3 10.4 %collective-permute-start.1 = (bf16[264,384]{1,0:T(8,128)(2,1)}, bf16[264,384]{1,0:T(8,128)(2,1)S(1)}, u32[]{:S(2)}, u32[]{:S(2)}) collective-permute-start(bf16[264,384]{1,0:T(8,128)(2,1)} %get-tuple-element.12), channel_id=1, source_target_pairs={{0,16},{1,17},{2,18},{3,19},{4,20},{5,21},{6,22},{7,23},{8,24},{9,... | collective-permute-start | bytes 608264 | tf_op jit(solution)/shard_map/ppermute | solution.py:335
  28.9 9.8 %collective-permute-start = (bf16[264,384]{1,0:T(8,128)(2,1)}, bf16[264,384]{1,0:T(8,128)(2,1)S(1)}, u32[]{:S(2)}, u32[]{:S(2)}) collective-permute-start(bf16[264,384]{1,0:T(8,128)(2,1)} %get-tuple-element.11), channel_id=1, source_target_pairs={{0,8},{1,9},{2,10},{3,11},{4,12},{5,13},{6,14},{7,15},{8,0},{9,1},... | collective-permute-start | bytes 608264 | tf_op jit(solution)/shard_map/ppermute | solution.py:335
  28.9 0.7 copy-start.1
  69.4 3.7 %collective-permute-start.12 = (f32[4,2048]{1,0:T(4,128)S(1)}, f32[4,2048]{1,0:T(4,128)S(1)}, u32[]{:S(2)}, u32[]{:S(2)}) collective-permute-start(f32[4,2048]{1,0:T(4,128)S(1)} %get-tuple-element.23), channel_id=1, source_target_pairs={{0,24},{1,25},{2,26},{3,27},{4,28},{5,29},{6,30},{7,31},{8,16},{9,... | collective-permute-start | bytes 98312 | tf_op jit(solution)/shard_map/ppermute | solution.py:335
  70.0 4.2 %collective-permute-start.11 = (f32[4,2048]{1,0:T(4,128)S(1)}, f32[4,2048]{1,0:T(4,128)S(1)}, u32[]{:S(2)}, u32[]{:S(2)}) collective-permute-start(f32[4,2048]{1,0:T(4,128)S(1)} %get-tuple-element.24), channel_id=1, source_target_pairs={{0,16},{1,17},{2,18},{3,19},{4,20},{5,21},{6,22},{7,23},{8,24},{9,... | collective-permute-start | bytes 98312 | tf_op jit(solution)/shard_map/ppermute | solution.py:335
  71.0 3.2 %collective-permute-start.10 = (f32[4,2048]{1,0:T(4,128)S(1)}, f32[4,2048]{1,0:T(4,128)S(1)}, u32[]{:S(2)}, u32[]{:S(2)}) collective-permute-start(f32[4,2048]{1,0:T(4,128)S(1)} %get-tuple-element.25), channel_id=1, source_target_pairs={{0,8},{1,9},{2,10},{3,11},{4,12},{5,13},{6,14},{7,15},{8,0},{9,1},... | collective-permute-start | bytes 98312 | tf_op jit(solution)/shard_map/ppermute | solution.py:335
